TPU v7x, 256 devices: a whole 4x4x8 slice. The times are simulated.
256 devices in a mesh: dp: 4 (over z_lo, core), seq: 64 (over z_hi, y, x).
Axes of the slice: x: 4, y: 4, z: 8 (z_hi: 4, z_lo: 2; z = z_hi * 2 + z_lo), core: 2. Of those that a mesh axis runs over, the one named last changes fastest.
Arguments:
- tokens: bfloat16 [4, 128, 524288], P('dp', None, 'seq'), may hold values from -6 to 6
- kernel: bfloat16 [2, 128, 524288], P(None, None, 'seq'), may hold values from -6 to 6
- skip: float32 [128], replicated, may hold values from -4 to 4
- w_proj: bfloat16 [128, 256], replicated, may hold values from -0.5 to 0.5
- w_out: bfloat16 [128, 128], replicated, may hold values from -0.5 to 0.5
- cotangent: bfloat16 [4, 128, 524288], P('dp', None, 'seq'), may hold values from -6 to 6
Outputs:
- input_grad: bfloat16 [4, 128, 524288], P('dp', None, 'seq')
- kernel_grad: bfloat16 [2, 128, 524288], P(None, 'dp', 'seq')
All inputs are finite; a program needn't handle non-finite values.
Results may differ from a plain program's by a relative error of at most 0.013.
Values may be sent and summed in bfloat16 or wider, within the bound.
No kernel may reach another device: no remote copies, remote signals or barrier semaphores. Data moves between devices by JAX's collectives and lax.ppermute only.
A program may use at most 128 MiB of HBM per device.

v0:
```python
import math

import jax
import jax.numpy as jnp
from jax import lax
from jax.sharding import PartitionSpec as P

F2 = 64
F3 = 128


def dft_pair(length, direction):
    indices = jnp.arange(length, dtype=jnp.int32)
    turn_ids = indices[:, None] * indices[None, :] % length
    angles = turn_ids.astype(jnp.float32) * (2.0 * math.pi / length)
    factor = 1.0 / math.sqrt(length)
    real_part = (jnp.cos(angles) * factor).astype(jnp.bfloat16)
    imag_part = (direction * jnp.sin(angles) * factor).astype(jnp.bfloat16)
    return (real_part, imag_part)


def block_matrix(length, direction):
    real_part, imag_part = dft_pair(length, direction)
    top_row = jnp.stack([real_part, -imag_part], axis=1)
    bottom_row = jnp.stack([imag_part, real_part], axis=1)
    return jnp.stack([top_row, bottom_row], axis=0)


def twiddle(turn_ids, modulus, direction):
    angles = (turn_ids % modulus).astype(jnp.float32) * (2.0 * math.pi / modulus)
    return (jnp.cos(angles), direction * jnp.sin(angles))


def rotate(stacked, cos_part, sin_part):
    real_out = stacked[0] * cos_part - stacked[1] * sin_part
    imag_out = stacked[0] * sin_part + stacked[1] * cos_part
    return jnp.stack([real_out, imag_out]).astype(jnp.bfloat16)


def complex_product(spectrum_a, spectrum_b, conjugate_first):
    a_real = spectrum_a[0].astype(jnp.float32)
    a_imag = spectrum_a[1].astype(jnp.float32)
    if conjugate_first:
        a_imag = -a_imag
    b_real = spectrum_b[0].astype(jnp.float32)
    b_imag = spectrum_b[1].astype(jnp.float32)
    return jnp.stack([a_real * b_real - a_imag * b_imag, a_real * b_imag + a_imag * b_real])


def section_first(signal, device, whole_len):
    first_len = signal.shape[1]
    flat_len = signal.shape[2]
    real_part, imag_part = dft_pair(first_len, -1.0)
    matrix = jnp.stack([real_part, imag_part])
    combined = jnp.einsum("okn,cnm->ockm", matrix, signal, preferred_element_type=jnp.float32)
    frequency = jnp.arange(first_len, dtype=jnp.int32)[:, None]
    offsets = device * flat_len + jnp.arange(flat_len, dtype=jnp.int32)[None, :]
    cos_part, sin_part = twiddle(frequency * offsets, whole_len, -1.0)
    return rotate(combined, cos_part, sin_part)


def local_forward(spread):
    mid_len = spread.shape[3]
    last_len = spread.shape[4]
    combined = jnp.einsum(
        "opiq,icjqt->ocjpt", block_matrix(mid_len, -1.0), spread, preferred_element_type=jnp.float32
    )
    grid_ids = (
        jnp.arange(mid_len, dtype=jnp.int32)[:, None]
        * jnp.arange(last_len, dtype=jnp.int32)[None, :]
    )
    cos_two, sin_two = twiddle(grid_ids, mid_len * last_len, -1.0)
    section_two = rotate(combined, cos_two, sin_two)
    combined = jnp.einsum(
        "opiq,icjkq->ocjkp",
        block_matrix(last_len, -1.0),
        section_two,
        preferred_element_type=jnp.float32,
    )
    return combined.astype(jnp.bfloat16)


def local_inverse(spectrum, frequency, whole_len):
    mid_len = spectrum.shape[3]
    last_len = spectrum.shape[4]
    combined = jnp.einsum(
        "opiq,icjkq->ocjkp",
        block_matrix(last_len, 1.0),
        spectrum,
        preferred_element_type=jnp.float32,
    )
    grid_ids = (
        jnp.arange(mid_len, dtype=jnp.int32)[:, None]
        * jnp.arange(last_len, dtype=jnp.int32)[None, :]
    )
    cos_two, sin_two = twiddle(grid_ids, mid_len * last_len, 1.0)
    back_one = rotate(combined, cos_two, sin_two)
    combined = jnp.einsum(
        "opiq,icjqt->ocjpt",
        block_matrix(mid_len, 1.0),
        back_one,
        preferred_element_type=jnp.float32,
    )
    offsets = (
        jnp.arange(mid_len, dtype=jnp.int32)[:, None] * last_len
        + jnp.arange(last_len, dtype=jnp.int32)[None, :]
    )
    cos_part, sin_part = twiddle(frequency * offsets, whole_len, 1.0)
    return rotate(combined, cos_part, sin_part)


def section_last(received):
    first_len = received.shape[2]
    real_part, imag_part = dft_pair(first_len, 1.0)
    matrix = jnp.stack([real_part, -imag_part])
    combined = jnp.einsum("ink,ickm->cnm", matrix, received, preferred_element_type=jnp.float32)
    return combined.astype(jnp.bfloat16)


def spectral_items(received):
    shaped = received.reshape(2, received.shape[1], received.shape[2], F2, F3)
    return local_forward(shaped)


def per_device(tokens, kernel, skip, w_proj, w_out, cotangent):
    groups = lax.axis_size("seq")
    device = lax.axis_index("seq")
    channels = tokens.shape[1]
    local_len = tokens.shape[2]
    whole_len = groups * local_len
    home_shape = (channels, 1, local_len)
    signal = tokens.reshape(home_shape)
    grad_in = cotangent.reshape(home_shape)

    def first_items(received):
        return section_first(received, device, whole_len)

    def to_spectrum(real_signal):
        spread = first_items(
            lax.all_to_all(real_signal, "seq", split_axis=2, concat_axis=1, tiled=True)
        )
        return spectral_items(
            lax.all_to_all(spread, "seq", split_axis=2, concat_axis=3, tiled=True)
        )

    def from_spectrum(spectrum):
        folded = local_inverse(spectrum, device, whole_len).reshape(2, channels, 1, local_len)
        result = section_last(
            lax.all_to_all(folded, "seq", split_axis=3, concat_axis=2, tiled=True)
        )
        result = lax.all_to_all(result, "seq", split_axis=1, concat_axis=2, tiled=True)
        return result

    kernel_local = kernel.reshape(2, channels, 1, F2, F3)
    skip_col = skip[:, None, None]
    projected = jnp.einsum("ce,c...->e...", w_proj, signal, preferred_element_type=jnp.float32)
    values = projected[:channels].astype(jnp.bfloat16)
    gates = projected[channels:]
    spec_values = to_spectrum(values)
    product = complex_product(kernel_local, spec_values, False).astype(jnp.bfloat16)
    convolved = from_spectrum(product)
    mixed = convolved.astype(jnp.float32) + skip_col * values.astype(jnp.float32)
    grad_hidden = jnp.einsum("cd,d...->c...", w_out, grad_in, preferred_element_type=jnp.float32)
    grad_mixed = (grad_hidden * gates).astype(jnp.bfloat16)
    grad_gates = grad_hidden * mixed
    spec_grad = to_spectrum(grad_mixed)
    kernel_terms = complex_product(spec_values, spec_grad, True).astype(jnp.bfloat16)
    kernel_terms = lax.optimization_barrier(kernel_terms)
    kernel_terms = kernel_terms.astype(jnp.float32).reshape(2, channels, local_len)
    back_product = complex_product(kernel_local, spec_grad, True).astype(jnp.bfloat16)
    back_conv = from_spectrum(back_product)
    grad_values = back_conv.astype(jnp.float32) + skip_col * grad_mixed.astype(jnp.float32)
    grad_proj = jnp.concatenate([grad_values, grad_gates], axis=0).astype(jnp.bfloat16)
    input_grad = jnp.einsum(
        "ce,e...->c...", w_proj, grad_proj, preferred_element_type=jnp.float32
    ).astype(jnp.bfloat16)
    summed = lax.psum(kernel_terms.astype(jnp.bfloat16), "dp").astype(jnp.float32)
    share_len = channels // lax.axis_size("dp")
    kernel_grad = lax.dynamic_slice_in_dim(summed, lax.axis_index("dp") * share_len, share_len, 1)
    return (input_grad.reshape(1, channels, local_len), kernel_grad.astype(jnp.bfloat16))


def solution(mesh):
    placed = (P("dp", None, "seq"), P(None, None, "seq"), P(), P(), P(), P("dp", None, "seq"))
    return jax.shard_map(
        per_device,
        mesh=mesh,
        in_specs=placed,
        out_specs=(P("dp", None, "seq"), P(None, "dp", "seq")),
        check_vma=False,
    )
```

profile of v0, /device:TPU:35, one launch (start us, length us, event | category | flops | bytes accessed | tf_op | source)
XLA Modules:
  0.0 1056.8 jit_solution(7521603783815556077)
XLA Ops:
  21.9 45.1 %reduce = bf16[8192,128]{1,0:T(8,128)(2,1)S(1)} reduce(bf16[8192,1,128]{2,1,0:T(2,128)(2,1)} %bitcast.335, bf16[]{:T(256)} %broadcast.997), dimensions={1}, to_apply=%bitcast.311.reduce_sub_computation | reduce | bytes 4194306
  69.0 13.5 %all-to-all-start.4 = ((bf16[64,2,8192]{2,1,0:T(2,128)(2,1)}), bf16[64,2,8192]{2,1,0:T(2,128)(2,1)S(1)}, u32[]{:S(2)}, u32[]{:S(2)}) async-start(bf16[64,2,8192]{2,1,0:T(2,128)(2,1)} %reshape.997), calls=%async_computation.4 | async-start | bytes 4194304 | tf_op jit(solution)/shard_map/all_to_all | solution.py:140
  82.8 51.7 %all-to-all-done.4 = bf16[64,2,8192]{2,1,0:T(2,128)(2,1)S(1)} async-done(((bf16[64,2,8192]{2,1,0:T(2,128)(2,1)}), bf16[64,2,8192]{2,1,0:T(2,128)(2,1)S(1)}, u32[]{:S(2)}, u32[]{:S(2)}) %all-to-all-start.4) | async-done | bytes 2097184 | tf_op jit(solution)/shard_map/all_to_all | solution.py:140
  187.2 64.9 %all-to-all-done.5 = bf16[2,128,64,128]{3,0,1,2:T(2,128)(2,1)} async-done(((bf16[2,128,64,128]{3,0,1,2:T(2,128)(2,1)}), bf16[2,128,64,128]{3,0,1,2:T(2,128)(2,1)}, u32[]{:S(2)}, u32[]{:S(2)}) %all-to-all-start.5) | async-done | bytes 4194336 | tf_op jit(solution)/shard_map/all_to_all | solution.py:143
  272.5 8.5 fusion.61
  306.2 10.9 %pad_maximum_fusion.4 = bf16[2,128,1,8192]{1,0,2,3:T(2,128)(2,1)} fusion(bf16[1,128,1,8192]{1,0,2,3:T(2,128)(2,1)} %copy.163, bf16[1,128,1,8192]{1,0,2,3:T(2,128)(2,1)} %copy.162), kind=kLoop, calls=%fused_computation.55 | loop fusion | flops 8388608 | bytes 8388608 | tf_op jit(solution)/shard_map/stack | solution.py:37
  317.1 12.7 %all-to-all-start.6 = ((bf16[2,128,1,8192]{1,0,2,3:T(2,128)(2,1)}), bf16[2,128,1,8192]{1,0,2,3:T(2,128)(2,1)}, u32[]{:S(2)}, u32[]{:S(2)}) async-start(bf16[2,128,1,8192]{1,0,2,3:T(2,128)(2,1)} %pad_maximum_fusion.4), calls=%async_computation.6 | async-start | bytes 8388608 | tf_op jit(solution)/shard_map/all_to_all | solution.py:149
  330.0 88.7 %all-to-all-done.6 = bf16[2,128,1,8192]{1,0,2,3:T(2,128)(2,1)} async-done(((bf16[2,128,1,8192]{1,0,2,3:T(2,128)(2,1)}), bf16[2,128,1,8192]{1,0,2,3:T(2,128)(2,1)}, u32[]{:S(2)}, u32[]{:S(2)}) %all-to-all-start.6) | async-done | bytes 4194336 | tf_op jit(solution)/shard_map/all_to_all | solution.py:149
  418.7 8.4 copy.215
  431.4 45.5 %all_to_all.84 = bf16[128,64,128]{2,0,1:T(8,128)(2,1)S(1)} all-to-all(bf16[128,64,128]{2,0,1:T(8,128)(2,1)S(1)} %copy.165), channel_id=1, replica_groups=mesh['dp'=4,'seq'=64] {'seq'}, dimensions={1} | all-to-all | bytes 4194304 | tf_op jit(solution)/shard_map/all_to_all | solution.py:151
  489.1 46.5 %reduce.1 = bf16[8192,128]{1,0:T(8,128)(2,1)} reduce(bf16[8192,1,128]{2,1,0:T(2,128)(2,1)} %bitcast.337, bf16[]{:T(256)} %broadcast.997), dimensions={1}, to_apply=%bitcast.313.reduce_sub_computation | reduce | bytes 4194306
  539.5 34.2 %all_to_all.85 = bf16[64,2,8192]{2,1,0:T(2,128)(2,1)} all-to-all(bf16[64,2,8192]{2,1,0:T(2,128)(2,1)} %reshape.999), channel_id=1, replica_groups=mesh['dp'=4,'seq'=64] {'seq'}, dimensions={0} | all-to-all | bytes 4194304 | tf_op jit(solution)/shard_map/all_to_all | solution.py:140
  573.7 10.4 reshape.1000
  614.3 34.1 %all-to-all-done.1 = bf16[2,128,64,128]{3,0,1,2:T(2,128)(2,1)} async-done(((bf16[2,128,64,128]{3,0,1,2:T(2,128)(2,1)}), bf16[2,128,64,128]{3,0,1,2:T(2,128)(2,1)}, u32[]{:S(2)}, u32[]{:S(2)}) %all-to-all-start.1) | async-done | bytes 4194336 | tf_op jit(solution)/shard_map/all_to_all | solution.py:143
  648.4 7.6 fusion.49
  672.6 8.3 fusion.52
  691.0 9.5 copy.140
  704.8 9.5 copy.141
  714.3 10.9 %pad_maximum_fusion.1 = bf16[2,128,1,8192]{1,0,2,3:T(2,128)(2,1)} fusion(bf16[1,128,1,8192]{1,0,2,3:T(2,128)(2,1)} %copy.141, bf16[1,128,1,8192]{1,0,2,3:T(2,128)(2,1)} %copy.140), kind=kLoop, calls=%fused_computation.50 | loop fusion | flops 8388608 | bytes 8388608 | tf_op jit(solution)/shard_map/stack | solution.py:37
  725.2 11.9 %all-to-all-start.2 = ((bf16[2,128,1,8192]{1,0,2,3:T(2,128)(2,1)}), bf16[2,128,1,8192]{1,0,2,3:T(2,128)(2,1)}, u32[]{:S(2)}, u32[]{:S(2)}) async-start(bf16[2,128,1,8192]{1,0,2,3:T(2,128)(2,1)} %pad_maximum_fusion.1), calls=%async_computation.2 | async-start | bytes 8388608 | tf_op jit(solution)/shard_map/all_to_all | solution.py:149
  748.2 26.9 %all-to-all-done.2 = bf16[2,128,1,8192]{1,0,2,3:T(2,128)(2,1)} async-done(((bf16[2,128,1,8192]{1,0,2,3:T(2,128)(2,1)}), bf16[2,128,1,8192]{1,0,2,3:T(2,128)(2,1)}, u32[]{:S(2)}, u32[]{:S(2)}) %all-to-all-start.2) | async-done | bytes 4194336 | tf_op jit(solution)/shard_map/all_to_all | solution.py:149
  775.1 8.4 copy.204
  789.2 12.6 %all-to-all-start.3 = ((bf16[128,64,128]{2,0,1:T(8,128)(2,1)}), bf16[128,64,128]{2,0,1:T(8,128)(2,1)}, u32[]{:S(2)}, u32[]{:S(2)}) async-start(bf16[128,64,128]{2,0,1:T(8,128)(2,1)} %copy.143), calls=%async_computation.3 | async-start | bytes 4194304 | tf_op jit(solution)/shard_map/all_to_all | solution.py:151
  801.8 228.9 %all-reduce.2.cloned.1.call-done = bf16[2,128,8192]{1,2,0:T(8,128)(2,1)} async-done(((bf16[2,128,8192]{1,2,0:T(8,128)(2,1)}), bf16[2,128,8192]{1,2,0:T(8,128)(2,1)}) %all-reduce.2.cloned.1.call-update) | async-done | bytes 4194320 | tf_op jit(solution)/shard_map/psum | solution.py:177
  (142 shorter events, 232.4 us)
Async XLA Ops:
  69.0 65.5 %all-to-all-start.4 = ((bf16[64,2,8192]{2,1,0:T(2,128)(2,1)}), bf16[64,2,8192]{2,1,0:T(2,128)(2,1)S(1)}, u32[]{:S(2)}, u32[]{:S(2)}) async-start(bf16[64,2,8192]{2,1,0:T(2,128)(2,1)} %reshape.997), calls=%async_computation.4 | async-start | bytes 4194304 | tf_op jit(solution)/shard_map/all_to_all | solution.py:140
  157.5 94.6 %all-to-all-start.5 = ((bf16[2,128,64,128]{3,0,1,2:T(2,128)(2,1)}), bf16[2,128,64,128]{3,0,1,2:T(2,128)(2,1)}, u32[]{:S(2)}, u32[]{:S(2)}) async-start(bf16[2,128,64,128]{3,0,1,2:T(2,128)(2,1)} %copy.147), calls=%async_computation.5 | async-start | bytes 8388608 | tf_op jit(solution)/shard_map/all_to_all | solution.py:143
  181.7 78.0 %copy-start.9 = (bf16[1,128,8192]{1,2,0:T(8,128)(2,1)}, bf16[1,128,8192]{1,2,0:T(8,128)(2,1)S(1)}, u32[]{:S(2)}) copy-start(bf16[1,128,8192]{1,2,0:T(8,128)(2,1)S(1)} %copy.218) | copy-start | bytes 6291460
  186.9 72.8 %copy-start.15 = (bf16[1,64,2,64]{3,1,2,0:T(8,128)(2,1)}, bf16[1,64,2,64]{3,1,2,0:T(8,128)(2,1)S(1)}, u32[]{:S(2)}) copy-start(bf16[1,64,2,64]{3,1,2,0:T(8,128)(2,1)S(1)} %get-tuple-element.37) | copy-start | bytes 49156
  186.9 72.8 %copy-start.17 = (bf16[1,64,2,64]{3,1,2,0:T(8,128)(2,1)}, bf16[1,64,2,64]{3,1,2,0:T(8,128)(2,1)S(1)}, u32[]{:S(2)}) copy-start(bf16[1,64,2,64]{3,1,2,0:T(8,128)(2,1)S(1)} %get-tuple-element.38) | copy-start | bytes 49156
  186.9 95.3 %copy-start.13 = (bf16[1,64,2,64]{3,1,2,0:T(8,128)(2,1)}, bf16[1,64,2,64]{3,1,2,0:T(8,128)(2,1)S(1)}, u32[]{:S(2)}) copy-start(bf16[1,64,2,64]{3,1,2,0:T(8,128)(2,1)S(1)} %get-tuple-element.36) | copy-start | bytes 49156
  186.9 74.4 %copy-start.19 = (bf16[1,128,2,128]{3,1,2,0:T(8,128)(2,1)}, bf16[1,128,2,128]{3,1,2,0:T(8,128)(2,1)S(1)}, u32[]{:S(2)}) copy-start(bf16[1,128,2,128]{3,1,2,0:T(8,128)(2,1)S(1)} %get-tuple-element.33) | copy-start | bytes 196612
  187.0 74.4 %copy-start.21 = (bf16[1,128,2,128]{3,1,2,0:T(8,128)(2,1)}, bf16[1,128,2,128]{3,1,2,0:T(8,128)(2,1)S(1)}, u32[]{:S(2)}) copy-start(bf16[1,128,2,128]{3,1,2,0:T(8,128)(2,1)S(1)} %get-tuple-element.34) | copy-start | bytes 196612
  261.3 5.5 copy-start.2
  261.4 5.5 copy-start.4
  317.1 101.5 %all-to-all-start.6 = ((bf16[2,128,1,8192]{1,0,2,3:T(2,128)(2,1)}), bf16[2,128,1,8192]{1,0,2,3:T(2,128)(2,1)}, u32[]{:S(2)}, u32[]{:S(2)}) async-start(bf16[2,128,1,8192]{1,0,2,3:T(2,128)(2,1)} %pad_maximum_fusion.4), calls=%async_computation.6 | async-start | bytes 8388608 | tf_op jit(solution)/shard_map/all_to_all | solution.py:149
  330.0 97.1 %copy-start.23 = (bf16[1,64,64]{2,1,0:T(8,128)(2,1)}, bf16[1,64,64]{2,1,0:T(8,128)(2,1)S(1)}, u32[]{:S(2)}) copy-start(bf16[1,64,64]{2,1,0:T(8,128)(2,1)S(1)} %fusion.144) | copy-start | bytes 24580
  430.0 46.9 %copy-start.11 = (bf16[1,128,8192]{2,1,0:T(8,128)(2,1)S(1)}, bf16[1,128,8192]{2,1,0:T(8,128)(2,1)}, u32[]{:S(2)}) copy-start(bf16[1,128,8192]{2,1,0:T(8,128)(2,1)} %param.11) | copy-start | bytes 6291460
  430.0 46.9 %copy-start.26 = (bf16[128,128]{1,0:T(8,128)(2,1)S(1)}, bf16[128,128]{1,0:T(8,128)(2,1)}, u32[]{:S(2)}) copy-start(bf16[128,128]{1,0:T(8,128)(2,1)} %param.10) | copy-start | bytes 98308
  430.0 46.9 %copy-start.27 = (f32[128]{0:T(128)S(1)}, f32[128]{0:T(128)}, u32[]{:S(2)}) copy-start(f32[128]{0:T(128)} %param.8) | copy-start | bytes 1540
  602.9 45.5 %all-to-all-start.1 = ((bf16[2,128,64,128]{3,0,1,2:T(2,128)(2,1)}), bf16[2,128,64,128]{3,0,1,2:T(2,128)(2,1)}, u32[]{:S(2)}, u32[]{:S(2)}) async-start(bf16[2,128,64,128]{3,0,1,2:T(2,128)(2,1)} %copy.123), calls=%async_computation.1 | async-start | bytes 8388608 | tf_op jit(solution)/shard_map/all_to_all | solution.py:143
  609.8 38.6 %copy-start.16 = (bf16[1,64,2,64]{3,1,2,0:T(8,128)(2,1)S(1)}, bf16[1,64,2,64]{3,1,2,0:T(8,128)(2,1)}, u32[]{:S(2)}) copy-start(bf16[1,64,2,64]{3,1,2,0:T(8,128)(2,1)} %copy-done.15) | copy-start | bytes 49156
  609.8 38.5 %copy-start.18 = (bf16[1,64,2,64]{3,1,2,0:T(8,128)(2,1)S(1)}, bf16[1,64,2,64]{3,1,2,0:T(8,128)(2,1)}, u32[]{:S(2)}) copy-start(bf16[1,64,2,64]{3,1,2,0:T(8,128)(2,1)} %copy-done.17) | copy-start | bytes 49156
  659.0 5.5 copy-start.5
  725.2 50.0 %all-to-all-start.2 = ((bf16[2,128,1,8192]{1,0,2,3:T(2,128)(2,1)}), bf16[2,128,1,8192]{1,0,2,3:T(2,128)(2,1)}, u32[]{:S(2)}, u32[]{:S(2)}) async-start(bf16[2,128,1,8192]{1,0,2,3:T(2,128)(2,1)} %pad_maximum_fusion.1), calls=%async_computation.2 | async-start | bytes 8388608 | tf_op jit(solution)/shard_map/all_to_all | solution.py:149
  737.1 293.5 %all-reduce.2.cloned.1.call-start = ((), (), s32[]{:S(2)}) async-start(), calls=%async_computation.8 | async-start | bytes 8388608 | tf_op jit(solution)/shard_map/psum | solution.py:177
  775.1 8.4 copy-start.24
  789.2 251.4 %all-to-all-start.3 = ((bf16[128,64,128]{2,0,1:T(8,128)(2,1)}), bf16[128,64,128]{2,0,1:T(8,128)(2,1)}, u32[]{:S(2)}, u32[]{:S(2)}) async-start(bf16[128,64,128]{2,0,1:T(8,128)(2,1)} %copy.143), calls=%async_computation.3 | async-start | bytes 4194304 | tf_op jit(solution)/shard_map/all_to_all | solution.py:151
  1043.0 6.7 copy-start.1
  (11 other events, 26.4 us)
Sparse Core Ops, SparseCore 0:
  748.3 282.2 all-reduce.1
where the time goes:
time: 1070 us; the launch traced here: 1060 us
  waiting for transfers between devices  495 us (46%)
  local copies, waits for them, and re-layouts  183 us (17%)
  other arithmetic  155 us (14%)
  blocking collectives  79.7 us (7%)
  matrix products  65.4 us (6%)
  starting transfers between devices  63.8 us (6%)
  between operations  14.9 us (1%)
    psum x1, waiting for transfers between devices, per_device(): lax.psum(kernel_terms.astype(jnp.bfloat16), 'dp').astype(jnp.float32)  229 us
    all_to_all x2, waiting for transfers between devices, from_spectrum(): lax.all_to_all(folded, 'seq', split_axis=3, concat_axis=2, tiled=True)  116 us
    all_to_all x2, waiting for transfers between devices, to_spectrum(): lax.all_to_all(spread, 'seq', split_axis=2, concat_axis=3, tiled=True)  99 us
    unnamed x2, other arithmetic  91.6 us
    another operation x10, local copies, waits for them, and re-layouts, rotate(): return jnp.stack([real_out, imag_out]).astype(jnp.bfloat16)  59.6 us
    unnamed x67, local copies, waits for them, and re-layouts  54.8 us
    all_to_all x1, waiting for transfers between devices, to_spectrum(): lax.all_to_all(real_signal, 'seq', split_axis=2, concat_axis=1, tiled=True)  51.7 us
    all_to_all x1, blocking collectives, from_spectrum(): lax.all_to_all(result, 'seq', split_axis=1, concat_axis=2, tiled=True)  45.5 us
  transfers between devices with their start and end apart: 7, of which 6 were waited for; matrix products, arithmetic and copies ran while one was open for 6% of the time, Pallas kernels for 0%

commit v1 on v0

v1 whole, which is shorter than its diff:
```python
import functools
import math

import jax
import jax.numpy as jnp
import numpy as np
from jax import lax
from jax.experimental import pallas as pl
from jax.experimental.pallas import tpu as pltpu
from jax.sharding import Mesh, PartitionSpec as P

BF = jnp.bfloat16
F32 = jnp.float32
F2 = 64
F3 = 128
LANES = 128


def dft_blocks(length, direction):
    ids = np.arange(length)
    angles = (ids[:, None] * ids[None, :] % length).astype(np.float32) * np.float32(
        2.0 * math.pi / length
    )
    scale = np.float32(1.0 / math.sqrt(length))
    real = np.cos(angles) * scale
    imag = direction * np.sin(angles) * scale
    return np.block([[real, -imag], [imag, real]]).astype(np.float32)


def turns(ids, modulus):
    angles = (ids % modulus).astype(np.float64) * (2.0 * math.pi / modulus)
    return np.stack([np.cos(angles), np.sin(angles)]).astype(np.float32)


def flip_matrix(size, shift):
    out = np.zeros((size, size), np.float32)
    for j in range(size):
        out[j, (size - shift - j) % size] = 1.0
    return out


def vmem_specs(count):
    return [pl.BlockSpec(memory_space=pltpu.VMEM)] * count


SMEM_SPEC = pl.BlockSpec(memory_space=pltpu.SMEM)


def call(body, out_shape, scratch, *args, smem=0, name):
    multi = isinstance(out_shape, (tuple, list))
    return pl.pallas_call(
        body,
        out_shape=out_shape,
        in_specs=[SMEM_SPEC] * smem + vmem_specs(len(args) - smem),
        out_specs=vmem_specs(len(out_shape)) if multi else vmem_specs(1)[0],
        scratch_shapes=scratch,
        compiler_params=pltpu.CompilerParams(vmem_limit_bytes=48 << 20),
        name=name,
    )(*args)


def dot(a, b):
    return jnp.dot(a, b, preferred_element_type=F32)


def loop(count, body, unroll=1):
    def step(i, carry):
        body(i)
        return carry

    lax.fori_loop(0, count, step, 0, unroll=unroll)


def loop_carry(count, body, init, unroll=1):
    return lax.fori_loop(0, count, body, init, unroll=unroll)


def lane_block(ref, i, rows=None):
    window = pl.ds(pl.multiple_of(i * LANES, LANES), LANES)
    return ref[:, window] if rows is None else ref[rows, window]


def spread_body(x_ref, out_ref, rows_ref):
    channels, blocks, _ = out_ref.shape

    def put(i):
        rows_ref[pl.ds(pl.multiple_of(i * channels, 8), channels), :] = lane_block(
            x_ref, i
        ).astype(F32)

    loop(blocks, put, 4)
    gather_rows(rows_ref, out_ref)


def gather_rows(rows_ref, out_ref):
    channels, blocks, _ = out_ref.shape

    def take(c):
        out_ref[c] = rows_ref[pl.ds(c, blocks, stride=channels), :].astype(out_ref.dtype)

    loop(channels, take, 4)


def unpack_rows(x_ref, rows_ref):
    items, blocks, _ = x_ref.shape

    def put(c):
        rows_ref[pl.ds(pl.multiple_of(c * blocks, 8), blocks), :] = x_ref[c].astype(F32)

    loop(items, put, 4)


def values_body(wv_ref, tok_ref, out_ref, rows_ref):
    channels, blocks, _ = out_ref.shape

    def put(i):
        rows_ref[pl.ds(pl.multiple_of(i * channels, 8), channels), :] = dot(
            wv_ref[...], lane_block(tok_ref, i)
        )

    loop(blocks, put, 4)
    gather_rows(rows_ref, out_ref)


def grad_body(wg_ref, wo_ref, tok_ref, cot_ref, out_ref, rows_ref):
    channels, blocks, _ = out_ref.shape

    def put(i):
        gates = dot(wg_ref[...], lane_block(tok_ref, i))
        hidden = dot(wo_ref[...], lane_block(cot_ref, i))
        rows_ref[pl.ds(pl.multiple_of(i * channels, 8), channels), :] = hidden * gates

    loop(blocks, put, 4)
    gather_rows(rows_ref, out_ref)


def rotate(re, im, cos_part, sin_part):
    return re * cos_part - im * sin_part, re * sin_part + im * cos_part


def first_stage(z_ref, m1_ref, tw_ref, rows_ref):
    count = m1_ref.shape[0]
    half = count // 2
    unpack_rows(z_ref, rows_ref)

    def step(m2, turn):
        cos_part, sin_part = turn
        x = rows_ref[pl.ds(m2, count, stride=F2), :].astype(BF)
        y = dot(m1_ref[...], x)
        re, im = rotate(y[:half], y[half:], cos_part, -sin_part)
        rows_ref[pl.ds(m2, half, stride=2 * F2), :] = re
        rows_ref[pl.ds(F2 + m2, half, stride=2 * F2), :] = im
        return rotate(cos_part, sin_part, tw_ref[2], tw_ref[3])

    loop_carry(F2, step, (tw_ref[0], tw_ref[1]), 2)


def last_stage(out_ref, m1_ref, tw_ref, rows_ref):
    count = m1_ref.shape[0]
    half = count // 2

    def step(m2, turn):
        cos_part, sin_part = turn
        re, im = rotate(
            rows_ref[pl.ds(m2, half, stride=2 * F2), :],
            rows_ref[pl.ds(F2 + m2, half, stride=2 * F2), :],
            cos_part,
            sin_part,
        )
        x = jnp.concatenate([re, im], axis=0).astype(BF)
        rows_ref[pl.ds(m2, count, stride=F2), :] = dot(m1_ref[...], x)
        return rotate(cos_part, sin_part, tw_ref[2], tw_ref[3])

    loop_carry(F2, step, (tw_ref[0], tw_ref[1]), 2)

    def put(c):
        out_ref[c] = rows_ref[pl.ds(pl.multiple_of(c * F2, 8), F2), :].astype(BF)

    loop(count, put, 4)


def to_spectrum(x, m2_ref, m3_ref, tw2_ref):
    y = dot(m2_ref[...], x)
    re, im = rotate(y[:F2], y[F2:], tw2_ref[0], -tw2_ref[1])
    return dot(jnp.concatenate([re, im], axis=1).astype(BF), m3_ref[...]).astype(BF)


def from_spectrum(re, im, m2_ref, m3_ref, tw2_ref):
    y = dot(jnp.concatenate([re, im], axis=1).astype(BF), m3_ref[...])
    re, im = rotate(y[:, :F3], y[:, F3:], tw2_ref[0], tw2_ref[1])
    return dot(m2_ref[...], jnp.concatenate([re, im], axis=0).astype(BF))


def k1_rows(k1):
    return pl.ds(pl.multiple_of(k1 * 2 * F2, 8), 2 * F2)


def forward_values_body(
    z_ref, kh_ref, m1_ref, m2_ref, m3_ref, n1_ref, n2_ref, n3_ref, tw_ref, tw2_ref,
    conv_ref, spec_ref, rows_ref,
):
    first_stage(z_ref, m1_ref, tw_ref, rows_ref)

    def step(k1):
        spec = to_spectrum(rows_ref[k1_rows(k1), :].astype(BF), m2_ref, m3_ref, tw2_ref)
        spec_ref[k1] = spec
        spec = spec.astype(F32)
        kern = kh_ref[k1]
        re, im = rotate(spec[:, :F3], spec[:, F3:], kern[:F2], kern[F2:])
        rows_ref[k1_rows(k1), :] = from_spectrum(re, im, n2_ref, n3_ref, tw2_ref)

    loop(kh_ref.shape[0], step, 4)
    last_stage(conv_ref, n1_ref, tw_ref, rows_ref)


def forward_grad_body(
    core_ref, z_ref, kh_ref, spec_ref, m1_ref, m2_ref, m3_ref, n1_ref, n2_ref, n3_ref,
    tw_ref, tw2_ref, flips_ref, lanes_ref,
    conv_ref, keep_ref, send_ref, rows_ref, terms_ref,
):
    first_stage(z_ref, m1_ref, tw_ref, rows_ref)
    count = kh_ref.shape[0]

    def step(k1):
        grad = to_spectrum(rows_ref[k1_rows(k1), :].astype(BF), m2_ref, m3_ref, tw2_ref)
        grad = grad.astype(F32)
        kern = kh_ref[k1]
        re, im = rotate(grad[:, :F3], grad[:, F3:], kern[:F2], -kern[F2:])
        rows_ref[k1_rows(k1), :] = from_spectrum(re, im, n2_ref, n3_ref, tw2_ref)
        spec = spec_ref[k1].astype(F32)
        re, im = rotate(grad[:, :F3], grad[:, F3:], spec[:, :F3], -spec[:, F3:])
        terms_ref[k1] = jnp.concatenate([re, im], axis=0).astype(BF)

    loop(count, step, 4)
    last_stage(conv_ref, n1_ref, tw_ref, rows_ref)
    on_core_zero = core_ref[0] == 0

    def mirror(k1):
        term = terms_ref[k1].astype(F32) + flipped(terms_ref, k1, flips_ref, lanes_ref)
        re, im = 0.5 * term[:F2], 0.5 * term[F2:]
        keep_ref[k1] = jnp.where(on_core_zero, re, im).astype(BF)
        send_ref[k1] = jnp.where(on_core_zero, im, re).astype(BF)

    loop(count, mirror, 4)


def flipped(ref, k1, flips_ref, lanes_ref):
    count = ref.shape[0]
    first = k1 == 0
    block = ref[jnp.where(first, 0, count - k1)]
    turned = dot(flips_ref[jnp.where(first, 1, 0)], dot(block, lanes_ref[0]).astype(BF))
    head = dot(flips_ref[jnp.where(first, 1, 0)], dot(block, lanes_ref[1]).astype(BF))
    row = lax.broadcasted_iota(jnp.int32, turned.shape, 0) % F2
    pick_head = jnp.logical_and(first, row == 0)
    return jnp.where(pick_head, head, turned)


def response_body(core_ref, own_ref, other_ref, flips_ref, lanes_ref, kh_ref, both_ref):
    on_core_zero = core_ref[0] == 0
    count = own_ref.shape[0]

    def gather(k1):
        own, other = own_ref[k1].astype(F32), other_ref[k1].astype(F32)
        both_ref[k1] = jnp.concatenate(
            [jnp.where(on_core_zero, own, other), jnp.where(on_core_zero, other, own)], axis=0
        ).astype(BF)

    loop(count, gather, 4)

    def mirror(k1):
        kh_ref[k1] = 0.5 * (
            both_ref[k1].astype(F32) + flipped(both_ref, k1, flips_ref, lanes_ref)
        )

    loop(count, mirror, 4)


def gates_body(
    wv_ref, wg_ref, wo_ref, wpg_ref, skip_ref, tok_ref, cot_ref, conv_ref,
    part_ref, own_ref, rows_ref,
):
    channels, blocks, _ = conv_ref.shape
    unpack_rows(conv_ref, rows_ref)

    def step(i):
        tok = lane_block(tok_ref, i)
        values = dot(wv_ref[...], tok).astype(BF).astype(F32)
        gates = dot(wg_ref[...], tok)
        hidden = dot(wo_ref[...], lane_block(cot_ref, i))
        conv = rows_ref[pl.ds(i, channels, stride=blocks), :]
        mixed = conv + skip_ref[...] * values
        window = pl.ds(pl.multiple_of(i * LANES, LANES), LANES)
        part_ref[:, window] = dot(wpg_ref[...], (hidden * mixed).astype(BF))
        own_ref[:, window] = (hidden * gates).astype(BF)

    loop(blocks, step, 2)


def final_body(wpv_ref, skip_ref, part_ref, own_ref, conv_ref, out_ref, rows_ref):
    channels, blocks, _ = conv_ref.shape
    unpack_rows(conv_ref, rows_ref)

    def step(i):
        window = pl.ds(pl.multiple_of(i * LANES, LANES), LANES)
        conv = rows_ref[pl.ds(i, channels, stride=blocks), :]
        grad = conv + skip_ref[...] * own_ref[:, window].astype(F32)
        out_ref[:, window] = (part_ref[:, window] + dot(wpv_ref[...], grad.astype(BF))).astype(BF)

    loop(blocks, step, 4)


def kernel_grad_body(core_ref, keep_ref, recv_ref, out_ref, rows_ref):
    channels, blocks, _ = keep_ref.shape
    core = core_ref[0]
    for ref, part in ((keep_ref, core), (recv_ref, 1 - core)):
        unpack_rows(ref, rows_ref)

        def step(i, part=part):
            window = pl.ds(pl.multiple_of(i * LANES, LANES), LANES)
            out_ref[part, :, window] = rows_ref[pl.ds(i, channels, stride=blocks), :].astype(BF)

        loop(blocks, step, 4)


SWAP = [(0, 1), (1, 0)]


def per_device(tokens, kernel, skip, w_proj, w_out, cotangent):
    first_len = lax.axis_size("seq")
    core = lax.axis_index("core")
    z_low = lax.axis_index("zl")
    channels, positions = tokens.shape[1:]
    whole = first_len * positions
    core_arr = core.astype(jnp.int32).reshape(1)
    tok = tokens.reshape(channels, positions)
    cot = cotangent.reshape(channels, positions)
    blocks = positions // LANES
    shaped = functools.partial(jax.ShapeDtypeStruct)

    bf = functools.partial(jnp.asarray, dtype=BF)
    wv = w_proj[:, :channels].T
    wg = w_proj[:, channels:].T
    wpv = w_proj[:, :channels]
    wpg = w_proj[:, channels:]
    skip_full = jnp.broadcast_to(skip[:, None], (channels, LANES))
    m1, n1 = bf(dft_blocks(first_len, -1.0)), bf(dft_blocks(first_len, 1.0))
    m2, n2 = bf(dft_blocks(F2, -1.0)), bf(dft_blocks(F2, 1.0))
    m3, n3 = bf(dft_blocks(F3, -1.0).T), bf(dft_blocks(F3, 1.0).T)
    freq = np.arange(first_len)[:, None]
    tw = jnp.asarray(
        np.concatenate(
            [
                turns(freq * np.arange(F3)[None, :], whole),
                turns(freq * F3 * np.ones((1, F3), np.int64), whole),
            ]
        )
    )
    tw2 = jnp.asarray(turns(np.arange(F2)[:, None] * np.arange(F3)[None, :], F2 * F3))
    pair = np.array([[1.0, 0.0], [0.0, -1.0]], np.float32)
    flips = bf(np.stack([np.kron(pair, flip_matrix(F2, 1)), np.kron(pair, flip_matrix(F2, 0))]))
    lanes = bf(np.stack([flip_matrix(F3, 1), flip_matrix(F3, 0)]))

    exchange = functools.partial(lax.all_to_all, split_axis=0, concat_axis=0, tiled=True)
    share = first_len
    rows = pltpu.VMEM((channels * blocks, LANES), F32)
    small_rows = pltpu.VMEM((share * blocks, LANES), F32)
    signal = shaped((channels, blocks, LANES), BF)
    comp = shaped((share, blocks, LANES), BF)

    chosen = lax.dynamic_slice(kernel, (core, z_low * share, 0), (1, share, positions))[0]
    response = call(spread_body, comp, [small_rows], chosen, name="spread")
    response = exchange(response, "seq")
    response_other = lax.ppermute(response, "core", SWAP)

    values = call(values_body, signal, [rows], wv, tok, name="values")
    values = exchange(values, ("zl", "seq"))
    grads = call(grad_body, signal, [rows], wg, w_out, tok, cot, name="grads")
    grads = exchange(grads, ("zl", "seq"))

    kh = call(
        response_body,
        shaped((first_len, 2 * F2, F3), F32),
        [pltpu.VMEM((first_len, 2 * F2, F3), BF)],
        core_arr, response, response_other, flips, lanes,
        smem=1, name="response",
    )
    z_rows = pltpu.VMEM((2 * first_len * F2, F3), F32)
    conv, spec = call(
        forward_values_body,
        (shaped((2 * first_len, F2, F3), BF), shaped((first_len, F2, 2 * F3), BF)),
        [z_rows],
        values, kh, m1, m2, m3, n1, n2, n3, tw, tw2,
        name="values_transform",
    )
    conv = exchange(conv, ("zl", "seq"))
    back, keep, send = call(
        forward_grad_body,
        (
            shaped((2 * first_len, F2, F3), BF),
            shaped((first_len, F2, F3), BF),
            shaped((first_len, F2, F3), BF),
        ),
        [z_rows, pltpu.VMEM((first_len, 2 * F2, F3), BF)],
        core_arr, grads, kh, spec, m1, m2, m3, n1, n2, n3, tw, tw2, flips, lanes,
        smem=1, name="grads_transform",
    )
    back = exchange(back, ("zl", "seq"))
    terms = keep.astype(F32) + lax.ppermute(send, "core", SWAP).astype(F32)
    terms = exchange(terms.astype(BF), "seq")
    part, own = call(
        gates_body,
        (shaped((channels, positions), F32), shaped((channels, positions), BF)),
        [rows],
        wv, wg, w_out, wpg, skip_full, tok, cot, conv,
        name="gates",
    )
    half = share // 2
    kept = lax.dynamic_slice_in_dim(terms, core * half, half, 0)
    sent = lax.dynamic_slice_in_dim(terms, (1 - core) * half, half, 0)
    kernel_grad = call(
        kernel_grad_body,
        shaped((2, half, positions), BF),
        [pltpu.VMEM((half * blocks, LANES), F32)],
        core_arr, kept, lax.ppermute(sent, "core", SWAP),
        smem=1, name="kernel_grad",
    )
    input_grad = call(
        final_body,
        shaped((channels, positions), BF),
        [rows],
        wpv, skip_full, part, own, back,
        name="final",
    )
    return input_grad.reshape(1, channels, positions), kernel_grad


def solution(mesh):
    sequences, groups = mesh.devices.shape
    fine = Mesh(mesh.devices.reshape(2, sequences // 2, groups), ("zl", "core", "seq"))
    dp = ("zl", "core")
    placed = (P(dp, None, "seq"), P(None, None, "seq"), P(), P(), P(), P(dp, None, "seq"))
    return jax.shard_map(
        per_device,
        mesh=fine,
        in_specs=placed,
        out_specs=(P(dp, None, "seq"), P(None, dp, "seq")),
        check_vma=False,
    )
```

time: 1070 us -> 410 us (0.38)
  waiting for transfers between devices: 495 us -> 86.1 us
  local copies, waits for them, and re-layouts: 183 us -> 13.3 us
  Pallas kernels: 0 us -> 157 us
  other arithmetic: 155 us -> 0.41 us
  matrix products: 65.4 us -> 0 us
  blocking collectives: 79.7 us -> 95.7 us
  between operations: 14.9 us -> 0.98 us
  starting transfers between devices: 63.8 us -> 51.3 us
    psum x1 -> x0, waiting for transfers between devices: 229 us -> none  [per_device(): lax.psum(kernel_terms.astype(jnp.bfloat16), 'dp').astype(jnp.float32)]
    all_to_all x6 -> x4, waiting for transfers between devices: 266 us -> 79.9 us  [the longest x1 36.6 us: per_device(): values = exchange(values, ('zl', 'seq'))]
    pallas_call x0 -> x9, Pallas kernels: none -> 157 us  [call(): pl.pallas_call(body, out_shape=out_shape, in_specs=[SMEM_SPEC] * smem + v...]
    unnamed x2 -> x0, other arithmetic: 91.6 us -> none
    dot_general x15 -> x0, matrix products: 65.4 us -> none  [the longest x2 16.7 us: local_inverse(): jnp.einsum('opiq,icjkq->ocjkp', block_matrix(last_len, 1.0), spectrum, pr...]
    another operation x10 -> x0, local copies, waits for them, and re-layouts: 59.6 us -> none  [rotate(): return jnp.stack([real_out, imag_out]).astype(jnp.bfloat16)]
    another operation x25 -> x0, other arithmetic: 56.1 us -> none  [the longest x11 29.2 us: rotate(): return jnp.stack([real_out, imag_out]).astype(jnp.bfloat16)]
    unnamed x67 -> x59, local copies, waits for them, and re-layouts: 54.8 us -> 11.1 us
  transfers between devices with their start and end apart: 7 -> 7, of which waited for: 6 -> 6; matrix products, arithmetic and copies ran while one was open for 6% -> 0% of each run, Pallas kernels for 0% -> 22%
where the time goes in v1:
time: 410 us; the launch traced here: 405 us
  Pallas kernels  157 us (38%)
  blocking collectives  95.7 us (23%)
  waiting for transfers between devices  86.1 us (21%)
  starting transfers between devices  51.3 us (13%)
  local copies, waits for them, and re-layouts  13.3 us (3%)
    pallas_call x9, Pallas kernels, call(): pl.pallas_call(body, out_shape=out_shape, in_specs=[SMEM_SPEC] * smem + v...  157 us
    all_to_all x1, blocking collectives, per_device(): conv = exchange(conv, ('zl', 'seq'))  55.6 us
    all_to_all x1, blocking collectives, per_device(): terms = exchange(terms.astype(BF), 'seq')  40.1 us
    all_to_all x1, waiting for transfers between devices, per_device(): values = exchange(values, ('zl', 'seq'))  36.6 us
    all_to_all x1, waiting for transfers between devices, per_device(): response = exchange(response, 'seq')  21.9 us
    all_to_all x1, waiting for transfers between devices, per_device(): back = exchange(back, ('zl', 'seq'))  21.4 us
    all_to_all x1, starting transfers between devices, per_device(): response = exchange(response, 'seq')  13.2 us
    all_to_all x1, starting transfers between devices, per_device(): grads = exchange(grads, ('zl', 'seq'))  12.6 us
  transfers between devices with their start and end apart: 7, of which 6 were waited for; matrix products, arithmetic and copies ran while one was open for 0% of the time, Pallas kernels for 22%

profile of v1, /device:TPU:35, one launch (start us, length us, event | category | flops | bytes accessed | tf_op | source)
XLA Modules:
  0.0 404.5 jit_solution(13877074465184956323)
XLA Ops:
  2.0 1.8 spread.1
  4.7 13.2 %all-to-all-start.1 = ((bf16[64,64,128]{2,1,0:T(8,128)(2,1)}), bf16[64,64,128]{2,1,0:T(8,128)(2,1)S(1)}, u32[]{:S(2)}, u32[]{:S(2)}) async-start(bf16[64,64,128]{2,1,0:T(8,128)(2,1)} %copy-done.3), calls=%async_computation.1 | async-start | bytes 2097152 | tf_op jit(solution)/shard_map/all_to_all | solution.py:372
  18.7 5.8 %values.1 = bf16[128,64,128]{2,1,0:T(8,128)(2,1)S(1)} custom-call(bf16[128,128]{1,0:T(8,128)(2,1)S(1)} %copy.20.wv_ref, bf16[128,8192]{1,0:T(8,128)(2,1)S(1)} %bitcast.9), custom_call_target="tpu_custom_call" | custom-call | tf_op jit(solution)/shard_map/values/pallas_call | solution.py:51
  25.8 21.9 %all-to-all-done.1.own_ref = bf16[64,64,128]{2,1,0:T(8,128)(2,1)S(1)} async-done(((bf16[64,64,128]{2,1,0:T(8,128)(2,1)}), bf16[64,64,128]{2,1,0:T(8,128)(2,1)S(1)}, u32[]{:S(2)}, u32[]{:S(2)}) %all-to-all-start.1) | async-done | bytes 1048608 | tf_op jit(solution)/shard_map/all_to_all | solution.py:372
  47.7 7.9 %all-to-all-start = ((bf16[128,64,128]{2,1,0:T(8,128)(2,1)}), bf16[128,64,128]{2,1,0:T(8,128)(2,1)}, u32[]{:S(2)}, u32[]{:S(2)}) async-start(bf16[128,64,128]{2,1,0:T(8,128)(2,1)} %copy-done.2), calls=%async_computation | async-start | bytes 4194304 | tf_op jit(solution)/shard_map/all_to_all | solution.py:376
  55.8 8.2 %grads.1 = bf16[128,64,128]{2,1,0:T(8,128)(2,1)S(1)} custom-call(bf16[128,128]{1,0:T(8,128)(2,1)S(1)} %bitcast.12, bf16[128,128]{1,0:T(8,128)(2,1)S(1)} %copy-done.24, bf16[128,8192]{1,0:T(8,128)(2,1)S(1)} %bitcast.10, bf16[128,8192]{1,0:T(8,128)(2,1)} %bitcast.14), custom_call_target="tpu_custom_call" | custom-call | tf_op jit(solution)/shard_map/grads/pallas_call | solution.py:51
  65.4 36.6 %all-to-all-done.z_ref = bf16[128,64,128]{2,1,0:T(8,128)(2,1)} async-done(((bf16[128,64,128]{2,1,0:T(8,128)(2,1)}), bf16[128,64,128]{2,1,0:T(8,128)(2,1)}, u32[]{:S(2)}, u32[]{:S(2)}) %all-to-all-start) | async-done | bytes 2097184 | tf_op jit(solution)/shard_map/all_to_all | solution.py:376
  102.1 12.6 %all-to-all-start.3 = ((bf16[128,64,128]{2,1,0:T(8,128)(2,1)}), bf16[128,64,128]{2,1,0:T(8,128)(2,1)}, u32[]{:S(2)}, u32[]{:S(2)}) async-start(bf16[128,64,128]{2,1,0:T(8,128)(2,1)} %copy-done.1), calls=%async_computation.3 | async-start | bytes 4194304 | tf_op jit(solution)/shard_map/all_to_all | solution.py:378
  114.7 2.3 collective-permute-start
  117.0 2.3 collective-permute-done.other_ref
  121.0 8.8 %response.1.kh_ref = f32[64,128,128]{2,1,0:T(8,128)} custom-call(s32[1]{0:T(128)} %bitcast.4.core_ref, bf16[64,64,128]{2,1,0:T(8,128)(2,1)S(1)} %all-to-all-done.1.own_ref, bf16[64,64,128]{2,1,0:T(8,128)(2,1)S(1)} %collective-permute-done.other_ref, bf16[2,128,128]{2,1,0:T(8,128)(2,1)S(1)} %copy-done.18, bf16[2,128,128]{2,1,0:T(8,128)(2,1)S(1)} %copy-done.20), custom_call_target="tpu_custom_call" | custom-call | tf_op jit(solution)/shard_map/response/pallas_call | solution.py:51
  129.9 47.6 %values_transform.1 = (bf16[128,64,128]{2,1,0:T(8,128)(2,1)S(1)}, bf16[64,64,256]{2,1,0:T(8,128)(2,1)S(1)}) custom-call(bf16[128,64,128]{2,1,0:T(8,128)(2,1)} %all-to-all-done.z_ref, f32[64,128,128]{2,1,0:T(8,128)} %response.1.kh_ref, bf16[128,128]{1,0:T(8,128)(2,1)S(1)} %copy-done.10, bf16[128,128]{1,0:T(8,128)(2,1)S(1)} %copy-done.10, ...), custom_call_target="tpu_custom_call" | custom-call | tf_op jit(solution)/shard_map/values_transform/pallas_call | solution.py:51
  180.2 55.0 %grads_transform.1 = (bf16[128,64,128]{2,1,0:T(8,128)(2,1)S(1)}, bf16[64,64,128]{2,1,0:T(8,128)(2,1)S(1)}, bf16[64,64,128]{2,1,0:T(8,128)(2,1)S(1)}) custom-call(s32[1]{0:T(128)} %bitcast.4.core_ref, bf16[128,64,128]{2,1,0:T(8,128)(2,1)} %all-to-all-done.3.z_ref, f32[64,128,128]{2,1,0:T(8,128)} %response.1.kh_ref, bf16[64,64,256]{2,1,0:T(8,128)(2,1)} %copy-done.4, ...), custom_call_target="tpu_custom_call" | custom-call | tf_op jit(solution)/shard_map/grads_transform/pallas_call | solution.py:51
  235.6 2.3 collective-permute-done.1
  238.3 40.1 %all_to_all.30 = bf16[64,64,128]{2,1,0:T(8,128)(2,1)S(1)} all-to-all(bf16[64,64,128]{2,1,0:T(8,128)(2,1)S(1)} %add_convert_fusion), channel_id=1, replica_groups=mesh['zl'=2,'core'=2,'seq'=64] {'seq'}, dimensions={0} | all-to-all | bytes 2097152 | tf_op jit(solution)/shard_map/all_to_all | solution.py:409
  278.4 55.6 %all_to_all.31.conv_ref = bf16[128,64,128]{2,1,0:T(8,128)(2,1)} all-to-all(bf16[128,64,128]{2,1,0:T(8,128)(2,1)S(1)} %copy-done.9), channel_id=1, replica_groups=mesh['zl'=2,'core'=2,'seq'=64] {'zl','seq'}, dimensions={0} | all-to-all | bytes 4194304 | tf_op jit(solution)/shard_map/all_to_all | solution.py:395
  334.1 12.5 %all-to-all-start.4 = ((bf16[128,64,128]{2,1,0:T(8,128)(2,1)}), bf16[128,64,128]{2,1,0:T(8,128)(2,1)}, u32[]{:S(2)}, u32[]{:S(2)}) async-start(bf16[128,64,128]{2,1,0:T(8,128)(2,1)} %copy-done.7), calls=%async_computation.4 | async-start | bytes 4194304 | tf_op jit(solution)/shard_map/all_to_all | solution.py:407
  346.7 2.2 collective-permute-start.2
  349.0 1.5 collective-permute-done.2.recv_ref
  350.5 2.6 kernel_grad.1
  353.3 17.0 %gates.1 = (f32[128,8192]{1,0:T(8,128)}, bf16[128,8192]{1,0:T(8,128)(2,1)S(1)}) custom-call(bf16[128,128]{1,0:T(8,128)(2,1)S(1)} %copy.20.wv_ref, bf16[128,128]{1,0:T(8,128)(2,1)S(1)} %bitcast.13, bf16[128,128]{1,0:T(8,128)(2,1)S(1)} %copy-done.25, bf16[128,128]{1,0:T(8,128)(2,1)S(1)} %copy-done.17, f32[128,128]{1,0:T(8,128)S(1)} %broadcast_in_dim.2.skip_ref, ...), custom_call_target="tpu_custom_call" | custom-call | tf_op jit(solution)/shard_map/gates/pallas_call | solution.py:51
  371.6 21.4 %all-to-all-done.4.conv_ref = bf16[128,64,128]{2,1,0:T(8,128)(2,1)} async-done(((bf16[128,64,128]{2,1,0:T(8,128)(2,1)}), bf16[128,64,128]{2,1,0:T(8,128)(2,1)}, u32[]{:S(2)}, u32[]{:S(2)}) %all-to-all-start.4) | async-done | bytes 2097184 | tf_op jit(solution)/shard_map/all_to_all | solution.py:407
  393.0 1.6 copy-done.6
  394.6 9.9 %final.1 = bf16[128,8192]{1,0:T(8,128)(2,1)} custom-call(bf16[128,128]{1,0:T(8,128)(2,1)S(1)} %copy-done.26, f32[128,128]{1,0:T(8,128)S(1)} %broadcast_in_dim.2.skip_ref, f32[128,8192]{1,0:T(8,128)} %get-tuple-element.10.part_ref, bf16[128,8192]{1,0:T(8,128)(2,1)S(1)} %copy-done.6, bf16[128,64,128]{2,1,0:T(8,128)(2,1)} %all-to-all-done.4.conv_ref), custom_call_target="tpu_custom_call" | custom-call | tf_op jit(solution)/shard_map/final/pallas_call | solution.py:51
  (66 shorter events, 12.6 us)
Async XLA Ops:
  1.9 16.0 %copy-start.27 = (bf16[128,256]{1,0:T(8,128)(2,1)S(1)}, bf16[128,256]{1,0:T(8,128)(2,1)}, u32[]{:S(2)}) copy-start(bf16[128,256]{1,0:T(8,128)(2,1)} %param.19) | copy-start | bytes 196612
  2.0 16.7 %copy-start = (bf16[1,128,8192]{2,1,0:T(8,128)(2,1)S(1)}, bf16[1,128,8192]{2,1,0:T(8,128)(2,1)}, u32[]{:S(2)}) copy-start(bf16[1,128,8192]{2,1,0:T(8,128)(2,1)} %param.16) | copy-start | bytes 6291460
  4.7 43.0 %all-to-all-start.1 = ((bf16[64,64,128]{2,1,0:T(8,128)(2,1)}), bf16[64,64,128]{2,1,0:T(8,128)(2,1)S(1)}, u32[]{:S(2)}, u32[]{:S(2)}) async-start(bf16[64,64,128]{2,1,0:T(8,128)(2,1)} %copy-done.3), calls=%async_computation.1 | async-start | bytes 2097152 | tf_op jit(solution)/shard_map/all_to_all | solution.py:372
  18.6 37.1 %copy-start.16 = (bf16[128,128]{1,0:T(8,128)(2,1)}, bf16[128,128]{1,0:T(8,128)(2,1)S(1)}, u32[]{:S(2)}) copy-start(bf16[128,128]{1,0:T(8,128)(2,1)S(1)} %get-tuple-element.18.wpg_ref) | copy-start | bytes 98308
  25.8 30.0 %copy-start.24 = (bf16[128,128]{1,0:T(8,128)(2,1)S(1)}, bf16[128,128]{1,0:T(8,128)(2,1)}, u32[]{:S(2)}) copy-start(bf16[128,128]{1,0:T(8,128)(2,1)} %wo_ref.3) | copy-start | bytes 98308
  47.7 54.3 %all-to-all-start = ((bf16[128,64,128]{2,1,0:T(8,128)(2,1)}), bf16[128,64,128]{2,1,0:T(8,128)(2,1)}, u32[]{:S(2)}, u32[]{:S(2)}) async-start(bf16[128,64,128]{2,1,0:T(8,128)(2,1)} %copy-done.2), calls=%async_computation | async-start | bytes 4194304 | tf_op jit(solution)/shard_map/all_to_all | solution.py:376
  102.1 78.1 %all-to-all-start.3 = ((bf16[128,64,128]{2,1,0:T(8,128)(2,1)}), bf16[128,64,128]{2,1,0:T(8,128)(2,1)}, u32[]{:S(2)}, u32[]{:S(2)}) async-start(bf16[128,64,128]{2,1,0:T(8,128)(2,1)} %copy-done.1), calls=%async_computation.3 | async-start | bytes 4194304 | tf_op jit(solution)/shard_map/all_to_all | solution.py:378
  114.7 4.6 %collective-permute-start = (bf16[64,64,128]{2,1,0:T(8,128)(2,1)S(1)}, bf16[64,64,128]{2,1,0:T(8,128)(2,1)S(1)}, u32[]{:S(2)}, u32[]{:S(2)}) collective-permute-start(bf16[64,64,128]{2,1,0:T(8,128)(2,1)S(1)} %all-to-all-done.1.own_ref), channel_id=1, source_target_pairs={{0,64},{64,0},{1,65},{65,1},{2,66},{66,2},{3,67},{67,3},{4,68},{68... | collective-permute-start | bytes 3145736 | tf_op jit(solution)/shard_map/ppermute | solution.py:373
  121.0 8.8 %copy-start.10 = (bf16[128,128]{1,0:T(8,128)(2,1)S(1)}, bf16[128,128]{1,0:T(8,128)(2,1)}, u32[]{:S(2)}) copy-start(bf16[128,128]{1,0:T(8,128)(2,1)} %constant.38.clone.m1_ref.m2_ref) | copy-start | bytes 98308
  121.0 8.8 %copy-start.11 = (bf16[128,128]{1,0:T(8,128)(2,1)S(1)}, bf16[128,128]{1,0:T(8,128)(2,1)}, u32[]{:S(2)}) copy-start(bf16[128,128]{1,0:T(8,128)(2,1)} %constant.39.clone.n1_ref.n2_ref) | copy-start | bytes 98308
  121.0 8.8 %copy-start.12 = (bf16[256,256]{1,0:T(8,128)(2,1)S(1)}, bf16[256,256]{1,0:T(8,128)(2,1)}, u32[]{:S(2)}) copy-start(bf16[256,256]{1,0:T(8,128)(2,1)} %constant.40.clone.m3_ref) | copy-start | bytes 393220
  121.0 8.8 %copy-start.13 = (bf16[256,256]{1,0:T(8,128)(2,1)S(1)}, bf16[256,256]{1,0:T(8,128)(2,1)}, u32[]{:S(2)}) copy-start(bf16[256,256]{1,0:T(8,128)(2,1)} %constant.41.clone.n3_ref) | copy-start | bytes 393220
  121.0 8.8 %copy-start.14 = (f32[4,64,128]{2,1,0:T(8,128)S(1)}, f32[4,64,128]{2,1,0:T(8,128)}, u32[]{:S(2)}) copy-start(f32[4,64,128]{2,1,0:T(8,128)} %constant.42.clone.tw_ref) | copy-start | bytes 393220
  121.0 8.8 %copy-start.22 = (f32[2,64,128]{2,1,0:T(8,128)S(1)}, f32[2,64,128]{2,1,0:T(8,128)}, u32[]{:S(2)}) copy-start(f32[2,64,128]{2,1,0:T(8,128)} %constant.43.clone.tw2_ref) | copy-start | bytes 196612
  129.8 50.4 %copy-start.15 = (f32[4,64,128]{2,1,0:T(8,128)S(1)}, f32[4,64,128]{2,1,0:T(8,128)}, u32[]{:S(2)}) copy-start(f32[4,64,128]{2,1,0:T(8,128)} %constant.42.clone.tw_ref) | copy-start | bytes 393220
  129.8 50.4 %copy-start.19 = (bf16[2,128,128]{2,1,0:T(8,128)(2,1)S(1)}, bf16[2,128,128]{2,1,0:T(8,128)(2,1)}, u32[]{:S(2)}) copy-start(bf16[2,128,128]{2,1,0:T(8,128)(2,1)} %constant.44.clone.flips_ref) | copy-start | bytes 196612
  129.9 50.3 %copy-start.21 = (bf16[2,128,128]{2,1,0:T(8,128)(2,1)S(1)}, bf16[2,128,128]{2,1,0:T(8,128)(2,1)}, u32[]{:S(2)}) copy-start(bf16[2,128,128]{2,1,0:T(8,128)(2,1)} %constant.45.clone.lanes_ref) | copy-start | bytes 196612
  129.9 50.3 %copy-start.23 = (f32[2,64,128]{2,1,0:T(8,128)S(1)}, f32[2,64,128]{2,1,0:T(8,128)}, u32[]{:S(2)}) copy-start(f32[2,64,128]{2,1,0:T(8,128)} %constant.43.clone.tw2_ref) | copy-start | bytes 196612
  235.2 43.3 %copy-start.7 = (bf16[128,64,128]{2,1,0:T(8,128)(2,1)}, bf16[128,64,128]{2,1,0:T(8,128)(2,1)S(1)}, u32[]{:S(2)}) copy-start(bf16[128,64,128]{2,1,0:T(8,128)(2,1)S(1)} %get-tuple-element.13) | copy-start | bytes 6291460
  235.2 2.7 collective-permute-start.1
  237.9 40.5 %copy-start.9 = (bf16[128,64,128]{2,1,0:T(8,128)(2,1)S(1)}, bf16[128,64,128]{2,1,0:T(8,128)(2,1)}, u32[]{:S(2)}) copy-start(bf16[128,64,128]{2,1,0:T(8,128)(2,1)} %copy-done.8) | copy-start | bytes 6291460
  334.1 58.9 %all-to-all-start.4 = ((bf16[128,64,128]{2,1,0:T(8,128)(2,1)}), bf16[128,64,128]{2,1,0:T(8,128)(2,1)}, u32[]{:S(2)}, u32[]{:S(2)}) async-start(bf16[128,64,128]{2,1,0:T(8,128)(2,1)} %copy-done.7), calls=%async_computation.4 | async-start | bytes 4194304 | tf_op jit(solution)/shard_map/all_to_all | solution.py:407
  346.7 3.8 collective-permute-start.2
  353.2 39.7 %copy-start.26 = (bf16[128,128]{1,0:T(8,128)(2,1)S(1)}, bf16[128,128]{1,0:T(8,128)(2,1)}, u32[]{:S(2)}) copy-start(bf16[128,128]{1,0:T(8,128)(2,1)} %get-tuple-element.20.wpv_ref) | copy-start | bytes 98308
  (12 other events, 30.7 us)

commit v2 on v1

v2 whole, which is shorter than its diff:
```python
import functools
import math

import jax
import jax.numpy as jnp
import numpy as np
from jax import lax
from jax.experimental import pallas as pl
from jax.experimental.pallas import tpu as pltpu
from jax.sharding import Mesh, PartitionSpec as P

BF = jnp.bfloat16
F32 = jnp.float32
F2 = 64
F3 = 128
LANES = 128


def dft_blocks(length, direction):
    ids = np.arange(length)
    angles = (ids[:, None] * ids[None, :] % length).astype(np.float32) * np.float32(
        2.0 * math.pi / length
    )
    scale = np.float32(1.0 / math.sqrt(length))
    real = np.cos(angles) * scale
    imag = direction * np.sin(angles) * scale
    return np.block([[real, -imag], [imag, real]]).astype(np.float32)


def turns(ids, modulus):
    angles = (ids % modulus).astype(np.float64) * (2.0 * math.pi / modulus)
    return np.stack([np.cos(angles), np.sin(angles)]).astype(np.float32)


def flip_matrix(size, shift):
    out = np.zeros((size, size), np.float32)
    for j in range(size):
        out[j, (size - shift - j) % size] = 1.0
    return out


def vmem_specs(count):
    return [pl.BlockSpec(memory_space=pltpu.VMEM)] * count


SMEM_SPEC = pl.BlockSpec(memory_space=pltpu.SMEM)


def call(body, out_shape, scratch, *args, smem=0, name, micros=20):
    multi = isinstance(out_shape, (tuple, list))
    return pl.pallas_call(
        body,
        out_shape=out_shape,
        in_specs=[SMEM_SPEC] * smem + vmem_specs(len(args) - smem),
        out_specs=vmem_specs(len(out_shape)) if multi else vmem_specs(1)[0],
        scratch_shapes=scratch,
        compiler_params=pltpu.CompilerParams(vmem_limit_bytes=48 << 20),
        cost_estimate=cost(micros),
        name=name,
    )(*args)


def cost(micros):
    return pl.CostEstimate(
        flops=micros * 10**9, transcendentals=0, bytes_accessed=micros * 3 * 10**6
    )


def dot(a, b):
    return jnp.dot(a, b, preferred_element_type=F32)


def loop(count, body, unroll=1):
    def step(i, carry):
        body(i)
        return carry

    lax.fori_loop(0, count, step, 0, unroll=unroll)


def loop_carry(count, body, init, unroll=1):
    return lax.fori_loop(0, count, body, init, unroll=unroll)


def lane_block(ref, i, rows=None):
    window = pl.ds(pl.multiple_of(i * LANES, LANES), LANES)
    return ref[:, window] if rows is None else ref[rows, window]


PAD = 2
TURN = 8
BATCH = 4


def turn_row(block, signal):
    return 2 * TURN * (block // TURN) + TURN * signal + block % TURN


def lane_part(x, i):
    return x[:, i * LANES : (i + 1) * LANES]


def row_part(x, i, size):
    return x[i * size : (i + 1) * size]


def dot_first(a, b):
    return lax.dot_general(a, b, (((0,), (0,)), ((), ())), preferred_element_type=F32)


def spread_body(x_ref, out_ref, rows_ref):
    channels, blocks, _ = out_ref.shape

    def put(i):
        rows_ref[pl.ds(i * (channels + PAD), channels), :] = lane_block(x_ref, i).astype(F32)

    loop(blocks, put, 4)

    def take(c):
        out_ref[c] = rows_ref[pl.ds(c, blocks, stride=channels + PAD), :].astype(BF)

    loop(channels, take, 4)


def unpack_rows(x_ref, rows_ref, offset=0, blocks=None):
    items = x_ref.shape[0]
    blocks = blocks or x_ref.shape[1]

    def put(c):
        block = x_ref[c, offset : offset + blocks, :]
        rows_ref[pl.ds(c * (blocks + PAD), blocks), :] = block.astype(F32)

    loop(items, put, 4)


def signals_body(wp_ref, wo_ref, tok_ref, cot_ref, out_ref, values_ref, grads_ref):
    channels = out_ref.shape[0]
    pitch = channels + PAD
    for p in range(TURN // 2):
        window = slice(2 * p * LANES, (2 * p + 2) * LANES)
        both = dot_first(wp_ref[...], tok_ref[:, window])
        values = both[:channels]
        grads = dot(wo_ref[...], cot_ref[:, window]) * both[channels:]
        for side in range(2):
            at = slice((2 * p + side) * pitch, (2 * p + side) * pitch + channels)
            values_ref[at, :] = lane_part(values, side)
            grads_ref[at, :] = lane_part(grads, side)

    def take(c):
        window = pl.ds(c, TURN, stride=pitch)
        out_ref[c] = jnp.concatenate(
            [values_ref[window, :], grads_ref[window, :]], axis=0
        ).astype(BF)

    loop(channels, take, 8)


def rotate(re, im, cos_part, sin_part):
    return re * cos_part - im * sin_part, re * sin_part + im * cos_part


def first_stage(rows_ref, signal, m1_ref, tw_ref, mid_ref):
    count = m1_ref.shape[0]
    half = count // 2
    pitch, mid = 2 * F2 + PAD, F2 + PAD

    def step(j, turn):
        cos_part, sin_part = turn
        at = turn_row(2 * j, signal)
        x = jnp.concatenate(
            [rows_ref[pl.ds(at + side, count, stride=pitch), :] for side in range(2)], axis=1
        )
        y = dot(m1_ref[...], x.astype(BF))
        re, im = rotate(y[:half], y[half:], cos_part, -sin_part)
        for side in range(2):
            mid_ref[pl.ds(2 * j + side, half, stride=2 * mid), :] = lane_part(re, side)
            mid_ref[pl.ds(mid + 2 * j + side, half, stride=2 * mid), :] = lane_part(im, side)
        return rotate(cos_part, sin_part, tw_ref[2], tw_ref[3])

    loop_carry(F2 // 2, step, (tw_ref[0], tw_ref[1]), 4)


def last_stage(rows_ref, signal, m1_ref, tw_ref, mid_ref):
    count = m1_ref.shape[0]
    half = count // 2
    pitch, mid = 2 * F2 + PAD, F2 + PAD

    def step(j, turn):
        cos_part, sin_part = turn
        parts = []
        for part in range(2):
            sides = [
                mid_ref[pl.ds(part * mid + 2 * j + side, half, stride=2 * mid), :]
                for side in range(2)
            ]
            parts.append(jnp.concatenate(sides, axis=1))
        re, im = rotate(parts[0], parts[1], cos_part, sin_part)
        y = dot(m1_ref[...], jnp.concatenate([re, im], axis=0).astype(BF))
        at = turn_row(2 * j, signal)
        for side in range(2):
            rows_ref[pl.ds(at + side, count, stride=pitch), :] = lane_part(y, side)
        return rotate(cos_part, sin_part, tw_ref[2], tw_ref[3])

    loop_carry(F2 // 2, step, (tw_ref[0], tw_ref[1]), 4)


def part_rows(k1, part):
    return pl.ds((2 * k1 + part) * (F2 + PAD), F2)


def to_spectrum(mid_ref, first, m2_ref, m3_ref, tw2_ref):
    stacked = []
    for p in range(BATCH // 2):
        pair = [
            jnp.concatenate([mid_ref[part_rows(k1, 0), :], mid_ref[part_rows(k1, 1), :]], axis=0)
            for k1 in (first + 2 * p, first + 2 * p + 1)
        ]
        y = dot(m2_ref[...], jnp.concatenate(pair, axis=1).astype(BF))
        re, im = rotate(y[:F2], y[F2:], tw2_ref[0], -tw2_ref[1])
        for side in range(2):
            stacked.append(
                jnp.concatenate([lane_part(re, side), lane_part(im, side)], axis=1).astype(BF)
            )
    return dot(jnp.concatenate(stacked, axis=0), m3_ref[...]).astype(BF)


def from_spectrum(mid_ref, first, blocks, m2_ref, m3_ref, tw2_ref):
    stacked = [jnp.concatenate(block, axis=1).astype(BF) for block in blocks]
    y = dot(jnp.concatenate(stacked, axis=0), m3_ref[...])
    for p in range(BATCH // 2):
        sides = [row_part(y, 2 * p + side, F2) for side in range(2)]
        re, im = rotate(
            jnp.concatenate([lane_part(s, 0) for s in sides], axis=1),
            jnp.concatenate([lane_part(s, 1) for s in sides], axis=1),
            tw2_ref[0],
            tw2_ref[1],
        )
        z = dot(m2_ref[...], jnp.concatenate([re, im], axis=0).astype(BF))
        for side in range(2):
            k1 = first + 2 * p + side
            mid_ref[part_rows(k1, 0), :] = lane_part(z[:F2], side)
            mid_ref[part_rows(k1, 1), :] = lane_part(z[F2:], side)


def split(spec):
    spec = spec.astype(F32)
    return spec[:, :F3], spec[:, F3:]


def spectra_body(
    core_ref, z_ref, m1_ref, m2_ref, m3_ref, tw_ref, tw2_ref,
    values_ref, grads_ref, keep_ref, send_ref, rows_ref, mid_ref,
):
    count = values_ref.shape[0]
    on_core_zero = core_ref[0] == 0
    unpack_rows(z_ref, rows_ref)
    first_stage(rows_ref, 0, m1_ref, tw_ref, mid_ref)

    def values(b):
        spec = to_spectrum(mid_ref, b * BATCH, m2_ref, m3_ref, tw2_ref)
        for t in range(BATCH):
            values_ref[b * BATCH + t] = row_part(spec, t, F2)

    loop(count // BATCH, values)
    first_stage(rows_ref, 1, m1_ref, tw_ref, mid_ref)

    def grads(b):
        spec = to_spectrum(mid_ref, b * BATCH, m2_ref, m3_ref, tw2_ref)
        for t in range(BATCH):
            k1 = b * BATCH + t
            grad = row_part(spec, t, F2)
            grads_ref[k1] = grad
            value_re, value_im = split(values_ref[k1])
            re, im = rotate(*split(grad), value_re, -value_im)
            keep_ref[k1] = jnp.where(on_core_zero, re, im).astype(BF)
            send_ref[k1] = jnp.where(on_core_zero, im, re).astype(BF)

    loop(count // BATCH, grads)


def hermitian(ref, sign, flip_rows_ref, flip_lanes_ref, head_rows_ref, head_lanes_ref, store):
    count = ref.shape[0]
    head = ref[0]
    turned = dot(head_rows_ref[...], dot(head, flip_lanes_ref[...]).astype(BF))
    first = dot(head_rows_ref[...], dot(head, head_lanes_ref[...]).astype(BF))
    row = lax.broadcasted_iota(jnp.int32, turned.shape, 0)
    store(0, 0.5 * (head.astype(F32) + sign * jnp.where(row == 0, first, turned)))

    def batch(b, keep=BATCH):
        low = count - BATCH - b * BATCH
        rows = jnp.concatenate([ref[low + t] for t in range(BATCH)], axis=0)
        turned = dot(flip_rows_ref[...], dot(rows, flip_lanes_ref[...]).astype(BF))
        for t in range(keep):
            k1 = b * BATCH + 1 + t
            store(k1, 0.5 * (ref[k1].astype(F32) + sign * row_part(turned, t, F2)))

    loop(count // BATCH - 1, batch, 3)
    batch(count // BATCH - 1, BATCH - 1)


def terms_body(
    core_ref, keep_ref, recv_ref, flip_rows_ref, flip_lanes_ref, head_rows_ref, head_lanes_ref,
    out_ref, sum_ref,
):
    sign = jnp.where(core_ref[0] == 0, 1.0, -1.0)

    def add(k1):
        sum_ref[k1] = (keep_ref[k1].astype(F32) + recv_ref[k1].astype(F32)).astype(BF)

    loop(keep_ref.shape[0], add, 4)

    def store(k1, block):
        out_ref[k1] = block.astype(BF)

    hermitian(
        sum_ref, sign, flip_rows_ref, flip_lanes_ref, head_rows_ref, head_lanes_ref, store
    )


def response_body(
    core_ref, own_ref, flip_rows_ref, flip_lanes_ref, head_rows_ref, head_lanes_ref, out_ref
):
    sign = jnp.where(core_ref[0] == 0, 1.0, -1.0)

    def store(k1, block):
        out_ref[k1] = block.astype(BF)

    hermitian(
        own_ref, sign, flip_rows_ref, flip_lanes_ref, head_rows_ref, head_lanes_ref, store
    )


def inverse_body(
    core_ref, own_ref, other_ref, values_ref, grads_ref, m1_ref, m2_ref, m3_ref,
    tw_ref, tw2_ref, out_ref, rows_ref, mid_ref,
):
    on_core_zero = core_ref[0] == 0
    count = own_ref.shape[0]

    for signal, spec_ref in ((0, values_ref), (1, grads_ref)):

        def product(b, signal=signal, spec_ref=spec_ref):
            blocks = []
            for t in range(BATCH):
                k1 = b * BATCH + t
                own, other = own_ref[k1].astype(F32), other_ref[k1].astype(F32)
                kern_re = jnp.where(on_core_zero, own, other)
                kern_im = jnp.where(on_core_zero, other, own)
                if signal:
                    kern_im = -kern_im
                blocks.append(rotate(*split(spec_ref[k1]), kern_re, kern_im))
            from_spectrum(mid_ref, b * BATCH, blocks, m2_ref, m3_ref, tw2_ref)

        loop(count // BATCH, product)
        last_stage(rows_ref, signal, m1_ref, tw_ref, mid_ref)

    items, blocks, _ = out_ref.shape

    def put(c):
        out_ref[c] = rows_ref[pl.ds(c * (blocks + PAD), blocks), :].astype(BF)

    loop(items, put, 2)


def home_body(wp_ref, wo_ref, skip_ref, tok_ref, cot_ref, direct_ref, own_ref, hidden_ref):
    channels = tok_ref.shape[0]
    for p in range(TURN // 2):
        window = slice(2 * p * LANES, (2 * p + 2) * LANES)
        both = dot_first(wp_ref[...], tok_ref[:, window])
        values, gates = both[:channels].astype(BF).astype(F32), both[channels:]
        hidden = dot(wo_ref[...], cot_ref[:, window])
        direct_ref[:, window] = skip_ref[...] * values
        own_ref[:, window] = skip_ref[...] * (hidden * gates).astype(BF).astype(F32)
        hidden_ref[:, window] = hidden


def final_body(wp_ref, direct_ref, own_ref, hidden_ref, got_ref, out_ref, rows_ref):
    channels = got_ref.shape[0]
    pitch = 2 * TURN + PAD
    unpack_rows(got_ref, rows_ref)
    for p in range(TURN // 2):
        window = slice(2 * p * LANES, (2 * p + 2) * LANES)
        conv, back = (
            jnp.concatenate(
                [
                    rows_ref[pl.ds(signal * TURN + 2 * p + side, channels, stride=pitch), :]
                    for side in range(2)
                ],
                axis=1,
            )
            for signal in range(2)
        )
        grad = back + own_ref[:, window]
        mixed = conv + direct_ref[:, window]
        stacked = jnp.concatenate([grad, hidden_ref[:, window] * mixed], axis=0).astype(BF)
        out_ref[:, window] = dot(wp_ref[...], stacked).astype(BF)


def chunked(body, name, micros, small, chunks, outs, messages=(), scratch=()):
    steps = chunks[0].shape[1] // (TURN * LANES)
    whole = [pl.BlockSpec(a.shape, lambda i: (0, 0)) for a in small]
    wide = lambda a: pl.BlockSpec((a.shape[0], TURN * LANES), lambda i: (0, i))
    turn = lambda a: pl.BlockSpec((a.shape[0], 2 * TURN, LANES), lambda i: (0, i, 0))
    spec = lambda a: wide(a) if len(a.shape) == 2 else turn(a)
    result = pl.pallas_call(
        body,
        grid=(steps,),
        out_shape=outs,
        in_specs=whole + [spec(a) for a in chunks + tuple(messages)],
        out_specs=[spec(a) for a in outs],
        scratch_shapes=list(scratch),
        compiler_params=pltpu.CompilerParams(vmem_limit_bytes=32 << 20),
        cost_estimate=cost(micros),
        name=name,
    )(*small, *(in_hbm(a) for a in chunks + tuple(messages)))
    return result


def in_hbm(a):
    return pltpu.with_memory_space_constraint(a, pltpu.HBM)


def kernel_grad_body(core_ref, keep_ref, recv_ref, out_ref, rows_ref):
    channels, blocks, _ = keep_ref.shape
    core = core_ref[0]
    for ref, part in ((keep_ref, core), (recv_ref, 1 - core)):
        unpack_rows(ref, rows_ref)

        def step(i, part=part):
            window = pl.ds(pl.multiple_of(i * LANES, LANES), LANES)
            rows = rows_ref[pl.ds(i, channels, stride=blocks + PAD), :]
            out_ref[part, :, window] = rows.astype(BF)

        loop(blocks, step, 4)


SWAP = [(0, 1), (1, 0)]


def per_device(tokens, kernel, skip, w_proj, w_out, cotangent):
    first_len = lax.axis_size("seq")
    core = lax.axis_index("core")
    z_low = lax.axis_index("zl")
    channels, positions = tokens.shape[1:]
    whole = first_len * positions
    core_arr = core.astype(jnp.int32).reshape(1)
    tok = tokens.reshape(channels, positions)
    cot = cotangent.reshape(channels, positions)
    blocks = positions // LANES
    shaped = functools.partial(jax.ShapeDtypeStruct)

    bf = functools.partial(jnp.asarray, dtype=BF)
    skip_full = jnp.broadcast_to(skip[:, None], (channels, 2 * LANES))
    m1, n1 = bf(dft_blocks(first_len, -1.0)), bf(dft_blocks(first_len, 1.0))
    m2, n2 = bf(dft_blocks(F2, -1.0)), bf(dft_blocks(F2, 1.0))
    m3, n3 = bf(dft_blocks(F3, -1.0).T), bf(dft_blocks(F3, 1.0).T)
    freq = np.arange(first_len)[:, None]
    pair = np.arange(2 * F3)[None, :]
    tw = jnp.asarray(
        np.concatenate(
            [turns(freq * pair, whole), turns(freq * np.full_like(pair, 2 * F3), whole)]
        )
    )
    tw2 = turns(np.arange(F2)[:, None] * np.arange(F3)[None, :], F2 * F3)
    tw2 = jnp.asarray(np.concatenate([tw2, tw2], axis=2))
    flips = (
        bf(flip_matrix(BATCH * F2, 1)),
        bf(flip_matrix(F3, 1)),
        bf(flip_matrix(F2, 0)),
        bf(flip_matrix(F3, 0)),
    )

    exchange = functools.partial(lax.all_to_all, split_axis=0, concat_axis=0, tiled=True)
    share = first_len
    half = share // 2
    pair_rows = pltpu.VMEM((2 * first_len * (2 * F2 + PAD), F3), F32)
    mid_rows = pltpu.VMEM((2 * first_len * (F2 + PAD), F3), F32)
    part = shaped((share, blocks, LANES), BF)

    turn_rows = pltpu.VMEM((TURN * (channels + PAD), LANES), F32)
    (signals,) = chunked(
        signals_body, "signals", 8, (w_proj, w_out), (tok, cot),
        (pltpu.HBM((channels, 2 * blocks, LANES), BF),), (), (turn_rows, turn_rows),
    )
    signals = exchange(signals, ("zl", "seq"))
    chosen = lax.dynamic_slice(kernel, (core, z_low * share, 0), (1, share, positions))[0]
    response = call(
        spread_body, part, [pltpu.VMEM((blocks * (share + PAD), LANES), F32)],
        chosen, name="spread", micros=3,
    )
    response, signals = lax.optimization_barrier((response, signals))
    response = exchange(response, "seq")
    spectrum = shaped((first_len, F2, 2 * F3), BF)
    values, grads, keep, send = call(
        spectra_body,
        (spectrum, spectrum, part, part),
        [pair_rows, mid_rows],
        core_arr, signals, m1, m2, m3, tw, tw2,
        smem=1, name="spectra", micros=20,
    )
    terms = call(
        terms_body, part, [pltpu.VMEM((first_len, F2, F3), BF)],
        core_arr, keep, lax.ppermute(send, "core", SWAP), *flips,
        smem=1, name="terms", micros=4,
    )
    terms, response = lax.optimization_barrier((terms, response))
    terms = exchange(terms, "seq")
    response = call(
        response_body, part, [], core_arr, response, *flips, smem=1, name="response", micros=4
    )
    received = call(
        inverse_body,
        shaped((2 * first_len, 2 * F2, F3), BF),
        [pair_rows, mid_rows],
        core_arr, response, lax.ppermute(response, "core", SWAP), values, grads,
        n1, n2, n3, tw, tw2,
        smem=1, name="inverse", micros=20,
    )
    received, terms = lax.optimization_barrier((received, terms))
    received = exchange(received, ("zl", "seq"))
    kept = lax.dynamic_slice_in_dim(terms, core * half, half, 0)
    sent = lax.dynamic_slice_in_dim(terms, (1 - core) * half, half, 0)
    kernel_grad = call(
        kernel_grad_body,
        shaped((2, half, positions), BF),
        [pltpu.VMEM((half * (blocks + PAD), LANES), F32)],
        core_arr, kept, lax.ppermute(sent, "core", SWAP),
        smem=1, name="kernel_grad", micros=3,
    )
    wide = pltpu.HBM((channels, positions), F32)
    direct, own, hidden = chunked(
        home_body, "home", 8, (w_proj, w_out, skip_full), (tok, cot), (wide, wide, wide)
    )
    (input_grad,) = chunked(
        final_body, "final", 8, (w_proj,), (direct, own, hidden),
        (pltpu.HBM((channels, positions), BF),), (received,),
        (pltpu.VMEM((channels * (2 * TURN + PAD), LANES), F32),),
    )
    return input_grad.reshape(1, channels, positions), kernel_grad


def solution(mesh):
    sequences, groups = mesh.devices.shape
    fine = Mesh(mesh.devices.reshape(2, sequences // 2, groups), ("zl", "core", "seq"))
    dp = ("zl", "core")
    placed = (P(dp, None, "seq"), P(None, None, "seq"), P(), P(), P(), P(dp, None, "seq"))
    return jax.shard_map(
        per_device,
        mesh=fine,
        in_specs=placed,
        out_specs=(P(dp, None, "seq"), P(None, dp, "seq")),
        check_vma=False,
    )
```

time: 410 us -> 321 us (0.78)
  blocking collectives: 95.7 us -> 0 us
  waiting for transfers between devices: 86.1 us -> 177 us
  Pallas kernels: 157 us -> 79.7 us
  local copies, waits for them, and re-layouts: 13.3 us -> 7.25 us
    all_to_all x3, waiting for transfers between devices: 58 us -> 175 us  [the longest x1 88.9 us: per_device(): signals = exchange(signals, ('zl', 'seq'))]
    pallas_call x9 -> x6, Pallas kernels: 157 us -> 52.1 us  [call(): pl.pallas_call(body, out_shape=out_shape, in_specs=[SMEM_SPEC] * smem + v...]
    all_to_all x2 -> x0, blocking collectives: 95.7 us -> none  [the longest x1 55.6 us: per_device(): conv = exchange(conv, ('zl', 'seq'))]
    pallas_call x0 -> x3, Pallas kernels: none -> 27.6 us  [chunked(): pl.pallas_call(body, grid=(steps,), out_shape=outs, in_specs=whole + [spe...]
    all_to_all x1, waiting for transfers between devices: 21.9 us -> 0.01 us  [per_device(): response = exchange(response, 'seq')]
    unnamed x59 -> x34, local copies, waits for them, and re-layouts: 11.1 us -> 4.6 us
  transfers between devices with their start and end apart: 7 -> 7, of which waited for: 6 -> 4; matrix products, arithmetic and copies ran while one was open for 0% -> 1% of each run, Pallas kernels for 22% -> 18%
where the time goes in v2:
time: 321 us; the launch traced here: 315 us
  waiting for transfers between devices  177 us (55%)
  Pallas kernels  79.7 us (25%)
  starting transfers between devices  50.4 us (16%)
  local copies, waits for them, and re-layouts  7.25 us (2%)
    all_to_all x1, waiting for transfers between devices, per_device(): signals = exchange(signals, ('zl', 'seq'))  88.9 us
    all_to_all x1, waiting for transfers between devices, per_device(): received = exchange(received, ('zl', 'seq'))  78.3 us
    pallas_call x6, Pallas kernels, call(): pl.pallas_call(body, out_shape=out_shape, in_specs=[SMEM_SPEC] * smem + v...  52.1 us
    pallas_call x3, Pallas kernels, chunked(): pl.pallas_call(body, grid=(steps,), out_shape=outs, in_specs=whole + [spe...  27.6 us
    all_to_all x1, starting transfers between devices, per_device(): signals = exchange(signals, ('zl', 'seq'))  15.2 us
    all_to_all x1, starting transfers between devices, per_device(): terms = exchange(terms, 'seq')  12.4 us
    all_to_all x1, starting transfers between devices, per_device(): response = exchange(response, 'seq')  10.3 us
    all_to_all x1, starting transfers between devices, per_device(): received = exchange(received, ('zl', 'seq'))  7.91 us
  transfers between devices with their start and end apart: 7, of which 4 were waited for; matrix products, arithmetic and copies ran while one was open for 1% of the time, Pallas kernels for 18%

profile of v2, /device:TPU:35, one launch (start us, length us, event | category | flops | bytes accessed | tf_op | source)
XLA Modules:
  0.0 315.1 jit_solution(18319795850708577149)
XLA Ops:
  0.6 0.8 copy-done
  2.2 8.3 %signals.1 = bf16[128,128,128]{2,1,0:T(8,128)(2,1)} custom-call(bf16[128,256]{1,0:T(8,128)(2,1)S(1)} %copy-done, bf16[128,128]{1,0:T(8,128)(2,1)S(1)} %copy-done.2, bf16[128,8192]{1,0:T(8,128)(2,1)} %bitcast.6, bf16[128,8192]{1,0:T(8,128)(2,1)} %bitcast.8), custom_call_target="tpu_custom_call" | custom-call | flops 8000000000 | bytes 24000000 | tf_op jit(solution)/shard_map/signals/pallas_call | solution.py:405
  10.5 15.2 %all-to-all-start = ((bf16[128,128,128]{2,1,0:T(8,128)(2,1)}), bf16[128,128,128]{2,1,0:T(8,128)(2,1)}, u32[]{:S(2)}, u32[]{:S(2)}) async-start(bf16[128,128,128]{2,1,0:T(8,128)(2,1)} %signals.1), calls=%async_computation | async-start | bytes 8388608 | tf_op jit(solution)/shard_map/all_to_all | solution.py:485
  25.7 1.3 dynamic-slice_bitcast_fusion.x_ref
  27.1 1.5 spread.1
  28.6 88.9 %all-to-all-done.z_ref = bf16[128,128,128]{2,1,0:T(8,128)(2,1)} async-done(((bf16[128,128,128]{2,1,0:T(8,128)(2,1)}), bf16[128,128,128]{2,1,0:T(8,128)(2,1)}, u32[]{:S(2)}, u32[]{:S(2)}) %all-to-all-start) | async-done | bytes 4194336 | tf_op jit(solution)/shard_map/all_to_all | solution.py:485
  117.5 10.3 %all-to-all-start.1 = ((bf16[64,64,128]{2,1,0:T(8,128)(2,1)}), bf16[64,64,128]{2,1,0:T(8,128)(2,1)S(1)}, u32[]{:S(2)}, u32[]{:S(2)}) async-start(bf16[64,64,128]{2,1,0:T(8,128)(2,1)} %spread.1), calls=%async_computation.1 | async-start | bytes 2097152 | tf_op jit(solution)/shard_map/all_to_all | solution.py:492
  127.9 19.3 %spectra.1 = (bf16[64,64,256]{2,1,0:T(8,128)(2,1)S(1)}, bf16[64,64,256]{2,1,0:T(8,128)(2,1)}, bf16[64,64,128]{2,1,0:T(8,128)(2,1)S(1)}, bf16[64,64,128]{2,1,0:T(8,128)(2,1)S(1)}) custom-call(s32[1]{0:T(128)} %bitcast.2.core_ref, bf16[128,128,128]{2,1,0:T(8,128)(2,1)} %all-to-all-done.z_ref, bf16[128,128]{1,0:T(8,128)(2,1)S(1)} %copy-done.12, ...), custom_call_target="tpu_custom_call" | custom-call | flops 20000000000 | bytes 60000000 | tf_op jit(solution)/shard_map/spectra/pallas_call | solution.py:51
  147.1 1.4 copy-done.14
  148.5 2.5 collective-permute-start
  151.0 2.3 collective-permute-done.recv_ref
  153.3 4.9 %terms.1 = bf16[64,64,128]{2,1,0:T(8,128)(2,1)} custom-call(s32[1]{0:T(128)} %bitcast.2.core_ref, bf16[64,64,128]{2,1,0:T(8,128)(2,1)S(1)} %get-tuple-element.19.keep_ref, bf16[64,64,128]{2,1,0:T(8,128)(2,1)S(1)} %collective-permute-done.recv_ref, bf16[256,256]{1,0:T(8,128)(2,1)S(1)} %copy-done.7, bf16[128,128]{1,0:T(8,128)(2,1)S(1)} %copy-done.11, ...), custom_call_target="tpu_custom_call" | custom-call | flops 4000000000 | bytes 12000000 | tf_op jit(solution)/shard_map/terms/pallas_call | solution.py:51
  158.2 3.6 %response.1.own_ref = bf16[64,64,128]{2,1,0:T(8,128)(2,1)S(1)} custom-call(s32[1]{0:T(128)} %bitcast.2.core_ref, bf16[64,64,128]{2,1,0:T(8,128)(2,1)S(1)} %all-to-all-done.1.own_ref, bf16[256,256]{1,0:T(8,128)(2,1)S(1)} %copy-done.7, bf16[128,128]{1,0:T(8,128)(2,1)S(1)} %copy-done.11, bf16[64,64]{1,0:T(8,128)(2,1)S(1)} %copy-done.13, ...), custom_call_target="tpu_custom_call" | custom-call | flops 4000000000 | bytes 12000000 | tf_op jit(solution)/shard_map/response/pallas_call | solution.py:51
  162.3 12.4 %all-to-all-start.2 = ((bf16[64,64,128]{2,1,0:T(8,128)(2,1)}), bf16[64,64,128]{2,1,0:T(8,128)(2,1)}, u32[]{:S(2)}, u32[]{:S(2)}) async-start(bf16[64,64,128]{2,1,0:T(8,128)(2,1)} %terms.1), calls=%async_computation.2 | async-start | bytes 2097152 | tf_op jit(solution)/shard_map/all_to_all | solution.py:507
  174.7 1.6 copy-done.15
  176.3 21.2 %inverse.1 = bf16[128,128,128]{2,1,0:T(8,128)(2,1)} custom-call(s32[1]{0:T(128)} %bitcast.2.core_ref, bf16[64,64,128]{2,1,0:T(8,128)(2,1)S(1)} %response.1.own_ref, bf16[64,64,128]{2,1,0:T(8,128)(2,1)S(1)} %collective-permute-done.1.other_ref, bf16[64,64,256]{2,1,0:T(8,128)(2,1)S(1)} %copy-done.15, bf16[64,64,256]{2,1,0:T(8,128)(2,1)} %get-tuple-element.24.grads_ref, ...), custom_call_target="tpu_custom_call" | custom-call | flops 20000000000 | bytes 60000000 | tf_op jit(solution)/shard_map/inverse/pallas_call | solution.py:51
  197.5 7.4 %all-to-all-done.2 = bf16[64,64,128]{2,1,0:T(8,128)(2,1)} async-done(((bf16[64,64,128]{2,1,0:T(8,128)(2,1)}), bf16[64,64,128]{2,1,0:T(8,128)(2,1)}, u32[]{:S(2)}, u32[]{:S(2)}) %all-to-all-start.2) | async-done | bytes 1048608 | tf_op jit(solution)/shard_map/all_to_all | solution.py:507
  204.9 7.9 %all-to-all-start.3 = ((bf16[128,128,128]{2,1,0:T(8,128)(2,1)}), bf16[128,128,128]{2,1,0:T(8,128)(2,1)}, u32[]{:S(2)}, u32[]{:S(2)}) async-start(bf16[128,128,128]{2,1,0:T(8,128)(2,1)} %inverse.1), calls=%async_computation.3 | async-start | bytes 8388608 | tf_op jit(solution)/shard_map/all_to_all | solution.py:520
  212.8 1.3 constant_dynamic-slice_fusion
  214.1 1.6 collective-permute-start.2
  215.8 9.1 %home.1 = (f32[128,8192]{1,0:T(8,128)}, f32[128,8192]{1,0:T(8,128)}, f32[128,8192]{1,0:T(8,128)}) custom-call(bf16[128,256]{1,0:T(8,128)(2,1)S(1)} %copy-done.1, bf16[128,128]{1,0:T(8,128)(2,1)S(1)} %copy-done.3, f32[128,256]{1,0:T(8,128)S(1)} %broadcast_in_dim.2.skip_ref, bf16[128,8192]{1,0:T(8,128)(2,1)} %bitcast.7, bf16[128,8192]{1,0:T(8,128)(2,1)} %bitcast.9), custom_call_target="tpu_custom_call" | custom-call | flops 8000000000 | bytes 24000000 | tf_op jit(solution)/shard_map/home/pallas_call | solution.py:405
  225.0 1.6 kernel_grad.1
  226.5 78.3 %all-to-all-done.3.got_ref = bf16[128,128,128]{2,1,0:T(8,128)(2,1)} async-done(((bf16[128,128,128]{2,1,0:T(8,128)(2,1)}), bf16[128,128,128]{2,1,0:T(8,128)(2,1)}, u32[]{:S(2)}, u32[]{:S(2)}) %all-to-all-start.3) | async-done | bytes 4194336 | tf_op jit(solution)/shard_map/all_to_all | solution.py:520
  304.9 10.2 %final.1 = bf16[128,8192]{1,0:T(8,128)(2,1)} custom-call(bf16[128,256]{1,0:T(8,128)(2,1)S(1)} %copy-done.1, f32[128,8192]{1,0:T(8,128)} %get-tuple-element.15.direct_ref, f32[128,8192]{1,0:T(8,128)} %get-tuple-element.16.own_ref, f32[128,8192]{1,0:T(8,128)} %get-tuple-element.17.hidden_ref, bf16[128,128,128]{2,1,0:T(8,128)(2,1)} %all-to-all-done.3.got_ref), custom_call_target="tpu_custom_call" | custom-call | flops 8000000000 | bytes 24000000 | tf_op jit(solution)/shard_map/final/pallas_call | solution.py:405
  (36 shorter events, 1.4 us)
Async XLA Ops:
  0.6 0.8 copy-start
  1.5 0.8 copy-start.2
  10.5 107.0 %all-to-all-start = ((bf16[128,128,128]{2,1,0:T(8,128)(2,1)}), bf16[128,128,128]{2,1,0:T(8,128)(2,1)}, u32[]{:S(2)}, u32[]{:S(2)}) async-start(bf16[128,128,128]{2,1,0:T(8,128)(2,1)} %signals.1), calls=%async_computation | async-start | bytes 8388608 | tf_op jit(solution)/shard_map/all_to_all | solution.py:485
  27.0 100.8 %copy-start.4 = (f32[4,64,256]{2,1,0:T(8,128)S(1)}, f32[4,64,256]{2,1,0:T(8,128)}, u32[]{:S(2)}) copy-start(f32[4,64,256]{2,1,0:T(8,128)} %constant.46.clone.tw_ref) | copy-start | bytes 786436
  27.0 100.8 %copy-start.5 = (f32[2,64,256]{2,1,0:T(8,128)S(1)}, f32[2,64,256]{2,1,0:T(8,128)}, u32[]{:S(2)}) copy-start(f32[2,64,256]{2,1,0:T(8,128)} %constant.47.clone.tw2_ref) | copy-start | bytes 393220
  27.0 100.8 %copy-start.8 = (bf16[256,256]{1,0:T(8,128)(2,1)S(1)}, bf16[256,256]{1,0:T(8,128)(2,1)}, u32[]{:S(2)}) copy-start(bf16[256,256]{1,0:T(8,128)(2,1)} %constant.44.clone.m3_ref) | copy-start | bytes 393220
  27.0 100.8 %copy-start.12 = (bf16[128,128]{1,0:T(8,128)(2,1)S(1)}, bf16[128,128]{1,0:T(8,128)(2,1)}, u32[]{:S(2)}) copy-start(bf16[128,128]{1,0:T(8,128)(2,1)} %constant.42.clone.m1_ref.m2_ref) | copy-start | bytes 98308
  117.5 40.7 %all-to-all-start.1 = ((bf16[64,64,128]{2,1,0:T(8,128)(2,1)}), bf16[64,64,128]{2,1,0:T(8,128)(2,1)S(1)}, u32[]{:S(2)}, u32[]{:S(2)}) async-start(bf16[64,64,128]{2,1,0:T(8,128)(2,1)} %spread.1), calls=%async_computation.1 | async-start | bytes 2097152 | tf_op jit(solution)/shard_map/all_to_all | solution.py:492
  127.8 25.5 %copy-start.7 = (bf16[256,256]{1,0:T(8,128)(2,1)S(1)}, bf16[256,256]{1,0:T(8,128)(2,1)}, u32[]{:S(2)}) copy-start(bf16[256,256]{1,0:T(8,128)(2,1)} %constant.48.clone.flip_rows_ref) | copy-start | bytes 393220
  127.8 25.5 %copy-start.10 = (bf16[128,128]{1,0:T(8,128)(2,1)S(1)}, bf16[128,128]{1,0:T(8,128)(2,1)}, u32[]{:S(2)}) copy-start(bf16[128,128]{1,0:T(8,128)(2,1)} %constant.51.clone.head_lanes_ref) | copy-start | bytes 98308
  127.8 25.4 %copy-start.11 = (bf16[128,128]{1,0:T(8,128)(2,1)S(1)}, bf16[128,128]{1,0:T(8,128)(2,1)}, u32[]{:S(2)}) copy-start(bf16[128,128]{1,0:T(8,128)(2,1)} %constant.49.clone.flip_lanes_ref) | copy-start | bytes 98308
  127.9 25.4 %copy-start.13 = (bf16[64,64]{1,0:T(8,128)(2,1)S(1)}, bf16[64,64]{1,0:T(8,128)(2,1)}, u32[]{:S(2)}) copy-start(bf16[64,64]{1,0:T(8,128)(2,1)} %constant.50.clone.head_rows_ref) | copy-start | bytes 24580
  147.1 1.4 copy-start.14
  148.5 4.8 %collective-permute-start = (bf16[64,64,128]{2,1,0:T(8,128)(2,1)S(1)}, bf16[64,64,128]{2,1,0:T(8,128)(2,1)S(1)}, u32[]{:S(2)}, u32[]{:S(2)}) collective-permute-start(bf16[64,64,128]{2,1,0:T(8,128)(2,1)S(1)} %get-tuple-element.20), channel_id=1, source_target_pairs={{0,64},{64,0},{1,65},{65,1},{2,66},{66,2},{3,67},{67,3},{4,68},{68... | collective-permute-start | bytes 3145736 | tf_op jit(solution)/shard_map/ppermute | solution.py:503
  158.2 16.5 %copy-start.6 = (bf16[256,256]{1,0:T(8,128)(2,1)S(1)}, bf16[256,256]{1,0:T(8,128)(2,1)}, u32[]{:S(2)}) copy-start(bf16[256,256]{1,0:T(8,128)(2,1)} %constant.45.clone.m3_ref) | copy-start | bytes 393220
  158.2 16.5 %copy-start.9 = (bf16[128,128]{1,0:T(8,128)(2,1)S(1)}, bf16[128,128]{1,0:T(8,128)(2,1)}, u32[]{:S(2)}) copy-start(bf16[128,128]{1,0:T(8,128)(2,1)} %constant.43.clone.m1_ref.m2_ref) | copy-start | bytes 98308
  161.8 12.8 %collective-permute-start.1 = (bf16[64,64,128]{2,1,0:T(8,128)(2,1)S(1)}, bf16[64,64,128]{2,1,0:T(8,128)(2,1)S(1)}, u32[]{:S(2)}, u32[]{:S(2)}) collective-permute-start(bf16[64,64,128]{2,1,0:T(8,128)(2,1)S(1)} %response.1.own_ref), channel_id=1, source_target_pairs={{0,64},{64,0},{1,65},{65,1},{2,66},{66,2},{3,67},{67,3},{4,68},{68... | collective-permute-start | bytes 3145736 | tf_op jit(solution)/shard_map/ppermute | solution.py:515
  162.3 42.6 %all-to-all-start.2 = ((bf16[64,64,128]{2,1,0:T(8,128)(2,1)}), bf16[64,64,128]{2,1,0:T(8,128)(2,1)}, u32[]{:S(2)}, u32[]{:S(2)}) async-start(bf16[64,64,128]{2,1,0:T(8,128)(2,1)} %terms.1), calls=%async_computation.2 | async-start | bytes 2097152 | tf_op jit(solution)/shard_map/all_to_all | solution.py:507
  174.7 1.6 copy-start.15
  197.5 18.2 %copy-start.16 = (f32[128]{0:T(128)S(1)}, f32[128]{0:T(128)}, u32[]{:S(2)}) copy-start(f32[128]{0:T(128)} %param.20) | copy-start | bytes 1540
  197.5 18.3 %copy-start.1 = (bf16[128,256]{1,0:T(8,128)(2,1)S(1)}, bf16[128,256]{1,0:T(8,128)(2,1)}, u32[]{:S(2)}) copy-start(bf16[128,256]{1,0:T(8,128)(2,1)} %wp_ref.5) | copy-start | bytes 196612
  197.5 18.3 %copy-start.3 = (bf16[128,128]{1,0:T(8,128)(2,1)S(1)}, bf16[128,128]{1,0:T(8,128)(2,1)}, u32[]{:S(2)}) copy-start(bf16[128,128]{1,0:T(8,128)(2,1)} %wo_ref.3) | copy-start | bytes 98308
  204.9 100.0 %all-to-all-start.3 = ((bf16[128,128,128]{2,1,0:T(8,128)(2,1)}), bf16[128,128,128]{2,1,0:T(8,128)(2,1)}, u32[]{:S(2)}, u32[]{:S(2)}) async-start(bf16[128,128,128]{2,1,0:T(8,128)(2,1)} %inverse.1), calls=%async_computation.3 | async-start | bytes 8388608 | tf_op jit(solution)/shard_map/all_to_all | solution.py:520
  214.1 10.9 %collective-permute-start.2 = (bf16[32,64,128]{2,1,0:T(8,128)(2,1)S(1)}, bf16[32,64,128]{2,1,0:T(8,128)(2,1)S(1)}, u32[]{:S(2)}, u32[]{:S(2)}) collective-permute-start(bf16[32,64,128]{2,1,0:T(8,128)(2,1)S(1)} %get-tuple-element.28), channel_id=1, source_target_pairs={{0,64},{64,0},{1,65},{65,1},{2,66},{66,2},{3,67},{67,3},{4,68},{68... | collective-permute-start | bytes 1572872 | tf_op jit(solution)/shard_map/ppermute | solution.py:527

commit v3 on v2

v3 whole, which is shorter than its diff:
```python
import functools
import math

import jax
import jax.numpy as jnp
import numpy as np
from jax import lax
from jax.experimental import pallas as pl
from jax.experimental.pallas import tpu as pltpu
from jax.sharding import Mesh, PartitionSpec as P


BF = jnp.bfloat16
F32 = jnp.float32
F2 = 64
F3 = 128
LANES = 128


def dft_blocks(length, direction):
    ids = np.arange(length)
    angles = (ids[:, None] * ids[None, :] % length).astype(np.float32) * np.float32(
        2.0 * math.pi / length
    )
    scale = np.float32(1.0 / math.sqrt(length))
    real = np.cos(angles) * scale
    imag = direction * np.sin(angles) * scale
    return np.block([[real, -imag], [imag, real]]).astype(np.float32)


def turns(ids, modulus):
    angles = (ids % modulus).astype(np.float64) * (2.0 * math.pi / modulus)
    return np.stack([np.cos(angles), np.sin(angles)]).astype(np.float32)


def flip_matrix(size, shift):
    row = lax.broadcasted_iota(jnp.int32, (size, size), 0)
    column = lax.broadcasted_iota(jnp.int32, (size, size), 1)
    total = row + column
    hit = total == size - shift
    if not shift:
        hit = jnp.logical_or(hit, total == 0)
    return jnp.where(hit, 1.0, 0.0).astype(BF)


def vmem_specs(count):
    return [pl.BlockSpec(memory_space=pltpu.VMEM)] * count


SMEM_SPEC = pl.BlockSpec(memory_space=pltpu.SMEM)


def call(body, out_shape, scratch, *args, smem=0, micros=20):
    multi = isinstance(out_shape, (tuple, list))
    return pl.pallas_call(
        body,
        out_shape=out_shape,
        in_specs=[SMEM_SPEC] * smem + vmem_specs(len(args) - smem),
        out_specs=vmem_specs(len(out_shape)) if multi else vmem_specs(1)[0],
        scratch_shapes=scratch,
        compiler_params=pltpu.CompilerParams(vmem_limit_bytes=48 << 20),
        cost_estimate=cost(micros),
    )(*args)


def cost(micros):
    return pl.CostEstimate(
        flops=micros * 10**9, transcendentals=0, bytes_accessed=micros * 3 * 10**6
    )


def dot(a, b):
    return jnp.dot(a, b, preferred_element_type=F32)


def loop(count, body, unroll=1):
    def step(i, carry):
        body(i)
        return carry

    lax.fori_loop(0, count, step, 0, unroll=unroll)


def loop_carry(count, body, init, unroll=1):
    return lax.fori_loop(0, count, body, init, unroll=unroll)


def lane_block(ref, i, rows=None):
    window = pl.ds(pl.multiple_of(i * LANES, LANES), LANES)
    return ref[:, window] if rows is None else ref[rows, window]


PAD = 2
TURN = 8
BATCH = 4


def lane_part(x, i):
    return x[:, i * LANES : (i + 1) * LANES]


def row_part(x, i, size):
    return x[i * size : (i + 1) * size]


def spread_body(x_ref, out_ref, rows_ref):
    channels, blocks, _ = out_ref.shape

    def put(i):
        rows_ref[pl.ds(i * (channels + PAD), channels), :] = lane_block(x_ref, i).astype(F32)

    loop(blocks, put, 4)

    def take(c):
        out_ref[c] = rows_ref[pl.ds(c, blocks, stride=channels + PAD), :].astype(BF)

    loop(channels, take, 4)


def unpack_rows(x_ref, rows_ref, offset=0, blocks=None):
    items = x_ref.shape[0]
    blocks = blocks or x_ref.shape[1]

    def put(c):
        block = x_ref[c, offset : offset + blocks, :]
        rows_ref[pl.ds(c * (blocks + PAD), blocks), :] = block.astype(F32)

    loop(items, put, 4)


def take_turn(rows_ref, out_ref):
    channels = out_ref.shape[0]

    def take(c):
        out_ref[c] = rows_ref[pl.ds(c, TURN, stride=channels + PAD), :].astype(BF)

    loop(channels, take, 8)


def put_pair(rows_ref, pair, x):
    channels = x.shape[0]
    pitch = channels + PAD
    for side in range(2):
        at = (2 * pair + side) * pitch
        rows_ref[at : at + channels, :] = lane_part(x, side)


def pair_window(pair):
    return slice(2 * pair * LANES, (2 * pair + 2) * LANES)


def values_body(wv_ref, tok_ref, out_ref, rows_ref):
    for p in range(TURN // 2):
        put_pair(rows_ref, p, dot(wv_ref[...], tok_ref[:, pair_window(p)]))
    take_turn(rows_ref, out_ref)


def grads_body(wg_ref, wo_ref, tok_ref, cot_ref, out_ref, rows_ref):
    for p in range(TURN // 2):
        gates = dot(wg_ref[...], tok_ref[:, pair_window(p)])
        put_pair(rows_ref, p, dot(wo_ref[...], cot_ref[:, pair_window(p)]) * gates)
    take_turn(rows_ref, out_ref)


def rotate(re, im, cos_part, sin_part):
    return re * cos_part - im * sin_part, re * sin_part + im * cos_part


def first_stage(rows_ref, m1_ref, tw_ref, mid_ref):
    count = m1_ref.shape[0]
    half = count // 2
    mid = F2 + PAD

    def step(j, turn):
        cos_part, sin_part = turn
        x = jnp.concatenate(
            [rows_ref[pl.ds(2 * j + side, count, stride=mid), :] for side in range(2)], axis=1
        )
        y = dot(m1_ref[...], x.astype(BF))
        re, im = rotate(y[:half], y[half:], cos_part, -sin_part)
        for side in range(2):
            mid_ref[pl.ds(2 * j + side, half, stride=2 * mid), :] = lane_part(re, side)
            mid_ref[pl.ds(mid + 2 * j + side, half, stride=2 * mid), :] = lane_part(im, side)
        return rotate(cos_part, sin_part, tw_ref[2], tw_ref[3])

    loop_carry(F2 // 2, step, (tw_ref[0], tw_ref[1]), 2)


def last_stage(rows_ref, m1_ref, tw_ref, mid_ref):
    count = m1_ref.shape[0]
    half = count // 2
    mid = F2 + PAD

    def step(j, turn):
        cos_part, sin_part = turn
        parts = []
        for part in range(2):
            sides = [
                mid_ref[pl.ds(part * mid + 2 * j + side, half, stride=2 * mid), :]
                for side in range(2)
            ]
            parts.append(jnp.concatenate(sides, axis=1))
        re, im = rotate(parts[0], parts[1], cos_part, sin_part)
        y = dot(m1_ref[...], jnp.concatenate([re, im], axis=0).astype(BF))
        for side in range(2):
            rows_ref[pl.ds(2 * j + side, count, stride=mid), :] = lane_part(y, side)
        return rotate(cos_part, sin_part, tw_ref[2], tw_ref[3])

    loop_carry(F2 // 2, step, (tw_ref[0], tw_ref[1]), 2)


def part_rows(k1, part):
    return pl.ds((2 * k1 + part) * (F2 + PAD), F2)


def to_spectrum(mid_ref, first, m2_ref, m3_ref, tw2_ref):
    stacked = []
    for p in range(BATCH // 2):
        pair = [
            jnp.concatenate([mid_ref[part_rows(k1, 0), :], mid_ref[part_rows(k1, 1), :]], axis=0)
            for k1 in (first + 2 * p, first + 2 * p + 1)
        ]
        y = dot(m2_ref[...], jnp.concatenate(pair, axis=1).astype(BF))
        re, im = rotate(y[:F2], y[F2:], tw2_ref[0], -tw2_ref[1])
        for side in range(2):
            stacked.append(
                jnp.concatenate([lane_part(re, side), lane_part(im, side)], axis=1).astype(BF)
            )
    return dot(jnp.concatenate(stacked, axis=0), m3_ref[...]).astype(BF)


def from_spectrum(mid_ref, first, blocks, m2_ref, m3_ref, tw2_ref):
    stacked = [jnp.concatenate(block, axis=1).astype(BF) for block in blocks]
    y = dot(jnp.concatenate(stacked, axis=0), m3_ref[...])
    for p in range(BATCH // 2):
        sides = [row_part(y, 2 * p + side, F2) for side in range(2)]
        re, im = rotate(
            jnp.concatenate([lane_part(s, 0) for s in sides], axis=1),
            jnp.concatenate([lane_part(s, 1) for s in sides], axis=1),
            tw2_ref[0],
            tw2_ref[1],
        )
        z = dot(m2_ref[...], jnp.concatenate([re, im], axis=0).astype(BF))
        for side in range(2):
            k1 = first + 2 * p + side
            mid_ref[part_rows(k1, 0), :] = lane_part(z[:F2], side)
            mid_ref[part_rows(k1, 1), :] = lane_part(z[F2:], side)


def split(spec):
    spec = spec.astype(F32)
    return spec[:, :F3], spec[:, F3:]


def kernel_parts(core_ref, own_ref, other_ref, k1):
    own, other = own_ref[k1].astype(F32), other_ref[k1].astype(F32)
    on_core_zero = core_ref[0] == 0
    return jnp.where(on_core_zero, own, other), jnp.where(on_core_zero, other, own)


def pack_rows(rows_ref, out_ref):
    items, blocks, _ = out_ref.shape

    def put(c):
        out_ref[c] = rows_ref[pl.ds(c * (blocks + PAD), blocks), :].astype(BF)

    loop(items, put, 4)


def values_transform_body(
    core_ref, z_ref, own_ref, other_ref, m1_ref, m2_ref, m3_ref, n1_ref, n2_ref, n3_ref,
    tw_ref, tw2_ref, out_ref, spec_ref, rows_ref, mid_ref,
):
    count = spec_ref.shape[0]
    unpack_rows(z_ref, rows_ref)
    first_stage(rows_ref, m1_ref, tw_ref, mid_ref)

    def spectrum(b):
        spec = to_spectrum(mid_ref, b * BATCH, m2_ref, m3_ref, tw2_ref)
        for t in range(BATCH):
            spec_ref[b * BATCH + t] = row_part(spec, t, F2)

    loop(count // BATCH, spectrum)

    def product(b):
        blocks = []
        for t in range(BATCH):
            k1 = b * BATCH + t
            kern_re, kern_im = kernel_parts(core_ref, own_ref, other_ref, k1)
            blocks.append(rotate(*split(spec_ref[k1]), kern_re, kern_im))
        from_spectrum(mid_ref, b * BATCH, blocks, n2_ref, n3_ref, tw2_ref)

    loop(count // BATCH, product)
    last_stage(rows_ref, n1_ref, tw_ref, mid_ref)
    pack_rows(rows_ref, out_ref)


def grads_transform_body(
    core_ref, z_ref, own_ref, other_ref, values_ref, m1_ref, m2_ref, m3_ref, n1_ref, n2_ref,
    n3_ref, tw_ref, tw2_ref, out_ref, keep_ref, send_ref, rows_ref, mid_ref, spec_ref,
):
    count = values_ref.shape[0]
    on_core_zero = core_ref[0] == 0
    unpack_rows(z_ref, rows_ref)
    first_stage(rows_ref, m1_ref, tw_ref, mid_ref)

    def spectrum(b):
        spec = to_spectrum(mid_ref, b * BATCH, m2_ref, m3_ref, tw2_ref)
        for t in range(BATCH):
            k1 = b * BATCH + t
            grad = row_part(spec, t, F2)
            spec_ref[k1] = grad
            value_re, value_im = split(values_ref[k1])
            re, im = rotate(*split(grad), value_re, -value_im)
            keep_ref[k1] = jnp.where(on_core_zero, re, im).astype(BF)
            send_ref[k1] = jnp.where(on_core_zero, im, re).astype(BF)

    loop(count // BATCH, spectrum)

    def product(b):
        blocks = []
        for t in range(BATCH):
            k1 = b * BATCH + t
            kern_re, kern_im = kernel_parts(core_ref, own_ref, other_ref, k1)
            blocks.append(rotate(*split(spec_ref[k1]), kern_re, -kern_im))
        from_spectrum(mid_ref, b * BATCH, blocks, n2_ref, n3_ref, tw2_ref)

    loop(count // BATCH, product)
    last_stage(rows_ref, n1_ref, tw_ref, mid_ref)
    pack_rows(rows_ref, out_ref)


def hermitian(ref, sign, flip_rows_ref, flip_lanes_ref, store):
    count = ref.shape[0]
    flip_rows_ref[...] = flip_matrix(BATCH * F2, 1)
    flip_lanes_ref[...] = flip_matrix(F3, 1)
    head = ref[0]
    head_rows = flip_matrix(F2, 0)
    turned = dot(head_rows, dot(head, flip_lanes_ref[...]).astype(BF))
    first = dot(head_rows, dot(head, flip_matrix(F3, 0)).astype(BF))
    row = lax.broadcasted_iota(jnp.int32, turned.shape, 0)
    store(0, 0.5 * (head.astype(F32) + sign * jnp.where(row == 0, first, turned)))

    def batch(b, keep=BATCH):
        low = count - BATCH - b * BATCH
        rows = jnp.concatenate([ref[low + t] for t in range(BATCH)], axis=0)
        turned = dot(flip_rows_ref[...], dot(rows, flip_lanes_ref[...]).astype(BF))
        for t in range(keep):
            k1 = b * BATCH + 1 + t
            store(k1, 0.5 * (ref[k1].astype(F32) + sign * row_part(turned, t, F2)))

    loop(count // BATCH - 1, batch, 3)
    batch(count // BATCH - 1, BATCH - 1)


def terms_body(
    core_ref, keep_ref, recv_ref, out_ref, sum_ref, flip_rows_ref, flip_lanes_ref
):
    sign = jnp.where(core_ref[0] == 0, 1.0, -1.0)

    def add(k1):
        sum_ref[k1] = (keep_ref[k1].astype(F32) + recv_ref[k1].astype(F32)).astype(BF)

    loop(keep_ref.shape[0], add, 4)

    def store(k1, block):
        out_ref[k1] = block.astype(BF)

    hermitian(sum_ref, sign, flip_rows_ref, flip_lanes_ref, store)


def slot(place_ref, index, size, axes=3):
    at = 0
    for axis in range(3 - axes, 3):
        digit = lax.rem(lax.div(index, size ** (2 - axis)), size)
        at = at * size + lax.rem(place_ref[1 + axis] - digit + size, size)
    return at


def response_body(
    size, place_ref, got_ref, out_ref, own_ref, flip_rows_ref, flip_lanes_ref
):
    sign = jnp.where(place_ref[0] == 0, 1.0, -1.0)

    def order(k1):
        own_ref[k1] = got_ref[slot(place_ref, k1, size)]

    loop(own_ref.shape[0], order, 4)

    def store(k1, block):
        out_ref[k1] = block.astype(BF)

    hermitian(own_ref, sign, flip_rows_ref, flip_lanes_ref, store)


def gather_pair(rows_ref, pair, channels):
    return jnp.concatenate(
        [rows_ref[pl.ds(2 * pair + side, channels, stride=TURN + PAD), :] for side in range(2)],
        axis=1,
    )


def gates_body(
    wv_ref, wg_ref, wo_ref, wpg_ref, skip_ref, tok_ref, cot_ref, conv_ref,
    part_ref, own_ref, rows_ref,
):
    channels = conv_ref.shape[0]
    unpack_rows(conv_ref, rows_ref)
    for p in range(TURN // 2):
        window = pair_window(p)
        tok = tok_ref[:, window]
        values = dot(wv_ref[...], tok).astype(BF).astype(F32)
        hidden = dot(wo_ref[...], cot_ref[:, window])
        own = (hidden * dot(wg_ref[...], tok)).astype(BF).astype(F32)
        mixed = gather_pair(rows_ref, p, channels) + skip_ref[...] * values
        part_ref[:, window] = dot(wpg_ref[...], (hidden * mixed).astype(BF))
        own_ref[:, window] = skip_ref[...] * own


def final_body(wpv_ref, part_ref, own_ref, back_ref, out_ref, rows_ref):
    channels = back_ref.shape[0]
    unpack_rows(back_ref, rows_ref)
    for p in range(TURN // 2):
        window = pair_window(p)
        grad = gather_pair(rows_ref, p, channels) + own_ref[:, window]
        out_ref[:, window] = (part_ref[:, window] + dot(wpv_ref[...], grad.astype(BF))).astype(BF)


def chunked(body, micros, small, chunks, outs, messages=(), scratch=()):
    steps = chunks[0].shape[1] // (TURN * LANES)
    whole = [pl.BlockSpec(a.shape, lambda i: (0, 0)) for a in small]
    wide = lambda a: pl.BlockSpec((a.shape[0], TURN * LANES), lambda i: (0, i))
    turn = lambda a: pl.BlockSpec((a.shape[0], TURN, LANES), lambda i: (0, i, 0))
    spec = lambda a: wide(a) if len(a.shape) == 2 else turn(a)
    return pl.pallas_call(
        body,
        grid=(steps,),
        out_shape=outs,
        in_specs=whole + [spec(a) for a in chunks + tuple(messages)],
        out_specs=[spec(a) for a in outs],
        scratch_shapes=list(scratch),
        compiler_params=pltpu.CompilerParams(vmem_limit_bytes=32 << 20),
        cost_estimate=cost(micros),
    )(*small, *(in_hbm(a) for a in chunks + tuple(messages)))


def in_hbm(a):
    return pltpu.with_memory_space_constraint(a, pltpu.HBM)


def kernel_grad_body(size, place_ref, keep_ref, recv_ref, out_ref, rows_ref):
    channels, blocks, _ = keep_ref.shape
    core = place_ref[0]
    for ref, part in ((keep_ref, core), (recv_ref, 1 - core)):

        def put(c, ref=ref):
            at = lax.div(c, size * size) * size * size + slot(place_ref, c, size, 2)
            rows_ref[pl.ds(c * (blocks + PAD), blocks), :] = ref[at].astype(F32)

        loop(channels, put, 4)

        def step(i, part=part):
            window = pl.ds(pl.multiple_of(i * LANES, LANES), LANES)
            rows = rows_ref[pl.ds(i, channels, stride=blocks + PAD), :]
            out_ref[part, :, window] = rows.astype(BF)

        loop(blocks, step, 4)


SWAP = [(0, 1), (1, 0)]
RING = ("zh", "y", "x")
SEQ = RING
GROUP = ("zl",) + RING


def ring_step(y, axis, size):
    me = lax.axis_index(RING[axis])
    parts = []
    for step in range(size):
        slab = lax.dynamic_slice_in_dim(y, lax.rem(me + step, size), 1, axis)
        ring = [(i, (i + step) % size) for i in range(size)]
        parts.append(lax.ppermute(slab, RING[axis], ring) if step else slab)
    return jnp.concatenate(parts, axis=axis)


def cube(x, size):
    return x.reshape((size, size, size) + x.shape[1:])


def exchange(x):
    return lax.all_to_all(x, GROUP, split_axis=0, concat_axis=0, tiled=True)


def per_device(tokens, kernel, skip, w_proj, w_out, cotangent):
    size = lax.axis_size("x")
    first_len = size**3
    core = lax.axis_index("core")
    z_low = lax.axis_index("zl")
    channels, positions = tokens.shape[1:]
    whole = first_len * positions
    place = jnp.stack([core] + [lax.axis_index(name) for name in RING]).astype(jnp.int32)
    tok = tokens.reshape(channels, positions)
    cot = cotangent.reshape(channels, positions)
    blocks = positions // LANES
    shaped = jax.ShapeDtypeStruct

    bf = functools.partial(jnp.asarray, dtype=BF)
    skip_full = jnp.broadcast_to(skip[:, None], (channels, 2 * LANES))
    m1, n1 = bf(dft_blocks(first_len, -1.0)), bf(dft_blocks(first_len, 1.0))
    m2, n2 = bf(dft_blocks(F2, -1.0)), bf(dft_blocks(F2, 1.0))
    m3, n3 = bf(dft_blocks(F3, -1.0).T), bf(dft_blocks(F3, 1.0).T)
    freq = np.arange(first_len)[:, None]
    pair = np.arange(2 * F3)[None, :]
    tw = jnp.asarray(
        np.concatenate(
            [turns(freq * pair, whole), turns(freq * np.full_like(pair, 2 * F3), whole)]
        )
    )
    tw2 = turns(np.arange(F2)[:, None] * np.arange(F3)[None, :], F2 * F3)
    tw2 = jnp.asarray(np.concatenate([tw2, tw2], axis=2))
    share = first_len
    half = share // 2
    mid_rows = pltpu.VMEM((2 * first_len * (F2 + PAD), F3), F32)
    turn_rows = pltpu.VMEM((TURN * (channels + PAD), LANES), F32)
    turn_items = pltpu.VMEM((channels * (TURN + PAD), LANES), F32)
    part = shaped((share, blocks, LANES), BF)
    flip_scratch = [
        pltpu.VMEM((first_len, F2, F3), BF),
        pltpu.VMEM((BATCH * F2, BATCH * F2), BF),
        pltpu.VMEM((F3, F3), BF),
    ]
    message = pltpu.HBM((channels, blocks, LANES), BF)
    spectrum = shaped((first_len, F2, 2 * F3), BF)
    wv, wg = w_proj[:, :channels].T, w_proj[:, channels:].T
    wpv, wpg = w_proj[:, :channels], w_proj[:, channels:]

    (values,) = chunked(values_body, 5, (wv,), (tok,), (message,), (), (turn_rows,))
    values = exchange(values)

    chosen = lax.dynamic_slice(kernel, (core, z_low * share, 0), (1, share, positions))[0]
    response = call(
        spread_body, part, [pltpu.VMEM((blocks * (share + PAD), LANES), F32)],
        chosen, micros=3,
    )
    response = ring_step(cube(response, size), 2, size)
    (grads,) = chunked(grads_body, 6, (wg, w_out), (tok, cot), (message,), (), (turn_rows,))
    grads, response = lax.optimization_barrier((grads, response))
    response = ring_step(ring_step(response, 1, size), 0, size)
    grads, values = lax.optimization_barrier((grads, values))
    grads = exchange(grads)
    response = call(
        functools.partial(response_body, size), part, flip_scratch,
        place, response.reshape(part.shape),
        smem=1, micros=4,
    )
    other = lax.ppermute(response, "core", SWAP)
    tables = (m1, m2, m3, n1, n2, n3, tw, tw2)
    conv, spec = call(
        values_transform_body, (message, spectrum), [mid_rows, mid_rows],
        place, values, response, other, *tables,
        smem=1, micros=20,
    )
    conv, grads = lax.optimization_barrier((conv, grads))
    conv = exchange(conv)
    back, keep, send = call(
        grads_transform_body, (message, part, part),
        [mid_rows, mid_rows, pltpu.VMEM((first_len, F2, 2 * F3), BF)],
        place, grads, response, other, spec, *tables,
        smem=1, micros=22,
    )
    terms = call(
        terms_body, part, flip_scratch,
        place, keep, lax.ppermute(send, "core", SWAP),
        smem=1, micros=5,
    )
    terms = ring_step(cube(terms, size), 0, size)
    back, conv = lax.optimization_barrier((back, conv))
    back = exchange(back)
    gates, own = chunked(
        gates_body, 10, (wv, wg, w_out, wpg, skip_full), (tok, cot),
        (pltpu.HBM((channels, positions), F32),) * 2, (conv,), (turn_items,),
    )
    terms = ring_step(ring_step(terms, 1, size), 2, size)
    me = lax.axis_index(RING[0])

    def halves(of_core):
        slabs = [
            lax.dynamic_slice_in_dim(terms, lax.rem(me - of_core * (size // 2) - i + size, size), 1, 0)
            for i in range(size // 2)
        ]
        return jnp.concatenate(slabs, axis=0).reshape(half, blocks, LANES)

    kernel_grad = call(
        functools.partial(kernel_grad_body, size),
        shaped((2, half, positions), BF),
        [pltpu.VMEM((half * (blocks + PAD), LANES), F32)],
        place, halves(core), lax.ppermute(halves(1 - core), "core", SWAP),
        smem=1, micros=3,
    )
    (input_grad,) = chunked(
        final_body, 6, (wpv,), (gates, own),
        (pltpu.HBM((channels, positions), BF),), (back,), (turn_items,),
    )
    return input_grad.reshape(1, channels, positions), kernel_grad


def solution(mesh):
    sequences, groups = mesh.devices.shape
    size = round(groups ** (1 / 3))
    fine = Mesh(
        mesh.devices.reshape(2, sequences // 2, size, size, size), ("zl", "core") + RING
    )
    dp = ("zl", "core")
    signal = P(dp, None, SEQ)
    return jax.shard_map(
        per_device,
        mesh=fine,
        in_specs=(signal, P(None, None, SEQ), P(), P(), P(), signal),
        out_specs=(signal, P(None, dp, SEQ)),
        check_vma=False,
    )
```

time: 321 us -> 389 us (1.21)
  starting transfers between devices: 50.4 us -> 82.5 us
  waiting for transfers between devices: 177 us -> 198 us
  Pallas kernels: 79.7 us -> 92.1 us
    ppermute x2 -> x20, waiting for transfers between devices: 0.01 us -> 162 us  [the longest x18 158 us: ring_step(): parts.append(lax.ppermute(slab, RING[axis], ring) if step else slab)]
    all_to_all x4, waiting for transfers between devices: 175 us -> 35.4 us  [exchange(): return lax.all_to_all(x, GROUP, split_axis=0, concat_axis=0, tiled=True)]
    ppermute x2 -> x20, starting transfers between devices: 2.09 us -> 33.9 us  [the longest x18 30.7 us: ring_step(): parts.append(lax.ppermute(slab, RING[axis], ring) if step else slab)]
    pallas_call x3 -> x4, Pallas kernels: 27.6 us -> 34.6 us  [chunked(): pl.pallas_call(body, grid=(steps,), out_shape=outs, in_specs=whole + [spe...]
    pallas_call x6, Pallas kernels: 52.1 us -> 57.5 us  [call(): pl.pallas_call(body, out_shape=out_shape, in_specs=[SMEM_SPEC] * smem + v...]
  transfers between devices with their start and end apart: 7 -> 25, of which waited for: 4 -> 16; matrix products, arithmetic and copies ran while one was open for 1% -> 1% of each run, Pallas kernels for 18% -> 20%
where the time goes in v3:
time: 389 us; the launch traced here: 386 us
  waiting for transfers between devices  198 us (51%)
  Pallas kernels  92.1 us (24%)
  starting transfers between devices  82.5 us (21%)
  local copies, waits for them, and re-layouts  9.52 us (2%)
    ppermute x18, waiting for transfers between devices, ring_step(): parts.append(lax.ppermute(slab, RING[axis], ring) if step else slab)  158 us
    pallas_call x6, Pallas kernels, call(): pl.pallas_call(body, out_shape=out_shape, in_specs=[SMEM_SPEC] * smem + v...  57.5 us
    all_to_all x4, starting transfers between devices, exchange(): return lax.all_to_all(x, GROUP, split_axis=0, concat_axis=0, tiled=True)  47.6 us
    all_to_all x4, waiting for transfers between devices, exchange(): return lax.all_to_all(x, GROUP, split_axis=0, concat_axis=0, tiled=True)  35.4 us
    pallas_call x4, Pallas kernels, chunked(): pl.pallas_call(body, grid=(steps,), out_shape=outs, in_specs=whole + [spe...  34.6 us
    ppermute x18, starting transfers between devices, ring_step(): parts.append(lax.ppermute(slab, RING[axis], ring) if step else slab)  30.7 us
  transfers between devices with their start and end apart: 25, of which 16 were waited for; matrix products, arithmetic and copies ran while one was open for 1% of the time, Pallas kernels for 20%

profile of v3, /device:TPU:35, one launch (start us, length us, event | category | flops | bytes accessed | tf_op | source)
XLA Modules:
  0.0 385.9 jit_solution(10105885446213311716)
XLA Ops:
  1.5 6.8 %shard_map.151 = bf16[128,64,128]{2,1,0:T(8,128)(2,1)} custom-call(bf16[128,128]{1,0:T(8,128)(2,1)S(1)} %copy.18.wv_ref, bf16[128,8192]{1,0:T(8,128)(2,1)} %bitcast.23), custom_call_target="tpu_custom_call" | custom-call | flops 5000000000 | bytes 15000000 | tf_op jit(solution)/shard_map/pallas_call | solution.py:435
  8.3 14.7 %all-to-all-start = ((bf16[128,64,128]{2,1,0:T(8,128)(2,1)}), bf16[128,64,128]{2,1,0:T(8,128)(2,1)S(1)}, u32[]{:S(2)}, u32[]{:S(2)}) async-start(bf16[128,64,128]{2,1,0:T(8,128)(2,1)} %shard_map.151), calls=%async_computation | async-start | bytes 4194304 | tf_op jit(solution)/shard_map/all_to_all | solution.py:491
  29.1 7.6 %shard_map.149 = bf16[128,64,128]{2,1,0:T(8,128)(2,1)} custom-call(bf16[128,128]{1,0:T(8,128)(2,1)S(1)} %copy.19.wg_ref, bf16[128,128]{1,0:T(8,128)(2,1)S(1)} %copy-done, bf16[128,8192]{1,0:T(8,128)(2,1)} %bitcast.24, bf16[128,8192]{1,0:T(8,128)(2,1)} %bitcast.26), custom_call_target="tpu_custom_call" | custom-call | flops 6000000000 | bytes 18000000 | tf_op jit(solution)/shard_map/pallas_call | solution.py:435
  38.2 10.0 %collective-permute-done.1 = bf16[4,4,1,64,128]{4,3,2,1,0:T(8,128)(2,1)} collective-permute-done((bf16[4,4,1,64,128]{4,3,2,1,0:T(8,128)(2,1)S(1)}, bf16[4,4,1,64,128]{4,3,2,1,0:T(8,128)(2,1)}, u32[]{:S(2)}, u32[]{:S(2)}) %collective-permute-start.1) | collective-permute-done | bytes 262176 | tf_op jit(solution)/shard_map/ppermute | solution.py:482
  49.5 3.7 collective-permute-start.5
  55.5 15.2 %all-to-all-done.z_ref = bf16[128,64,128]{2,1,0:T(8,128)(2,1)S(1)} async-done(((bf16[128,64,128]{2,1,0:T(8,128)(2,1)}), bf16[128,64,128]{2,1,0:T(8,128)(2,1)S(1)}, u32[]{:S(2)}, u32[]{:S(2)}) %all-to-all-start) | async-done | bytes 2097184 | tf_op jit(solution)/shard_map/all_to_all | solution.py:491
  72.0 11.9 %all-to-all-start.1 = ((bf16[128,64,128]{2,1,0:T(8,128)(2,1)}), bf16[128,64,128]{2,1,0:T(8,128)(2,1)}, u32[]{:S(2)}, u32[]{:S(2)}) async-start(bf16[128,64,128]{2,1,0:T(8,128)(2,1)} %shard_map.149), calls=%async_computation.1 | async-start | bytes 4194304 | tf_op jit(solution)/shard_map/all_to_all | solution.py:491
  92.3 47.0 %collective-permute-done.8 = bf16[1,4,4,64,128]{4,3,2,1,0:T(8,128)(2,1)S(1)} collective-permute-done((bf16[1,4,4,64,128]{4,3,2,1,0:T(8,128)(2,1)S(1)}, bf16[1,4,4,64,128]{4,3,2,1,0:T(8,128)(2,1)S(1)}, u32[]{:S(2)}, u32[]{:S(2)}) %collective-permute-start.8) | collective-permute-done | bytes 262176 | tf_op jit(solution)/shard_map/ppermute | solution.py:482
  139.2 15.5 %collective-permute-done.7 = bf16[1,4,4,64,128]{4,3,2,1,0:T(8,128)(2,1)S(1)} collective-permute-done((bf16[1,4,4,64,128]{4,3,2,1,0:T(8,128)(2,1)S(1)}, bf16[1,4,4,64,128]{4,3,2,1,0:T(8,128)(2,1)S(1)}, u32[]{:S(2)}, u32[]{:S(2)}) %collective-permute-start.7) | collective-permute-done | bytes 262176 | tf_op jit(solution)/shard_map/ppermute | solution.py:482
  155.0 5.2 %shard_map.152.own_ref = bf16[64,64,128]{2,1,0:T(8,128)(2,1)S(1)} custom-call(s32[4]{0:T(128)S(1)} %pad_add_fusion.place_ref.core_ref, bf16[64,64,128]{2,1,0:T(8,128)(2,1)S(1)} %bitcast.20), custom_call_target="tpu_custom_call" | custom-call | flops 4000000000 | bytes 12000000 | tf_op jit(solution)/shard_map/pallas_call | solution.py:55
  164.1 21.7 %shard_map.153 = (bf16[128,64,128]{2,1,0:T(8,128)(2,1)}, bf16[64,64,256]{2,1,0:T(8,128)(2,1)S(1)}) custom-call(s32[4]{0:T(128)S(1)} %pad_add_fusion.place_ref.core_ref, bf16[128,64,128]{2,1,0:T(8,128)(2,1)} %copy-done.13, bf16[64,64,128]{2,1,0:T(8,128)(2,1)S(1)} %shard_map.152.own_ref, bf16[64,64,128]{2,1,0:T(8,128)(2,1)S(1)} %collective-permute-done.9.other_ref, ...), custom_call_target="tpu_custom_call" | custom-call | flops 20000000000 | bytes 60000000 | tf_op jit(solution)/shard_map/pallas_call | solution.py:55
  187.1 9.5 %all-to-all-start.2 = ((bf16[128,64,128]{2,1,0:T(8,128)(2,1)}), bf16[128,64,128]{2,1,0:T(8,128)(2,1)}, u32[]{:S(2)}, u32[]{:S(2)}) async-start(bf16[128,64,128]{2,1,0:T(8,128)(2,1)} %get-tuple-element.25), calls=%async_computation.2 | async-start | bytes 4194304 | tf_op jit(solution)/shard_map/all_to_all | solution.py:491
  199.4 22.9 %shard_map.154 = (bf16[128,64,128]{2,1,0:T(8,128)(2,1)}, bf16[64,64,128]{2,1,0:T(8,128)(2,1)S(1)}, bf16[64,64,128]{2,1,0:T(8,128)(2,1)S(1)}) custom-call(s32[4]{0:T(128)S(1)} %pad_add_fusion.place_ref.core_ref, bf16[128,64,128]{2,1,0:T(8,128)(2,1)} %all-to-all-done.1.z_ref, bf16[64,64,128]{2,1,0:T(8,128)(2,1)S(1)} %shard_map.152.own_ref, ...), custom_call_target="tpu_custom_call" | custom-call | flops 22000001024 | bytes 66000000 | tf_op jit(solution)/shard_map/pallas_call | solution.py:55
  224.2 20.2 %all-to-all-done.2.conv_ref = bf16[128,64,128]{2,1,0:T(8,128)(2,1)} async-done(((bf16[128,64,128]{2,1,0:T(8,128)(2,1)}), bf16[128,64,128]{2,1,0:T(8,128)(2,1)}, u32[]{:S(2)}, u32[]{:S(2)}) %all-to-all-start.2) | async-done | bytes 2097184 | tf_op jit(solution)/shard_map/all_to_all | solution.py:491
  244.4 11.5 %all-to-all-start.3 = ((bf16[128,64,128]{2,1,0:T(8,128)(2,1)}), bf16[128,64,128]{2,1,0:T(8,128)(2,1)}, u32[]{:S(2)}, u32[]{:S(2)}) async-start(bf16[128,64,128]{2,1,0:T(8,128)(2,1)} %get-tuple-element.29), calls=%async_computation.3 | async-start | bytes 4194304 | tf_op jit(solution)/shard_map/all_to_all | solution.py:491
  255.9 4.5 %shard_map.157 = bf16[64,64,128]{2,1,0:T(8,128)(2,1)S(1)} custom-call(s32[4]{0:T(128)S(1)} %pad_add_fusion.place_ref.core_ref, bf16[64,64,128]{2,1,0:T(8,128)(2,1)S(1)} %copy-done.11, bf16[64,64,128]{2,1,0:T(8,128)(2,1)S(1)} %collective-permute-done.10.recv_ref), custom_call_target="tpu_custom_call" | custom-call | flops 5000000000 | bytes 15000000 | tf_op jit(solution)/shard_map/pallas_call | solution.py:55
  267.4 43.8 %collective-permute-done.13 = bf16[1,4,4,64,128]{4,3,2,1,0:T(8,128)(2,1)S(1)} collective-permute-done((bf16[1,4,4,64,128]{4,3,2,1,0:T(8,128)(2,1)S(1)}, bf16[1,4,4,64,128]{4,3,2,1,0:T(8,128)(2,1)S(1)}, u32[]{:S(2)}, u32[]{:S(2)}) %collective-permute-start.13) | collective-permute-done | bytes 262176 | tf_op jit(solution)/shard_map/ppermute | solution.py:482
  311.2 15.6 %collective-permute-done.12 = bf16[1,4,4,64,128]{4,3,2,1,0:T(8,128)(2,1)S(1)} collective-permute-done((bf16[1,4,4,64,128]{4,3,2,1,0:T(8,128)(2,1)S(1)}, bf16[1,4,4,64,128]{4,3,2,1,0:T(8,128)(2,1)S(1)}, u32[]{:S(2)}, u32[]{:S(2)}) %collective-permute-start.12) | collective-permute-done | bytes 262176 | tf_op jit(solution)/shard_map/ppermute | solution.py:482
  330.1 3.4 collective-permute-done.16
  336.7 7.8 %collective-permute-done.14 = bf16[4,1,4,64,128]{4,3,2,1,0:T(8,128)(2,1)S(1)} collective-permute-done((bf16[4,1,4,64,128]{4,3,2,1,0:T(8,128)(2,1)S(1)}, bf16[4,1,4,64,128]{4,3,2,1,0:T(8,128)(2,1)S(1)}, u32[]{:S(2)}, u32[]{:S(2)}) %collective-permute-start.14) | collective-permute-done | bytes 262176 | tf_op jit(solution)/shard_map/ppermute | solution.py:482
  348.8 3.4 collective-permute-done.19
  352.2 6.4 %collective-permute-done.18 = bf16[4,4,1,64,128]{4,3,2,1,0:T(8,128)(2,1)S(1)} collective-permute-done((bf16[4,4,1,64,128]{4,3,2,1,0:T(8,128)(2,1)S(1)}, bf16[4,4,1,64,128]{4,3,2,1,0:T(8,128)(2,1)S(1)}, u32[]{:S(2)}, u32[]{:S(2)}) %collective-permute-start.18) | collective-permute-done | bytes 262176 | tf_op jit(solution)/shard_map/ppermute | solution.py:482
  365.7 11.5 %shard_map.155 = (f32[128,8192]{1,0:T(8,128)}, f32[128,8192]{1,0:T(8,128)}) custom-call(bf16[128,128]{1,0:T(8,128)(2,1)S(1)} %copy.18.wv_ref, bf16[128,128]{1,0:T(8,128)(2,1)S(1)} %copy.19.wg_ref, bf16[128,128]{1,0:T(8,128)(2,1)S(1)} %copy-done, bf16[128,128]{1,0:T(8,128)(2,1)S(1)} %get-tuple-element.60.wpg_ref, f32[128,256]{1,0:T(8,128)S(1)} %broadcast_in_dim.2.skip_ref, ...), custom_call_target="tpu_custom_call" | custom-call | flops 10000000000 | bytes 30000000 | tf_op jit(solution)/shard_map/pallas_call | solution.py:435
  377.3 8.6 %shard_map.156 = bf16[128,8192]{1,0:T(8,128)(2,1)} custom-call(bf16[128,128]{1,0:T(8,128)(2,1)S(1)} %get-tuple-element.63.wpv_ref, f32[128,8192]{1,0:T(8,128)} %get-tuple-element.27.part_ref, f32[128,8192]{1,0:T(8,128)} %get-tuple-element.28.own_ref, bf16[128,64,128]{2,1,0:T(8,128)(2,1)} %all-to-all-done.3.back_ref), custom_call_target="tpu_custom_call" | custom-call | flops 6000000000 | bytes 18000000 | tf_op jit(solution)/shard_map/pallas_call | solution.py:435
  (87 shorter events, 56.4 us)
Async XLA Ops:
  8.3 62.3 %all-to-all-start = ((bf16[128,64,128]{2,1,0:T(8,128)(2,1)}), bf16[128,64,128]{2,1,0:T(8,128)(2,1)S(1)}, u32[]{:S(2)}, u32[]{:S(2)}) async-start(bf16[128,64,128]{2,1,0:T(8,128)(2,1)} %shard_map.151), calls=%async_computation | async-start | bytes 4194304 | tf_op jit(solution)/shard_map/all_to_all | solution.py:491
  25.1 13.1 %collective-permute-start.2 = (bf16[4,4,1,64,128]{4,3,2,1,0:T(8,128)(2,1)S(1)}, bf16[4,4,1,64,128]{4,3,2,1,0:T(8,128)(2,1)}, u32[]{:S(2)}, u32[]{:S(2)}) collective-permute-start(bf16[4,4,1,64,128]{4,3,2,1,0:T(8,128)(2,1)S(1)} %get-tuple-element.57), channel_id=1, source_target_pairs={{0,3},{1,0},{2,1},{3,2},{4,7},{5,4},{6,5},{7,6},{8,11},{9,8},{10,9... | collective-permute-start | bytes 786440 | tf_op jit(solution)/shard_map/ppermute | solution.py:482
  25.4 22.7 %collective-permute-start.1 = (bf16[4,4,1,64,128]{4,3,2,1,0:T(8,128)(2,1)S(1)}, bf16[4,4,1,64,128]{4,3,2,1,0:T(8,128)(2,1)}, u32[]{:S(2)}, u32[]{:S(2)}) collective-permute-start(bf16[4,4,1,64,128]{4,3,2,1,0:T(8,128)(2,1)S(1)} %get-tuple-element.58), channel_id=1, source_target_pairs={{0,2},{1,3},{2,0},{3,1},{4,6},{5,7},{6,4},{7,5},{8,10},{9,11},{10,... | collective-permute-start | bytes 786440 | tf_op jit(solution)/shard_map/ppermute | solution.py:482
  27.5 20.6 %collective-permute-start = (bf16[4,4,1,64,128]{4,3,2,1,0:T(8,128)(2,1)S(1)}, bf16[4,4,1,64,128]{4,3,2,1,0:T(8,128)(2,1)}, u32[]{:S(2)}, u32[]{:S(2)}) collective-permute-start(bf16[4,4,1,64,128]{4,3,2,1,0:T(8,128)(2,1)S(1)} %get-tuple-element.59), channel_id=1, source_target_pairs={{0,1},{1,2},{2,3},{3,0},{4,5},{5,6},{6,7},{7,4},{8,9},{9,10},{10,1... | collective-permute-start | bytes 786440 | tf_op jit(solution)/shard_map/ppermute | solution.py:482
  49.5 34.4 %collective-permute-start.5 = (bf16[4,1,4,64,128]{4,3,2,1,0:T(8,128)(2,1)S(1)}, bf16[4,1,4,64,128]{4,3,2,1,0:T(8,128)(2,1)}, u32[]{:S(2)}, u32[]{:S(2)}) collective-permute-start(bf16[4,1,4,64,128]{4,3,2,1,0:T(8,128)(2,1)S(1)} %get-tuple-element.53), channel_id=1, source_target_pairs={{0,12},{4,0},{8,4},{12,8},{1,13},{5,1},{9,5},{13,9},{2,14},{6,2},{... | collective-permute-start | bytes 786440 | tf_op jit(solution)/shard_map/ppermute | solution.py:482
  53.2 30.8 %collective-permute-start.4 = (bf16[4,1,4,64,128]{4,3,2,1,0:T(8,128)(2,1)S(1)}, bf16[4,1,4,64,128]{4,3,2,1,0:T(8,128)(2,1)}, u32[]{:S(2)}, u32[]{:S(2)}) collective-permute-start(bf16[4,1,4,64,128]{4,3,2,1,0:T(8,128)(2,1)S(1)} %get-tuple-element.54), channel_id=1, source_target_pairs={{0,8},{4,12},{8,0},{12,4},{1,9},{5,13},{9,1},{13,5},{2,10},{6,14},... | collective-permute-start | bytes 786440 | tf_op jit(solution)/shard_map/ppermute | solution.py:482
  55.5 28.5 %collective-permute-start.3 = (bf16[4,1,4,64,128]{4,3,2,1,0:T(8,128)(2,1)S(1)}, bf16[4,1,4,64,128]{4,3,2,1,0:T(8,128)(2,1)}, u32[]{:S(2)}, u32[]{:S(2)}) collective-permute-start(bf16[4,1,4,64,128]{4,3,2,1,0:T(8,128)(2,1)S(1)} %get-tuple-element.55), channel_id=1, source_target_pairs={{0,4},{4,8},{8,12},{12,0},{1,5},{5,9},{9,13},{13,1},{2,6},{6,10},{... | collective-permute-start | bytes 786440 | tf_op jit(solution)/shard_map/ppermute | solution.py:482
  72.0 115.1 %all-to-all-start.1 = ((bf16[128,64,128]{2,1,0:T(8,128)(2,1)}), bf16[128,64,128]{2,1,0:T(8,128)(2,1)}, u32[]{:S(2)}, u32[]{:S(2)}) async-start(bf16[128,64,128]{2,1,0:T(8,128)(2,1)} %shard_map.149), calls=%async_computation.1 | async-start | bytes 4194304 | tf_op jit(solution)/shard_map/all_to_all | solution.py:491
  85.3 53.9 %collective-permute-start.8 = (bf16[1,4,4,64,128]{4,3,2,1,0:T(8,128)(2,1)S(1)}, bf16[1,4,4,64,128]{4,3,2,1,0:T(8,128)(2,1)S(1)}, u32[]{:S(2)}, u32[]{:S(2)}) collective-permute-start(bf16[1,4,4,64,128]{4,3,2,1,0:T(8,128)(2,1)S(1)} %get-tuple-element.49), channel_id=1, source_target_pairs={{0,48},{16,0},{32,16},{48,32},{1,49},{17,1},{33,17},{49,33},{2,50}... | collective-permute-start | bytes 786440 | tf_op jit(solution)/shard_map/ppermute | solution.py:482
  88.1 66.6 %collective-permute-start.7 = (bf16[1,4,4,64,128]{4,3,2,1,0:T(8,128)(2,1)S(1)}, bf16[1,4,4,64,128]{4,3,2,1,0:T(8,128)(2,1)S(1)}, u32[]{:S(2)}, u32[]{:S(2)}) collective-permute-start(bf16[1,4,4,64,128]{4,3,2,1,0:T(8,128)(2,1)S(1)} %get-tuple-element.50), channel_id=1, source_target_pairs={{0,32},{16,48},{32,0},{48,16},{1,33},{17,49},{33,1},{49,17},{2,34}... | collective-permute-start | bytes 786440 | tf_op jit(solution)/shard_map/ppermute | solution.py:482
  90.9 63.9 %collective-permute-start.6 = (bf16[1,4,4,64,128]{4,3,2,1,0:T(8,128)(2,1)S(1)}, bf16[1,4,4,64,128]{4,3,2,1,0:T(8,128)(2,1)S(1)}, u32[]{:S(2)}, u32[]{:S(2)}) collective-permute-start(bf16[1,4,4,64,128]{4,3,2,1,0:T(8,128)(2,1)S(1)} %get-tuple-element.51), channel_id=1, source_target_pairs={{0,16},{16,32},{32,48},{48,0},{1,17},{17,33},{33,49},{49,1},{2,18}... | collective-permute-start | bytes 786440 | tf_op jit(solution)/shard_map/ppermute | solution.py:482
  160.2 3.9 %collective-permute-start.9 = (bf16[64,64,128]{2,1,0:T(8,128)(2,1)S(1)}, bf16[64,64,128]{2,1,0:T(8,128)(2,1)S(1)}, u32[]{:S(2)}, u32[]{:S(2)}) collective-permute-start(bf16[64,64,128]{2,1,0:T(8,128)(2,1)S(1)} %shard_map.152.own_ref), channel_id=1, source_target_pairs={{0,64},{64,0},{1,65},{65,1},{2,66},{66,2},{3,67},{67,3},{4,68},{68... | collective-permute-start | bytes 3145736 | tf_op jit(solution)/shard_map/ppermute | solution.py:556
  187.1 57.4 %all-to-all-start.2 = ((bf16[128,64,128]{2,1,0:T(8,128)(2,1)}), bf16[128,64,128]{2,1,0:T(8,128)(2,1)}, u32[]{:S(2)}, u32[]{:S(2)}) async-start(bf16[128,64,128]{2,1,0:T(8,128)(2,1)} %get-tuple-element.25), calls=%async_computation.2 | async-start | bytes 4194304 | tf_op jit(solution)/shard_map/all_to_all | solution.py:491
  223.2 32.6 %collective-permute-start.10 = (bf16[64,64,128]{2,1,0:T(8,128)(2,1)S(1)}, bf16[64,64,128]{2,1,0:T(8,128)(2,1)S(1)}, u32[]{:S(2)}, u32[]{:S(2)}) collective-permute-start(bf16[64,64,128]{2,1,0:T(8,128)(2,1)S(1)} %get-tuple-element.31), channel_id=1, source_target_pairs={{0,64},{64,0},{1,65},{65,1},{2,66},{66,2},{3,67},{67,3},{4,68},{68... | collective-permute-start | bytes 3145736 | tf_op jit(solution)/shard_map/ppermute | solution.py:573
  244.4 132.8 %all-to-all-start.3 = ((bf16[128,64,128]{2,1,0:T(8,128)(2,1)}), bf16[128,64,128]{2,1,0:T(8,128)(2,1)}, u32[]{:S(2)}, u32[]{:S(2)}) async-start(bf16[128,64,128]{2,1,0:T(8,128)(2,1)} %get-tuple-element.29), calls=%async_computation.3 | async-start | bytes 4194304 | tf_op jit(solution)/shard_map/all_to_all | solution.py:491
  260.5 50.7 %collective-permute-start.13 = (bf16[1,4,4,64,128]{4,3,2,1,0:T(8,128)(2,1)S(1)}, bf16[1,4,4,64,128]{4,3,2,1,0:T(8,128)(2,1)S(1)}, u32[]{:S(2)}, u32[]{:S(2)}) collective-permute-start(bf16[1,4,4,64,128]{4,3,2,1,0:T(8,128)(2,1)S(1)} %get-tuple-element.45), channel_id=1, source_target_pairs={{0,48},{16,0},{32,16},{48,32},{1,49},{17,1},{33,17},{49,33},{2,50}... | collective-permute-start | bytes 786440 | tf_op jit(solution)/shard_map/ppermute | solution.py:482
  263.3 63.5 %collective-permute-start.12 = (bf16[1,4,4,64,128]{4,3,2,1,0:T(8,128)(2,1)S(1)}, bf16[1,4,4,64,128]{4,3,2,1,0:T(8,128)(2,1)S(1)}, u32[]{:S(2)}, u32[]{:S(2)}) collective-permute-start(bf16[1,4,4,64,128]{4,3,2,1,0:T(8,128)(2,1)S(1)} %get-tuple-element.46), channel_id=1, source_target_pairs={{0,32},{16,48},{32,0},{48,16},{1,33},{17,49},{33,1},{49,17},{2,34}... | collective-permute-start | bytes 786440 | tf_op jit(solution)/shard_map/ppermute | solution.py:482
  266.1 60.7 %collective-permute-start.11 = (bf16[1,4,4,64,128]{4,3,2,1,0:T(8,128)(2,1)S(1)}, bf16[1,4,4,64,128]{4,3,2,1,0:T(8,128)(2,1)S(1)}, u32[]{:S(2)}, u32[]{:S(2)}) collective-permute-start(bf16[1,4,4,64,128]{4,3,2,1,0:T(8,128)(2,1)S(1)} %get-tuple-element.47), channel_id=1, source_target_pairs={{0,16},{16,32},{32,48},{48,0},{1,17},{17,33},{33,49},{49,1},{2,18}... | collective-permute-start | bytes 786440 | tf_op jit(solution)/shard_map/ppermute | solution.py:482
  327.0 6.5 %collective-permute-start.16 = (bf16[4,1,4,64,128]{4,3,2,1,0:T(8,128)(2,1)S(1)}, bf16[4,1,4,64,128]{4,3,2,1,0:T(8,128)(2,1)S(1)}, u32[]{:S(2)}, u32[]{:S(2)}) collective-permute-start(bf16[4,1,4,64,128]{4,3,2,1,0:T(8,128)(2,1)S(1)} %get-tuple-element.41), channel_id=1, source_target_pairs={{0,12},{4,0},{8,4},{12,8},{1,13},{5,1},{9,5},{13,9},{2,14},{6,2},{... | collective-permute-start | bytes 786440 | tf_op jit(solution)/shard_map/ppermute | solution.py:482
  329.2 7.6 %collective-permute-start.15 = (bf16[4,1,4,64,128]{4,3,2,1,0:T(8,128)(2,1)S(1)}, bf16[4,1,4,64,128]{4,3,2,1,0:T(8,128)(2,1)S(1)}, u32[]{:S(2)}, u32[]{:S(2)}) collective-permute-start(bf16[4,1,4,64,128]{4,3,2,1,0:T(8,128)(2,1)S(1)} %get-tuple-element.42), channel_id=1, source_target_pairs={{0,8},{4,12},{8,0},{12,4},{1,9},{5,13},{9,1},{13,5},{2,10},{6,14},... | collective-permute-start | bytes 786440 | tf_op jit(solution)/shard_map/ppermute | solution.py:482
  330.1 14.4 %collective-permute-start.14 = (bf16[4,1,4,64,128]{4,3,2,1,0:T(8,128)(2,1)S(1)}, bf16[4,1,4,64,128]{4,3,2,1,0:T(8,128)(2,1)S(1)}, u32[]{:S(2)}, u32[]{:S(2)}) collective-permute-start(bf16[4,1,4,64,128]{4,3,2,1,0:T(8,128)(2,1)S(1)} %get-tuple-element.43), channel_id=1, source_target_pairs={{0,4},{4,8},{8,12},{12,0},{1,5},{5,9},{9,13},{13,1},{2,6},{6,10},{... | collective-permute-start | bytes 786440 | tf_op jit(solution)/shard_map/ppermute | solution.py:482
  344.7 7.4 %collective-permute-start.19 = (bf16[4,4,1,64,128]{4,3,2,1,0:T(8,128)(2,1)S(1)}, bf16[4,4,1,64,128]{4,3,2,1,0:T(8,128)(2,1)S(1)}, u32[]{:S(2)}, u32[]{:S(2)}) collective-permute-start(bf16[4,4,1,64,128]{4,3,2,1,0:T(8,128)(2,1)S(1)} %get-tuple-element.37), channel_id=1, source_target_pairs={{0,3},{1,0},{2,1},{3,2},{4,7},{5,4},{6,5},{7,6},{8,11},{9,8},{10,9... | collective-permute-start | bytes 786440 | tf_op jit(solution)/shard_map/ppermute | solution.py:482
  345.1 13.5 %collective-permute-start.18 = (bf16[4,4,1,64,128]{4,3,2,1,0:T(8,128)(2,1)S(1)}, bf16[4,4,1,64,128]{4,3,2,1,0:T(8,128)(2,1)S(1)}, u32[]{:S(2)}, u32[]{:S(2)}) collective-permute-start(bf16[4,4,1,64,128]{4,3,2,1,0:T(8,128)(2,1)S(1)} %get-tuple-element.38), channel_id=1, source_target_pairs={{0,2},{1,3},{2,0},{3,1},{4,6},{5,7},{6,4},{7,5},{8,10},{9,11},{10,... | collective-permute-start | bytes 786440 | tf_op jit(solution)/shard_map/ppermute | solution.py:482
  347.1 12.4 %collective-permute-start.17 = (bf16[4,4,1,64,128]{4,3,2,1,0:T(8,128)(2,1)S(1)}, bf16[4,4,1,64,128]{4,3,2,1,0:T(8,128)(2,1)S(1)}, u32[]{:S(2)}, u32[]{:S(2)}) collective-permute-start(bf16[4,4,1,64,128]{4,3,2,1,0:T(8,128)(2,1)S(1)} %get-tuple-element.39), channel_id=1, source_target_pairs={{0,1},{1,2},{2,3},{3,0},{4,5},{5,6},{6,7},{7,4},{8,9},{9,10},{10,1... | collective-permute-start | bytes 786440 | tf_op jit(solution)/shard_map/ppermute | solution.py:482
  (16 other events, 82.7 us)

commit v4 on v3

--- a/solution.py
+++ b/solution.py
@@ -91,7 +91,7 @@
 
 
 PAD = 2
-TURN = 8
+TURN = 16
 BATCH = 4
 
 
@@ -125,7 +125,7 @@
         block = x_ref[c, offset : offset + blocks, :]
         rows_ref[pl.ds(c * (blocks + PAD), blocks), :] = block.astype(F32)
 
-    loop(items, put, 4)
+    loop(items, put, 16 if blocks <= TURN else 4)
 
 
 def take_turn(rows_ref, out_ref):
@@ -349,7 +349,7 @@
             k1 = b * BATCH + 1 + t
             store(k1, 0.5 * (ref[k1].astype(F32) + sign * row_part(turned, t, F2)))
 
-    loop(count // BATCH - 1, batch, 3)
+    loop(count // BATCH - 1, batch)
     batch(count // BATCH - 1, BATCH - 1)
 
 
@@ -534,18 +534,18 @@
     wv, wg = w_proj[:, :channels].T, w_proj[:, channels:].T
     wpv, wpg = w_proj[:, :channels], w_proj[:, channels:]
 
-    (values,) = chunked(values_body, 5, (wv,), (tok,), (message,), (), (turn_rows,))
-    values = exchange(values)
-
     chosen = lax.dynamic_slice(kernel, (core, z_low * share, 0), (1, share, positions))[0]
     response = call(
         spread_body, part, [pltpu.VMEM((blocks * (share + PAD), LANES), F32)],
         chosen, micros=3,
     )
-    response = ring_step(cube(response, size), 2, size)
+    response = ring_step(cube(response, size), 0, size)
+
+    (values,) = chunked(values_body, 5, (wv,), (tok,), (message,), (), (turn_rows,))
+    values = exchange(values)
     (grads,) = chunked(grads_body, 6, (wg, w_out), (tok, cot), (message,), (), (turn_rows,))
     grads, response = lax.optimization_barrier((grads, response))
-    response = ring_step(ring_step(response, 1, size), 0, size)
+    response = ring_step(ring_step(response, 1, size), 2, size)
     grads, values = lax.optimization_barrier((grads, values))
     grads = exchange(grads)
     response = call(

time: 389 us -> 371 us (0.954)
  waiting for transfers between devices: 198 us -> 188 us
  Pallas kernels: 92.1 us -> 88 us
    all_to_all x4, waiting for transfers between devices: 35.4 us -> 20.3 us  [exchange(): return lax.all_to_all(x, GROUP, split_axis=0, concat_axis=0, tiled=True)]
    pallas_call x4, Pallas kernels: 34.6 us -> 26 us  [chunked(): pl.pallas_call(body, grid=(steps,), out_shape=outs, in_specs=whole + [spe...]
    ppermute x18, waiting for transfers between devices: 158 us -> 164 us  [ring_step(): parts.append(lax.ppermute(slab, RING[axis], ring) if step else slab)]
    pallas_call x6, Pallas kernels: 57.5 us -> 62.1 us  [call(): pl.pallas_call(body, out_shape=out_shape, in_specs=[SMEM_SPEC] * smem + v...]
  transfers between devices with their start and end apart: 25 -> 25, of which waited for: 16 -> 16; matrix products, arithmetic and copies ran while one was open for 1% -> 1% of each run, Pallas kernels for 20% -> 21%
where the time goes in v4:
time: 371 us; the launch traced here: 368 us
  waiting for transfers between devices  188 us (51%)
  Pallas kernels  88 us (24%)
  starting transfers between devices  78.9 us (21%)
  local copies, waits for them, and re-layouts  9.52 us (3%)
    ppermute x18, waiting for transfers between devices, ring_step(): parts.append(lax.ppermute(slab, RING[axis], ring) if step else slab)  164 us
    pallas_call x6, Pallas kernels, call(): pl.pallas_call(body, out_shape=out_shape, in_specs=[SMEM_SPEC] * smem + v...  62.1 us
    all_to_all x4, starting transfers between devices, exchange(): return lax.all_to_all(x, GROUP, split_axis=0, concat_axis=0, tiled=True)  44.4 us
    ppermute x18, starting transfers between devices, ring_step(): parts.append(lax.ppermute(slab, RING[axis], ring) if step else slab)  30.3 us
    pallas_call x4, Pallas kernels, chunked(): pl.pallas_call(body, grid=(steps,), out_shape=outs, in_specs=whole + [spe...  26 us
    all_to_all x4, waiting for transfers between devices, exchange(): return lax.all_to_all(x, GROUP, split_axis=0, concat_axis=0, tiled=True)  20.3 us
  transfers between devices with their start and end apart: 25, of which 16 were waited for; matrix products, arithmetic and copies ran while one was open for 1% of the time, Pallas kernels for 21%

profile of v4, /device:TPU:35, one launch (start us, length us, event | category | flops | bytes accessed | tf_op | source)
XLA Modules:
  0.0 368.3 jit_solution(9488668900071423617)
XLA Ops:
  1.5 4.6 %shard_map.151 = bf16[128,64,128]{2,1,0:T(8,128)(2,1)} custom-call(bf16[128,128]{1,0:T(8,128)(2,1)S(1)} %copy.18.wv_ref, bf16[128,8192]{1,0:T(8,128)(2,1)} %bitcast.23), custom_call_target="tpu_custom_call" | custom-call | flops 5000000000 | bytes 15000000 | tf_op jit(solution)/shard_map/pallas_call | solution.py:435
  6.1 14.7 %all-to-all-start = ((bf16[128,64,128]{2,1,0:T(8,128)(2,1)}), bf16[128,64,128]{2,1,0:T(8,128)(2,1)S(1)}, u32[]{:S(2)}, u32[]{:S(2)}) async-start(bf16[128,64,128]{2,1,0:T(8,128)(2,1)} %shard_map.151), calls=%async_computation | async-start | bytes 4194304 | tf_op jit(solution)/shard_map/all_to_all | solution.py:491
  29.8 5.3 %shard_map.149 = bf16[128,64,128]{2,1,0:T(8,128)(2,1)} custom-call(bf16[128,128]{1,0:T(8,128)(2,1)S(1)} %copy.19.wg_ref, bf16[128,128]{1,0:T(8,128)(2,1)S(1)} %copy-done, bf16[128,8192]{1,0:T(8,128)(2,1)} %bitcast.24, bf16[128,8192]{1,0:T(8,128)(2,1)} %bitcast.26), custom_call_target="tpu_custom_call" | custom-call | flops 6000000000 | bytes 18000000 | tf_op jit(solution)/shard_map/pallas_call | solution.py:435
  35.1 43.4 %collective-permute-done.2 = bf16[1,4,4,64,128]{4,3,2,1,0:T(8,128)(2,1)} collective-permute-done((bf16[1,4,4,64,128]{4,3,2,1,0:T(8,128)(2,1)S(1)}, bf16[1,4,4,64,128]{4,3,2,1,0:T(8,128)(2,1)}, u32[]{:S(2)}, u32[]{:S(2)}) %collective-permute-start.2) | collective-permute-done | bytes 262176 | tf_op jit(solution)/shard_map/ppermute | solution.py:482
  78.5 14.1 %collective-permute-done.1 = bf16[1,4,4,64,128]{4,3,2,1,0:T(8,128)(2,1)} collective-permute-done((bf16[1,4,4,64,128]{4,3,2,1,0:T(8,128)(2,1)S(1)}, bf16[1,4,4,64,128]{4,3,2,1,0:T(8,128)(2,1)}, u32[]{:S(2)}, u32[]{:S(2)}) %collective-permute-start.1) | collective-permute-done | bytes 262176 | tf_op jit(solution)/shard_map/ppermute | solution.py:482
  98.6 9.4 %all-to-all-start.1 = ((bf16[128,64,128]{2,1,0:T(8,128)(2,1)}), bf16[128,64,128]{2,1,0:T(8,128)(2,1)}, u32[]{:S(2)}, u32[]{:S(2)}) async-start(bf16[128,64,128]{2,1,0:T(8,128)(2,1)} %shard_map.149), calls=%async_computation.1 | async-start | bytes 4194304 | tf_op jit(solution)/shard_map/all_to_all | solution.py:491
  108.0 4.6 %collective-permute-done.3 = bf16[4,1,4,64,128]{4,3,2,1,0:T(8,128)(2,1)} collective-permute-done((bf16[4,1,4,64,128]{4,3,2,1,0:T(8,128)(2,1)S(1)}, bf16[4,1,4,64,128]{4,3,2,1,0:T(8,128)(2,1)}, u32[]{:S(2)}, u32[]{:S(2)}) %collective-permute-start.3) | collective-permute-done | bytes 262176 | tf_op jit(solution)/shard_map/ppermute | solution.py:482
  114.1 4.0 %collective-permute-start.7 = (bf16[4,4,1,64,128]{4,3,2,1,0:T(8,128)(2,1)S(1)}, bf16[4,4,1,64,128]{4,3,2,1,0:T(8,128)(2,1)S(1)}, u32[]{:S(2)}, u32[]{:S(2)}) collective-permute-start(bf16[4,4,1,64,128]{4,3,2,1,0:T(8,128)(2,1)S(1)} %get-tuple-element.50), channel_id=1, source_target_pairs={{0,2},{1,3},{2,0},{3,1},{4,6},{5,7},{6,4},{7,5},{8,10},{9,11},{10,... | collective-permute-start | bytes 786440 | tf_op jit(solution)/shard_map/ppermute | solution.py:482
  120.1 5.4 %collective-permute-done.8 = bf16[4,4,1,64,128]{4,3,2,1,0:T(8,128)(2,1)S(1)} collective-permute-done((bf16[4,4,1,64,128]{4,3,2,1,0:T(8,128)(2,1)S(1)}, bf16[4,4,1,64,128]{4,3,2,1,0:T(8,128)(2,1)S(1)}, u32[]{:S(2)}, u32[]{:S(2)}) %collective-permute-start.8) | collective-permute-done | bytes 262176 | tf_op jit(solution)/shard_map/ppermute | solution.py:482
  125.5 13.9 %collective-permute-done.7 = bf16[4,4,1,64,128]{4,3,2,1,0:T(8,128)(2,1)S(1)} collective-permute-done((bf16[4,4,1,64,128]{4,3,2,1,0:T(8,128)(2,1)S(1)}, bf16[4,4,1,64,128]{4,3,2,1,0:T(8,128)(2,1)S(1)}, u32[]{:S(2)}, u32[]{:S(2)}) %collective-permute-start.7) | collective-permute-done | bytes 262176 | tf_op jit(solution)/shard_map/ppermute | solution.py:482
  139.6 7.5 %shard_map.152.own_ref = bf16[64,64,128]{2,1,0:T(8,128)(2,1)S(1)} custom-call(s32[4]{0:T(128)S(1)} %pad_add_fusion.place_ref.core_ref, bf16[64,64,128]{2,1,0:T(8,128)(2,1)S(1)} %bitcast.20), custom_call_target="tpu_custom_call" | custom-call | flops 4000000000 | bytes 12000000 | tf_op jit(solution)/shard_map/pallas_call | solution.py:55
  151.0 21.7 %shard_map.153 = (bf16[128,64,128]{2,1,0:T(8,128)(2,1)}, bf16[64,64,256]{2,1,0:T(8,128)(2,1)S(1)}) custom-call(s32[4]{0:T(128)S(1)} %pad_add_fusion.place_ref.core_ref, bf16[128,64,128]{2,1,0:T(8,128)(2,1)} %copy-done.13, bf16[64,64,128]{2,1,0:T(8,128)(2,1)S(1)} %shard_map.152.own_ref, bf16[64,64,128]{2,1,0:T(8,128)(2,1)S(1)} %collective-permute-done.9.other_ref, ...), custom_call_target="tpu_custom_call" | custom-call | flops 20000000000 | bytes 60000000 | tf_op jit(solution)/shard_map/pallas_call | solution.py:55
  174.0 8.8 %all-to-all-start.2 = ((bf16[128,64,128]{2,1,0:T(8,128)(2,1)}), bf16[128,64,128]{2,1,0:T(8,128)(2,1)}, u32[]{:S(2)}, u32[]{:S(2)}) async-start(bf16[128,64,128]{2,1,0:T(8,128)(2,1)} %get-tuple-element.25), calls=%async_computation.2 | async-start | bytes 4194304 | tf_op jit(solution)/shard_map/all_to_all | solution.py:491
  185.6 22.9 %shard_map.154 = (bf16[128,64,128]{2,1,0:T(8,128)(2,1)}, bf16[64,64,128]{2,1,0:T(8,128)(2,1)S(1)}, bf16[64,64,128]{2,1,0:T(8,128)(2,1)S(1)}) custom-call(s32[4]{0:T(128)S(1)} %pad_add_fusion.place_ref.core_ref, bf16[128,64,128]{2,1,0:T(8,128)(2,1)} %all-to-all-done.1.z_ref, bf16[64,64,128]{2,1,0:T(8,128)(2,1)S(1)} %shard_map.152.own_ref, ...), custom_call_target="tpu_custom_call" | custom-call | flops 22000001024 | bytes 66000000 | tf_op jit(solution)/shard_map/pallas_call | solution.py:55
  210.4 20.2 %all-to-all-done.2.conv_ref = bf16[128,64,128]{2,1,0:T(8,128)(2,1)} async-done(((bf16[128,64,128]{2,1,0:T(8,128)(2,1)}), bf16[128,64,128]{2,1,0:T(8,128)(2,1)}, u32[]{:S(2)}, u32[]{:S(2)}) %all-to-all-start.2) | async-done | bytes 2097184 | tf_op jit(solution)/shard_map/all_to_all | solution.py:491
  230.7 11.5 %all-to-all-start.3 = ((bf16[128,64,128]{2,1,0:T(8,128)(2,1)}), bf16[128,64,128]{2,1,0:T(8,128)(2,1)}, u32[]{:S(2)}, u32[]{:S(2)}) async-start(bf16[128,64,128]{2,1,0:T(8,128)(2,1)} %get-tuple-element.29), calls=%async_computation.3 | async-start | bytes 4194304 | tf_op jit(solution)/shard_map/all_to_all | solution.py:491
  242.1 6.8 %shard_map.157 = bf16[64,64,128]{2,1,0:T(8,128)(2,1)S(1)} custom-call(s32[4]{0:T(128)S(1)} %pad_add_fusion.place_ref.core_ref, bf16[64,64,128]{2,1,0:T(8,128)(2,1)S(1)} %copy-done.11, bf16[64,64,128]{2,1,0:T(8,128)(2,1)S(1)} %collective-permute-done.10.recv_ref), custom_call_target="tpu_custom_call" | custom-call | flops 5000000000 | bytes 15000000 | tf_op jit(solution)/shard_map/pallas_call | solution.py:55
  255.9 41.6 %collective-permute-done.13 = bf16[1,4,4,64,128]{4,3,2,1,0:T(8,128)(2,1)S(1)} collective-permute-done((bf16[1,4,4,64,128]{4,3,2,1,0:T(8,128)(2,1)S(1)}, bf16[1,4,4,64,128]{4,3,2,1,0:T(8,128)(2,1)S(1)}, u32[]{:S(2)}, u32[]{:S(2)}) %collective-permute-start.13) | collective-permute-done | bytes 262176 | tf_op jit(solution)/shard_map/ppermute | solution.py:482
  297.4 15.6 %collective-permute-done.12 = bf16[1,4,4,64,128]{4,3,2,1,0:T(8,128)(2,1)S(1)} collective-permute-done((bf16[1,4,4,64,128]{4,3,2,1,0:T(8,128)(2,1)S(1)}, bf16[1,4,4,64,128]{4,3,2,1,0:T(8,128)(2,1)S(1)}, u32[]{:S(2)}, u32[]{:S(2)}) %collective-permute-start.12) | collective-permute-done | bytes 262176 | tf_op jit(solution)/shard_map/ppermute | solution.py:482
  323.0 7.8 %collective-permute-done.14 = bf16[4,1,4,64,128]{4,3,2,1,0:T(8,128)(2,1)S(1)} collective-permute-done((bf16[4,1,4,64,128]{4,3,2,1,0:T(8,128)(2,1)S(1)}, bf16[4,1,4,64,128]{4,3,2,1,0:T(8,128)(2,1)S(1)}, u32[]{:S(2)}, u32[]{:S(2)}) %collective-permute-start.14) | collective-permute-done | bytes 262176 | tf_op jit(solution)/shard_map/ppermute | solution.py:482
  335.2 3.4 collective-permute-done.19
  338.6 6.4 %collective-permute-done.18 = bf16[4,4,1,64,128]{4,3,2,1,0:T(8,128)(2,1)S(1)} collective-permute-done((bf16[4,4,1,64,128]{4,3,2,1,0:T(8,128)(2,1)S(1)}, bf16[4,4,1,64,128]{4,3,2,1,0:T(8,128)(2,1)S(1)}, u32[]{:S(2)}, u32[]{:S(2)}) %collective-permute-start.18) | collective-permute-done | bytes 262176 | tf_op jit(solution)/shard_map/ppermute | solution.py:482
  352.2 9.8 %shard_map.155 = (f32[128,8192]{1,0:T(8,128)}, f32[128,8192]{1,0:T(8,128)}) custom-call(bf16[128,128]{1,0:T(8,128)(2,1)S(1)} %copy.18.wv_ref, bf16[128,128]{1,0:T(8,128)(2,1)S(1)} %copy.19.wg_ref, bf16[128,128]{1,0:T(8,128)(2,1)S(1)} %copy-done, bf16[128,128]{1,0:T(8,128)(2,1)S(1)} %get-tuple-element.60.wpg_ref, f32[128,256]{1,0:T(8,128)S(1)} %broadcast_in_dim.2.skip_ref, ...), custom_call_target="tpu_custom_call" | custom-call | flops 10000000000 | bytes 30000000 | tf_op jit(solution)/shard_map/pallas_call | solution.py:435
  362.0 6.3 %shard_map.156 = bf16[128,8192]{1,0:T(8,128)(2,1)} custom-call(bf16[128,128]{1,0:T(8,128)(2,1)S(1)} %get-tuple-element.63.wpv_ref, f32[128,8192]{1,0:T(8,128)} %get-tuple-element.27.part_ref, f32[128,8192]{1,0:T(8,128)} %get-tuple-element.28.own_ref, bf16[128,64,128]{2,1,0:T(8,128)(2,1)} %all-to-all-done.3.back_ref), custom_call_target="tpu_custom_call" | custom-call | flops 6000000000 | bytes 18000000 | tf_op jit(solution)/shard_map/pallas_call | solution.py:435
  (87 shorter events, 57.7 us)
Async XLA Ops:
  6.1 91.2 %all-to-all-start = ((bf16[128,64,128]{2,1,0:T(8,128)(2,1)}), bf16[128,64,128]{2,1,0:T(8,128)(2,1)S(1)}, u32[]{:S(2)}, u32[]{:S(2)}) async-start(bf16[128,64,128]{2,1,0:T(8,128)(2,1)} %shard_map.151), calls=%async_computation | async-start | bytes 4194304 | tf_op jit(solution)/shard_map/all_to_all | solution.py:491
  22.8 55.7 %collective-permute-start.2 = (bf16[1,4,4,64,128]{4,3,2,1,0:T(8,128)(2,1)S(1)}, bf16[1,4,4,64,128]{4,3,2,1,0:T(8,128)(2,1)}, u32[]{:S(2)}, u32[]{:S(2)}) collective-permute-start(bf16[1,4,4,64,128]{4,3,2,1,0:T(8,128)(2,1)S(1)} %get-tuple-element.57), channel_id=1, source_target_pairs={{0,48},{16,0},{32,16},{48,32},{1,49},{17,1},{33,17},{49,33},{2,50}... | collective-permute-start | bytes 786440 | tf_op jit(solution)/shard_map/ppermute | solution.py:482
  25.6 67.0 %collective-permute-start.1 = (bf16[1,4,4,64,128]{4,3,2,1,0:T(8,128)(2,1)S(1)}, bf16[1,4,4,64,128]{4,3,2,1,0:T(8,128)(2,1)}, u32[]{:S(2)}, u32[]{:S(2)}) collective-permute-start(bf16[1,4,4,64,128]{4,3,2,1,0:T(8,128)(2,1)S(1)} %get-tuple-element.58), channel_id=1, source_target_pairs={{0,32},{16,48},{32,0},{48,16},{1,33},{17,49},{33,1},{49,17},{2,34}... | collective-permute-start | bytes 786440 | tf_op jit(solution)/shard_map/ppermute | solution.py:482
  28.4 64.2 %collective-permute-start = (bf16[1,4,4,64,128]{4,3,2,1,0:T(8,128)(2,1)S(1)}, bf16[1,4,4,64,128]{4,3,2,1,0:T(8,128)(2,1)}, u32[]{:S(2)}, u32[]{:S(2)}) collective-permute-start(bf16[1,4,4,64,128]{4,3,2,1,0:T(8,128)(2,1)S(1)} %get-tuple-element.59), channel_id=1, source_target_pairs={{0,16},{16,32},{32,48},{48,0},{1,17},{17,33},{33,49},{49,1},{2,18}... | collective-permute-start | bytes 786440 | tf_op jit(solution)/shard_map/ppermute | solution.py:482
  94.0 14.1 %collective-permute-start.5 = (bf16[4,1,4,64,128]{4,3,2,1,0:T(8,128)(2,1)S(1)}, bf16[4,1,4,64,128]{4,3,2,1,0:T(8,128)(2,1)}, u32[]{:S(2)}, u32[]{:S(2)}) collective-permute-start(bf16[4,1,4,64,128]{4,3,2,1,0:T(8,128)(2,1)S(1)} %get-tuple-element.53), channel_id=1, source_target_pairs={{0,12},{4,0},{8,4},{12,8},{1,13},{5,1},{9,5},{13,9},{2,14},{6,2},{... | collective-permute-start | bytes 786440 | tf_op jit(solution)/shard_map/ppermute | solution.py:482
  96.0 12.0 %collective-permute-start.4 = (bf16[4,1,4,64,128]{4,3,2,1,0:T(8,128)(2,1)S(1)}, bf16[4,1,4,64,128]{4,3,2,1,0:T(8,128)(2,1)}, u32[]{:S(2)}, u32[]{:S(2)}) collective-permute-start(bf16[4,1,4,64,128]{4,3,2,1,0:T(8,128)(2,1)S(1)} %get-tuple-element.54), channel_id=1, source_target_pairs={{0,8},{4,12},{8,0},{12,4},{1,9},{5,13},{9,1},{13,5},{2,10},{6,14},... | collective-permute-start | bytes 786440 | tf_op jit(solution)/shard_map/ppermute | solution.py:482
  97.1 15.6 %collective-permute-start.3 = (bf16[4,1,4,64,128]{4,3,2,1,0:T(8,128)(2,1)S(1)}, bf16[4,1,4,64,128]{4,3,2,1,0:T(8,128)(2,1)}, u32[]{:S(2)}, u32[]{:S(2)}) collective-permute-start(bf16[4,1,4,64,128]{4,3,2,1,0:T(8,128)(2,1)S(1)} %get-tuple-element.55), channel_id=1, source_target_pairs={{0,4},{4,8},{8,12},{12,0},{1,5},{5,9},{9,13},{13,1},{2,6},{6,10},{... | collective-permute-start | bytes 786440 | tf_op jit(solution)/shard_map/ppermute | solution.py:482
  98.6 75.5 %all-to-all-start.1 = ((bf16[128,64,128]{2,1,0:T(8,128)(2,1)}), bf16[128,64,128]{2,1,0:T(8,128)(2,1)}, u32[]{:S(2)}, u32[]{:S(2)}) async-start(bf16[128,64,128]{2,1,0:T(8,128)(2,1)} %shard_map.149), calls=%async_computation.1 | async-start | bytes 4194304 | tf_op jit(solution)/shard_map/all_to_all | solution.py:491
  114.0 11.5 %collective-permute-start.8 = (bf16[4,4,1,64,128]{4,3,2,1,0:T(8,128)(2,1)S(1)}, bf16[4,4,1,64,128]{4,3,2,1,0:T(8,128)(2,1)S(1)}, u32[]{:S(2)}, u32[]{:S(2)}) collective-permute-start(bf16[4,4,1,64,128]{4,3,2,1,0:T(8,128)(2,1)S(1)} %get-tuple-element.49), channel_id=1, source_target_pairs={{0,3},{1,0},{2,1},{3,2},{4,7},{5,4},{6,5},{7,6},{8,11},{9,8},{10,9... | collective-permute-start | bytes 786440 | tf_op jit(solution)/shard_map/ppermute | solution.py:482
  114.1 25.3 %collective-permute-start.7 = (bf16[4,4,1,64,128]{4,3,2,1,0:T(8,128)(2,1)S(1)}, bf16[4,4,1,64,128]{4,3,2,1,0:T(8,128)(2,1)S(1)}, u32[]{:S(2)}, u32[]{:S(2)}) collective-permute-start(bf16[4,4,1,64,128]{4,3,2,1,0:T(8,128)(2,1)S(1)} %get-tuple-element.50), channel_id=1, source_target_pairs={{0,2},{1,3},{2,0},{3,1},{4,6},{5,7},{6,4},{7,5},{8,10},{9,11},{10,... | collective-permute-start | bytes 786440 | tf_op jit(solution)/shard_map/ppermute | solution.py:482
  118.1 21.4 %collective-permute-start.6 = (bf16[4,4,1,64,128]{4,3,2,1,0:T(8,128)(2,1)S(1)}, bf16[4,4,1,64,128]{4,3,2,1,0:T(8,128)(2,1)S(1)}, u32[]{:S(2)}, u32[]{:S(2)}) collective-permute-start(bf16[4,4,1,64,128]{4,3,2,1,0:T(8,128)(2,1)S(1)} %get-tuple-element.51), channel_id=1, source_target_pairs={{0,1},{1,2},{2,3},{3,0},{4,5},{5,6},{6,7},{7,4},{8,9},{9,10},{10,1... | collective-permute-start | bytes 786440 | tf_op jit(solution)/shard_map/ppermute | solution.py:482
  147.1 3.9 %collective-permute-start.9 = (bf16[64,64,128]{2,1,0:T(8,128)(2,1)S(1)}, bf16[64,64,128]{2,1,0:T(8,128)(2,1)S(1)}, u32[]{:S(2)}, u32[]{:S(2)}) collective-permute-start(bf16[64,64,128]{2,1,0:T(8,128)(2,1)S(1)} %shard_map.152.own_ref), channel_id=1, source_target_pairs={{0,64},{64,0},{1,65},{65,1},{2,66},{66,2},{3,67},{67,3},{4,68},{68... | collective-permute-start | bytes 3145736 | tf_op jit(solution)/shard_map/ppermute | solution.py:556
  174.0 56.6 %all-to-all-start.2 = ((bf16[128,64,128]{2,1,0:T(8,128)(2,1)}), bf16[128,64,128]{2,1,0:T(8,128)(2,1)}, u32[]{:S(2)}, u32[]{:S(2)}) async-start(bf16[128,64,128]{2,1,0:T(8,128)(2,1)} %get-tuple-element.25), calls=%async_computation.2 | async-start | bytes 4194304 | tf_op jit(solution)/shard_map/all_to_all | solution.py:491
  209.5 32.6 %collective-permute-start.10 = (bf16[64,64,128]{2,1,0:T(8,128)(2,1)S(1)}, bf16[64,64,128]{2,1,0:T(8,128)(2,1)S(1)}, u32[]{:S(2)}, u32[]{:S(2)}) collective-permute-start(bf16[64,64,128]{2,1,0:T(8,128)(2,1)S(1)} %get-tuple-element.31), channel_id=1, source_target_pairs={{0,64},{64,0},{1,65},{65,1},{2,66},{66,2},{3,67},{67,3},{4,68},{68... | collective-permute-start | bytes 3145736 | tf_op jit(solution)/shard_map/ppermute | solution.py:573
  230.7 131.3 %all-to-all-start.3 = ((bf16[128,64,128]{2,1,0:T(8,128)(2,1)}), bf16[128,64,128]{2,1,0:T(8,128)(2,1)}, u32[]{:S(2)}, u32[]{:S(2)}) async-start(bf16[128,64,128]{2,1,0:T(8,128)(2,1)} %get-tuple-element.29), calls=%async_computation.3 | async-start | bytes 4194304 | tf_op jit(solution)/shard_map/all_to_all | solution.py:491
  249.0 48.4 %collective-permute-start.13 = (bf16[1,4,4,64,128]{4,3,2,1,0:T(8,128)(2,1)S(1)}, bf16[1,4,4,64,128]{4,3,2,1,0:T(8,128)(2,1)S(1)}, u32[]{:S(2)}, u32[]{:S(2)}) collective-permute-start(bf16[1,4,4,64,128]{4,3,2,1,0:T(8,128)(2,1)S(1)} %get-tuple-element.45), channel_id=1, source_target_pairs={{0,48},{16,0},{32,16},{48,32},{1,49},{17,1},{33,17},{49,33},{2,50}... | collective-permute-start | bytes 786440 | tf_op jit(solution)/shard_map/ppermute | solution.py:482
  251.8 61.2 %collective-permute-start.12 = (bf16[1,4,4,64,128]{4,3,2,1,0:T(8,128)(2,1)S(1)}, bf16[1,4,4,64,128]{4,3,2,1,0:T(8,128)(2,1)S(1)}, u32[]{:S(2)}, u32[]{:S(2)}) collective-permute-start(bf16[1,4,4,64,128]{4,3,2,1,0:T(8,128)(2,1)S(1)} %get-tuple-element.46), channel_id=1, source_target_pairs={{0,32},{16,48},{32,0},{48,16},{1,33},{17,49},{33,1},{49,17},{2,34}... | collective-permute-start | bytes 786440 | tf_op jit(solution)/shard_map/ppermute | solution.py:482
  254.6 58.4 %collective-permute-start.11 = (bf16[1,4,4,64,128]{4,3,2,1,0:T(8,128)(2,1)S(1)}, bf16[1,4,4,64,128]{4,3,2,1,0:T(8,128)(2,1)S(1)}, u32[]{:S(2)}, u32[]{:S(2)}) collective-permute-start(bf16[1,4,4,64,128]{4,3,2,1,0:T(8,128)(2,1)S(1)} %get-tuple-element.47), channel_id=1, source_target_pairs={{0,16},{16,32},{32,48},{48,0},{1,17},{17,33},{33,49},{49,1},{2,18}... | collective-permute-start | bytes 786440 | tf_op jit(solution)/shard_map/ppermute | solution.py:482
  313.3 6.5 %collective-permute-start.16 = (bf16[4,1,4,64,128]{4,3,2,1,0:T(8,128)(2,1)S(1)}, bf16[4,1,4,64,128]{4,3,2,1,0:T(8,128)(2,1)S(1)}, u32[]{:S(2)}, u32[]{:S(2)}) collective-permute-start(bf16[4,1,4,64,128]{4,3,2,1,0:T(8,128)(2,1)S(1)} %get-tuple-element.41), channel_id=1, source_target_pairs={{0,12},{4,0},{8,4},{12,8},{1,13},{5,1},{9,5},{13,9},{2,14},{6,2},{... | collective-permute-start | bytes 786440 | tf_op jit(solution)/shard_map/ppermute | solution.py:482
  315.4 7.6 %collective-permute-start.15 = (bf16[4,1,4,64,128]{4,3,2,1,0:T(8,128)(2,1)S(1)}, bf16[4,1,4,64,128]{4,3,2,1,0:T(8,128)(2,1)S(1)}, u32[]{:S(2)}, u32[]{:S(2)}) collective-permute-start(bf16[4,1,4,64,128]{4,3,2,1,0:T(8,128)(2,1)S(1)} %get-tuple-element.42), channel_id=1, source_target_pairs={{0,8},{4,12},{8,0},{12,4},{1,9},{5,13},{9,1},{13,5},{2,10},{6,14},... | collective-permute-start | bytes 786440 | tf_op jit(solution)/shard_map/ppermute | solution.py:482
  316.3 14.4 %collective-permute-start.14 = (bf16[4,1,4,64,128]{4,3,2,1,0:T(8,128)(2,1)S(1)}, bf16[4,1,4,64,128]{4,3,2,1,0:T(8,128)(2,1)S(1)}, u32[]{:S(2)}, u32[]{:S(2)}) collective-permute-start(bf16[4,1,4,64,128]{4,3,2,1,0:T(8,128)(2,1)S(1)} %get-tuple-element.43), channel_id=1, source_target_pairs={{0,4},{4,8},{8,12},{12,0},{1,5},{5,9},{9,13},{13,1},{2,6},{6,10},{... | collective-permute-start | bytes 786440 | tf_op jit(solution)/shard_map/ppermute | solution.py:482
  331.0 7.7 %collective-permute-start.19 = (bf16[4,4,1,64,128]{4,3,2,1,0:T(8,128)(2,1)S(1)}, bf16[4,4,1,64,128]{4,3,2,1,0:T(8,128)(2,1)S(1)}, u32[]{:S(2)}, u32[]{:S(2)}) collective-permute-start(bf16[4,4,1,64,128]{4,3,2,1,0:T(8,128)(2,1)S(1)} %get-tuple-element.37), channel_id=1, source_target_pairs={{0,3},{1,0},{2,1},{3,2},{4,7},{5,4},{6,5},{7,6},{8,11},{9,8},{10,9... | collective-permute-start | bytes 786440 | tf_op jit(solution)/shard_map/ppermute | solution.py:482
  331.5 13.5 %collective-permute-start.18 = (bf16[4,4,1,64,128]{4,3,2,1,0:T(8,128)(2,1)S(1)}, bf16[4,4,1,64,128]{4,3,2,1,0:T(8,128)(2,1)S(1)}, u32[]{:S(2)}, u32[]{:S(2)}) collective-permute-start(bf16[4,4,1,64,128]{4,3,2,1,0:T(8,128)(2,1)S(1)} %get-tuple-element.38), channel_id=1, source_target_pairs={{0,2},{1,3},{2,0},{3,1},{4,6},{5,7},{6,4},{7,5},{8,10},{9,11},{10,... | collective-permute-start | bytes 786440 | tf_op jit(solution)/shard_map/ppermute | solution.py:482
  333.5 12.4 %collective-permute-start.17 = (bf16[4,4,1,64,128]{4,3,2,1,0:T(8,128)(2,1)S(1)}, bf16[4,4,1,64,128]{4,3,2,1,0:T(8,128)(2,1)S(1)}, u32[]{:S(2)}, u32[]{:S(2)}) collective-permute-start(bf16[4,4,1,64,128]{4,3,2,1,0:T(8,128)(2,1)S(1)} %get-tuple-element.39), channel_id=1, source_target_pairs={{0,1},{1,2},{2,3},{3,0},{4,5},{5,6},{6,7},{7,4},{8,9},{9,10},{10,1... | collective-permute-start | bytes 786440 | tf_op jit(solution)/shard_map/ppermute | solution.py:482
  (16 other events, 99.2 us)

commit v5 on v4

--- a/solution.py
+++ b/solution.py
@@ -115,6 +115,25 @@
         out_ref[c] = rows_ref[pl.ds(c, blocks, stride=channels + PAD), :].astype(BF)
 
     loop(channels, take, 4)
+
+
+def spread_call(kernel, at, share):
+    positions = kernel.shape[2]
+    blocks = positions // LANES
+    return pl.pallas_call(
+        lambda at_ref, x_ref, out_ref, rows_ref: spread_body(x_ref.at[0], out_ref, rows_ref),
+        grid_spec=pltpu.PrefetchScalarGridSpec(
+            num_scalar_prefetch=1,
+            grid=(1,),
+            in_specs=[pl.BlockSpec((1, share, positions), lambda i, at: (at[0], at[1], 0))],
+            out_specs=pl.BlockSpec((share, blocks, LANES), lambda i, at: (0, 0, 0)),
+            scratch_shapes=[pltpu.VMEM((blocks * (share + PAD), LANES), F32)],
+        ),
+        out_shape=jax.ShapeDtypeStruct((share, blocks, LANES), BF),
+        compiler_params=pltpu.CompilerParams(vmem_limit_bytes=32 << 20),
+        cost_estimate=cost(3),
+        name="spread",
+    )(at, in_hbm(kernel))
 
 
 def unpack_rows(x_ref, rows_ref, offset=0, blocks=None):
@@ -534,11 +553,7 @@
     wv, wg = w_proj[:, :channels].T, w_proj[:, channels:].T
     wpv, wpg = w_proj[:, :channels], w_proj[:, channels:]
 
-    chosen = lax.dynamic_slice(kernel, (core, z_low * share, 0), (1, share, positions))[0]
-    response = call(
-        spread_body, part, [pltpu.VMEM((blocks * (share + PAD), LANES), F32)],
-        chosen, micros=3,
-    )
+    response = spread_call(kernel, jnp.stack([core, z_low]).astype(jnp.int32), share)
     response = ring_step(cube(response, size), 0, size)
 
     (values,) = chunked(values_body, 5, (wv,), (tok,), (message,), (), (turn_rows,))

time: 371 us -> 371 us (level)
    pallas_call x6 -> x5, Pallas kernels: 62.1 us -> 61.6 us  [call(): pl.pallas_call(body, out_shape=out_shape, in_specs=[SMEM_SPEC] * smem + v...]
where the time goes in v5:
time: 371 us; the launch traced here: 368 us
  waiting for transfers between devices  187 us (50%)
  Pallas kernels  89.8 us (24%)
  starting transfers between devices  78.9 us (21%)
  local copies, waits for them, and re-layouts  8.22 us (2%)
    ppermute x18, waiting for transfers between devices, ring_step(): parts.append(lax.ppermute(slab, RING[axis], ring) if step else slab)  163 us
    pallas_call x5, Pallas kernels, call(): pl.pallas_call(body, out_shape=out_shape, in_specs=[SMEM_SPEC] * smem + v...  61.6 us
    all_to_all x4, starting transfers between devices, exchange(): return lax.all_to_all(x, GROUP, split_axis=0, concat_axis=0, tiled=True)  44.4 us
    ppermute x18, starting transfers between devices, ring_step(): parts.append(lax.ppermute(slab, RING[axis], ring) if step else slab)  30.3 us
    pallas_call x4, Pallas kernels, chunked(): pl.pallas_call(body, grid=(steps,), out_shape=outs, in_specs=whole + [spe...  26 us
    all_to_all x4, waiting for transfers between devices, exchange(): return lax.all_to_all(x, GROUP, split_axis=0, concat_axis=0, tiled=True)  20.3 us
  transfers between devices with their start and end apart: 25, of which 16 were waited for; matrix products, arithmetic and copies ran while one was open for 1% of the time, Pallas kernels for 21%

profile of v5, /device:TPU:35, one launch (start us, length us, event | category | flops | bytes accessed | tf_op | source)
XLA Modules:
  0.0 368.3 jit_solution(3877163313509088656)
XLA Ops:
  1.5 4.6 %shard_map.150 = bf16[128,64,128]{2,1,0:T(8,128)(2,1)} custom-call(bf16[128,128]{1,0:T(8,128)(2,1)S(1)} %copy.18.wv_ref, bf16[128,8192]{1,0:T(8,128)(2,1)} %bitcast.22), custom_call_target="tpu_custom_call" | custom-call | flops 5000000000 | bytes 15000000 | tf_op jit(solution)/shard_map/pallas_call | solution.py:454
  6.1 14.7 %all-to-all-start = ((bf16[128,64,128]{2,1,0:T(8,128)(2,1)}), bf16[128,64,128]{2,1,0:T(8,128)(2,1)S(1)}, u32[]{:S(2)}, u32[]{:S(2)}) async-start(bf16[128,64,128]{2,1,0:T(8,128)(2,1)} %shard_map.150), calls=%async_computation | async-start | bytes 4194304 | tf_op jit(solution)/shard_map/all_to_all | solution.py:510
  30.3 5.3 %shard_map.149 = bf16[128,64,128]{2,1,0:T(8,128)(2,1)} custom-call(bf16[128,128]{1,0:T(8,128)(2,1)S(1)} %copy.19.wg_ref, bf16[128,128]{1,0:T(8,128)(2,1)S(1)} %copy-done, bf16[128,8192]{1,0:T(8,128)(2,1)} %bitcast.23, bf16[128,8192]{1,0:T(8,128)(2,1)} %bitcast.25), custom_call_target="tpu_custom_call" | custom-call | flops 6000000000 | bytes 18000000 | tf_op jit(solution)/shard_map/pallas_call | solution.py:454
  35.7 42.8 %collective-permute-done.2 = bf16[1,4,4,64,128]{4,3,2,1,0:T(8,128)(2,1)} collective-permute-done((bf16[1,4,4,64,128]{4,3,2,1,0:T(8,128)(2,1)S(1)}, bf16[1,4,4,64,128]{4,3,2,1,0:T(8,128)(2,1)}, u32[]{:S(2)}, u32[]{:S(2)}) %collective-permute-start.2) | collective-permute-done | bytes 262176 | tf_op jit(solution)/shard_map/ppermute | solution.py:501
  78.5 14.1 %collective-permute-done.1 = bf16[1,4,4,64,128]{4,3,2,1,0:T(8,128)(2,1)} collective-permute-done((bf16[1,4,4,64,128]{4,3,2,1,0:T(8,128)(2,1)S(1)}, bf16[1,4,4,64,128]{4,3,2,1,0:T(8,128)(2,1)}, u32[]{:S(2)}, u32[]{:S(2)}) %collective-permute-start.1) | collective-permute-done | bytes 262176 | tf_op jit(solution)/shard_map/ppermute | solution.py:501
  98.6 9.4 %all-to-all-start.1 = ((bf16[128,64,128]{2,1,0:T(8,128)(2,1)}), bf16[128,64,128]{2,1,0:T(8,128)(2,1)}, u32[]{:S(2)}, u32[]{:S(2)}) async-start(bf16[128,64,128]{2,1,0:T(8,128)(2,1)} %shard_map.149), calls=%async_computation.1 | async-start | bytes 4194304 | tf_op jit(solution)/shard_map/all_to_all | solution.py:510
  108.0 4.6 %collective-permute-done.3 = bf16[4,1,4,64,128]{4,3,2,1,0:T(8,128)(2,1)} collective-permute-done((bf16[4,1,4,64,128]{4,3,2,1,0:T(8,128)(2,1)S(1)}, bf16[4,1,4,64,128]{4,3,2,1,0:T(8,128)(2,1)}, u32[]{:S(2)}, u32[]{:S(2)}) %collective-permute-start.3) | collective-permute-done | bytes 262176 | tf_op jit(solution)/shard_map/ppermute | solution.py:501
  114.1 4.0 %collective-permute-start.7 = (bf16[4,4,1,64,128]{4,3,2,1,0:T(8,128)(2,1)S(1)}, bf16[4,4,1,64,128]{4,3,2,1,0:T(8,128)(2,1)S(1)}, u32[]{:S(2)}, u32[]{:S(2)}) collective-permute-start(bf16[4,4,1,64,128]{4,3,2,1,0:T(8,128)(2,1)S(1)} %get-tuple-element.50), channel_id=1, source_target_pairs={{0,2},{1,3},{2,0},{3,1},{4,6},{5,7},{6,4},{7,5},{8,10},{9,11},{10,... | collective-permute-start | bytes 786440 | tf_op jit(solution)/shard_map/ppermute | solution.py:501
  120.1 5.4 %collective-permute-done.8 = bf16[4,4,1,64,128]{4,3,2,1,0:T(8,128)(2,1)S(1)} collective-permute-done((bf16[4,4,1,64,128]{4,3,2,1,0:T(8,128)(2,1)S(1)}, bf16[4,4,1,64,128]{4,3,2,1,0:T(8,128)(2,1)S(1)}, u32[]{:S(2)}, u32[]{:S(2)}) %collective-permute-start.8) | collective-permute-done | bytes 262176 | tf_op jit(solution)/shard_map/ppermute | solution.py:501
  125.5 13.9 %collective-permute-done.7 = bf16[4,4,1,64,128]{4,3,2,1,0:T(8,128)(2,1)S(1)} collective-permute-done((bf16[4,4,1,64,128]{4,3,2,1,0:T(8,128)(2,1)S(1)}, bf16[4,4,1,64,128]{4,3,2,1,0:T(8,128)(2,1)S(1)}, u32[]{:S(2)}, u32[]{:S(2)}) %collective-permute-start.7) | collective-permute-done | bytes 262176 | tf_op jit(solution)/shard_map/ppermute | solution.py:501
  139.6 7.5 %shard_map.151.own_ref = bf16[64,64,128]{2,1,0:T(8,128)(2,1)S(1)} custom-call(s32[4]{0:T(128)S(1)} %pad_add_fusion.place_ref.core_ref, bf16[64,64,128]{2,1,0:T(8,128)(2,1)S(1)} %bitcast.19), custom_call_target="tpu_custom_call" | custom-call | flops 4000000000 | bytes 12000000 | tf_op jit(solution)/shard_map/pallas_call | solution.py:55
  151.0 21.7 %shard_map.152 = (bf16[128,64,128]{2,1,0:T(8,128)(2,1)}, bf16[64,64,256]{2,1,0:T(8,128)(2,1)S(1)}) custom-call(s32[4]{0:T(128)S(1)} %pad_add_fusion.place_ref.core_ref, bf16[128,64,128]{2,1,0:T(8,128)(2,1)} %copy-done.13, bf16[64,64,128]{2,1,0:T(8,128)(2,1)S(1)} %shard_map.151.own_ref, bf16[64,64,128]{2,1,0:T(8,128)(2,1)S(1)} %collective-permute-done.9.other_ref, ...), custom_call_target="tpu_custom_call" | custom-call | flops 20000000000 | bytes 60000000 | tf_op jit(solution)/shard_map/pallas_call | solution.py:55
  174.0 8.8 %all-to-all-start.2 = ((bf16[128,64,128]{2,1,0:T(8,128)(2,1)}), bf16[128,64,128]{2,1,0:T(8,128)(2,1)}, u32[]{:S(2)}, u32[]{:S(2)}) async-start(bf16[128,64,128]{2,1,0:T(8,128)(2,1)} %get-tuple-element.25), calls=%async_computation.2 | async-start | bytes 4194304 | tf_op jit(solution)/shard_map/all_to_all | solution.py:510
  185.6 22.9 %shard_map.153 = (bf16[128,64,128]{2,1,0:T(8,128)(2,1)}, bf16[64,64,128]{2,1,0:T(8,128)(2,1)S(1)}, bf16[64,64,128]{2,1,0:T(8,128)(2,1)S(1)}) custom-call(s32[4]{0:T(128)S(1)} %pad_add_fusion.place_ref.core_ref, bf16[128,64,128]{2,1,0:T(8,128)(2,1)} %all-to-all-done.1.z_ref, bf16[64,64,128]{2,1,0:T(8,128)(2,1)S(1)} %shard_map.151.own_ref, ...), custom_call_target="tpu_custom_call" | custom-call | flops 22000001024 | bytes 66000000 | tf_op jit(solution)/shard_map/pallas_call | solution.py:55
  210.4 20.2 %all-to-all-done.2.conv_ref = bf16[128,64,128]{2,1,0:T(8,128)(2,1)} async-done(((bf16[128,64,128]{2,1,0:T(8,128)(2,1)}), bf16[128,64,128]{2,1,0:T(8,128)(2,1)}, u32[]{:S(2)}, u32[]{:S(2)}) %all-to-all-start.2) | async-done | bytes 2097184 | tf_op jit(solution)/shard_map/all_to_all | solution.py:510
  230.7 11.5 %all-to-all-start.3 = ((bf16[128,64,128]{2,1,0:T(8,128)(2,1)}), bf16[128,64,128]{2,1,0:T(8,128)(2,1)}, u32[]{:S(2)}, u32[]{:S(2)}) async-start(bf16[128,64,128]{2,1,0:T(8,128)(2,1)} %get-tuple-element.29), calls=%async_computation.3 | async-start | bytes 4194304 | tf_op jit(solution)/shard_map/all_to_all | solution.py:510
  242.1 6.8 %shard_map.156 = bf16[64,64,128]{2,1,0:T(8,128)(2,1)S(1)} custom-call(s32[4]{0:T(128)S(1)} %pad_add_fusion.place_ref.core_ref, bf16[64,64,128]{2,1,0:T(8,128)(2,1)S(1)} %copy-done.11, bf16[64,64,128]{2,1,0:T(8,128)(2,1)S(1)} %collective-permute-done.10.recv_ref), custom_call_target="tpu_custom_call" | custom-call | flops 5000000000 | bytes 15000000 | tf_op jit(solution)/shard_map/pallas_call | solution.py:55
  255.9 41.6 %collective-permute-done.13 = bf16[1,4,4,64,128]{4,3,2,1,0:T(8,128)(2,1)S(1)} collective-permute-done((bf16[1,4,4,64,128]{4,3,2,1,0:T(8,128)(2,1)S(1)}, bf16[1,4,4,64,128]{4,3,2,1,0:T(8,128)(2,1)S(1)}, u32[]{:S(2)}, u32[]{:S(2)}) %collective-permute-start.13) | collective-permute-done | bytes 262176 | tf_op jit(solution)/shard_map/ppermute | solution.py:501
  297.4 15.6 %collective-permute-done.12 = bf16[1,4,4,64,128]{4,3,2,1,0:T(8,128)(2,1)S(1)} collective-permute-done((bf16[1,4,4,64,128]{4,3,2,1,0:T(8,128)(2,1)S(1)}, bf16[1,4,4,64,128]{4,3,2,1,0:T(8,128)(2,1)S(1)}, u32[]{:S(2)}, u32[]{:S(2)}) %collective-permute-start.12) | collective-permute-done | bytes 262176 | tf_op jit(solution)/shard_map/ppermute | solution.py:501
  323.0 7.8 %collective-permute-done.14 = bf16[4,1,4,64,128]{4,3,2,1,0:T(8,128)(2,1)S(1)} collective-permute-done((bf16[4,1,4,64,128]{4,3,2,1,0:T(8,128)(2,1)S(1)}, bf16[4,1,4,64,128]{4,3,2,1,0:T(8,128)(2,1)S(1)}, u32[]{:S(2)}, u32[]{:S(2)}) %collective-permute-start.14) | collective-permute-done | bytes 262176 | tf_op jit(solution)/shard_map/ppermute | solution.py:501
  335.2 3.4 collective-permute-done.19
  338.6 6.4 %collective-permute-done.18 = bf16[4,4,1,64,128]{4,3,2,1,0:T(8,128)(2,1)S(1)} collective-permute-done((bf16[4,4,1,64,128]{4,3,2,1,0:T(8,128)(2,1)S(1)}, bf16[4,4,1,64,128]{4,3,2,1,0:T(8,128)(2,1)S(1)}, u32[]{:S(2)}, u32[]{:S(2)}) %collective-permute-start.18) | collective-permute-done | bytes 262176 | tf_op jit(solution)/shard_map/ppermute | solution.py:501
  352.2 9.8 %shard_map.154 = (f32[128,8192]{1,0:T(8,128)}, f32[128,8192]{1,0:T(8,128)}) custom-call(bf16[128,128]{1,0:T(8,128)(2,1)S(1)} %copy.18.wv_ref, bf16[128,128]{1,0:T(8,128)(2,1)S(1)} %copy.19.wg_ref, bf16[128,128]{1,0:T(8,128)(2,1)S(1)} %copy-done, bf16[128,128]{1,0:T(8,128)(2,1)S(1)} %get-tuple-element.60.wpg_ref, f32[128,256]{1,0:T(8,128)S(1)} %broadcast_in_dim.2.skip_ref, ...), custom_call_target="tpu_custom_call" | custom-call | flops 10000000000 | bytes 30000000 | tf_op jit(solution)/shard_map/pallas_call | solution.py:454
  362.0 6.3 %shard_map.155 = bf16[128,8192]{1,0:T(8,128)(2,1)} custom-call(bf16[128,128]{1,0:T(8,128)(2,1)S(1)} %get-tuple-element.63.wpv_ref, f32[128,8192]{1,0:T(8,128)} %get-tuple-element.27.part_ref, f32[128,8192]{1,0:T(8,128)} %get-tuple-element.28.own_ref, bf16[128,64,128]{2,1,0:T(8,128)(2,1)} %all-to-all-done.3.back_ref), custom_call_target="tpu_custom_call" | custom-call | flops 6000000000 | bytes 18000000 | tf_op jit(solution)/shard_map/pallas_call | solution.py:454
  (87 shorter events, 58.2 us)
Async XLA Ops:
  6.1 91.2 %all-to-all-start = ((bf16[128,64,128]{2,1,0:T(8,128)(2,1)}), bf16[128,64,128]{2,1,0:T(8,128)(2,1)S(1)}, u32[]{:S(2)}, u32[]{:S(2)}) async-start(bf16[128,64,128]{2,1,0:T(8,128)(2,1)} %shard_map.150), calls=%async_computation | async-start | bytes 4194304 | tf_op jit(solution)/shard_map/all_to_all | solution.py:510
  23.4 55.1 %collective-permute-start.2 = (bf16[1,4,4,64,128]{4,3,2,1,0:T(8,128)(2,1)S(1)}, bf16[1,4,4,64,128]{4,3,2,1,0:T(8,128)(2,1)}, u32[]{:S(2)}, u32[]{:S(2)}) collective-permute-start(bf16[1,4,4,64,128]{4,3,2,1,0:T(8,128)(2,1)S(1)} %get-tuple-element.57), channel_id=1, source_target_pairs={{0,48},{16,0},{32,16},{48,32},{1,49},{17,1},{33,17},{49,33},{2,50}... | collective-permute-start | bytes 786440 | tf_op jit(solution)/shard_map/ppermute | solution.py:501
  26.2 66.5 %collective-permute-start.1 = (bf16[1,4,4,64,128]{4,3,2,1,0:T(8,128)(2,1)S(1)}, bf16[1,4,4,64,128]{4,3,2,1,0:T(8,128)(2,1)}, u32[]{:S(2)}, u32[]{:S(2)}) collective-permute-start(bf16[1,4,4,64,128]{4,3,2,1,0:T(8,128)(2,1)S(1)} %get-tuple-element.58), channel_id=1, source_target_pairs={{0,32},{16,48},{32,0},{48,16},{1,33},{17,49},{33,1},{49,17},{2,34}... | collective-permute-start | bytes 786440 | tf_op jit(solution)/shard_map/ppermute | solution.py:501
  28.9 63.7 %collective-permute-start = (bf16[1,4,4,64,128]{4,3,2,1,0:T(8,128)(2,1)S(1)}, bf16[1,4,4,64,128]{4,3,2,1,0:T(8,128)(2,1)}, u32[]{:S(2)}, u32[]{:S(2)}) collective-permute-start(bf16[1,4,4,64,128]{4,3,2,1,0:T(8,128)(2,1)S(1)} %get-tuple-element.59), channel_id=1, source_target_pairs={{0,16},{16,32},{32,48},{48,0},{1,17},{17,33},{33,49},{49,1},{2,18}... | collective-permute-start | bytes 786440 | tf_op jit(solution)/shard_map/ppermute | solution.py:501
  94.0 14.1 %collective-permute-start.5 = (bf16[4,1,4,64,128]{4,3,2,1,0:T(8,128)(2,1)S(1)}, bf16[4,1,4,64,128]{4,3,2,1,0:T(8,128)(2,1)}, u32[]{:S(2)}, u32[]{:S(2)}) collective-permute-start(bf16[4,1,4,64,128]{4,3,2,1,0:T(8,128)(2,1)S(1)} %get-tuple-element.53), channel_id=1, source_target_pairs={{0,12},{4,0},{8,4},{12,8},{1,13},{5,1},{9,5},{13,9},{2,14},{6,2},{... | collective-permute-start | bytes 786440 | tf_op jit(solution)/shard_map/ppermute | solution.py:501
  96.0 12.0 %collective-permute-start.4 = (bf16[4,1,4,64,128]{4,3,2,1,0:T(8,128)(2,1)S(1)}, bf16[4,1,4,64,128]{4,3,2,1,0:T(8,128)(2,1)}, u32[]{:S(2)}, u32[]{:S(2)}) collective-permute-start(bf16[4,1,4,64,128]{4,3,2,1,0:T(8,128)(2,1)S(1)} %get-tuple-element.54), channel_id=1, source_target_pairs={{0,8},{4,12},{8,0},{12,4},{1,9},{5,13},{9,1},{13,5},{2,10},{6,14},... | collective-permute-start | bytes 786440 | tf_op jit(solution)/shard_map/ppermute | solution.py:501
  97.1 15.6 %collective-permute-start.3 = (bf16[4,1,4,64,128]{4,3,2,1,0:T(8,128)(2,1)S(1)}, bf16[4,1,4,64,128]{4,3,2,1,0:T(8,128)(2,1)}, u32[]{:S(2)}, u32[]{:S(2)}) collective-permute-start(bf16[4,1,4,64,128]{4,3,2,1,0:T(8,128)(2,1)S(1)} %get-tuple-element.55), channel_id=1, source_target_pairs={{0,4},{4,8},{8,12},{12,0},{1,5},{5,9},{9,13},{13,1},{2,6},{6,10},{... | collective-permute-start | bytes 786440 | tf_op jit(solution)/shard_map/ppermute | solution.py:501
  98.6 75.5 %all-to-all-start.1 = ((bf16[128,64,128]{2,1,0:T(8,128)(2,1)}), bf16[128,64,128]{2,1,0:T(8,128)(2,1)}, u32[]{:S(2)}, u32[]{:S(2)}) async-start(bf16[128,64,128]{2,1,0:T(8,128)(2,1)} %shard_map.149), calls=%async_computation.1 | async-start | bytes 4194304 | tf_op jit(solution)/shard_map/all_to_all | solution.py:510
  114.0 11.5 %collective-permute-start.8 = (bf16[4,4,1,64,128]{4,3,2,1,0:T(8,128)(2,1)S(1)}, bf16[4,4,1,64,128]{4,3,2,1,0:T(8,128)(2,1)S(1)}, u32[]{:S(2)}, u32[]{:S(2)}) collective-permute-start(bf16[4,4,1,64,128]{4,3,2,1,0:T(8,128)(2,1)S(1)} %get-tuple-element.49), channel_id=1, source_target_pairs={{0,3},{1,0},{2,1},{3,2},{4,7},{5,4},{6,5},{7,6},{8,11},{9,8},{10,9... | collective-permute-start | bytes 786440 | tf_op jit(solution)/shard_map/ppermute | solution.py:501
  114.1 25.3 %collective-permute-start.7 = (bf16[4,4,1,64,128]{4,3,2,1,0:T(8,128)(2,1)S(1)}, bf16[4,4,1,64,128]{4,3,2,1,0:T(8,128)(2,1)S(1)}, u32[]{:S(2)}, u32[]{:S(2)}) collective-permute-start(bf16[4,4,1,64,128]{4,3,2,1,0:T(8,128)(2,1)S(1)} %get-tuple-element.50), channel_id=1, source_target_pairs={{0,2},{1,3},{2,0},{3,1},{4,6},{5,7},{6,4},{7,5},{8,10},{9,11},{10,... | collective-permute-start | bytes 786440 | tf_op jit(solution)/shard_map/ppermute | solution.py:501
  118.1 21.4 %collective-permute-start.6 = (bf16[4,4,1,64,128]{4,3,2,1,0:T(8,128)(2,1)S(1)}, bf16[4,4,1,64,128]{4,3,2,1,0:T(8,128)(2,1)S(1)}, u32[]{:S(2)}, u32[]{:S(2)}) collective-permute-start(bf16[4,4,1,64,128]{4,3,2,1,0:T(8,128)(2,1)S(1)} %get-tuple-element.51), channel_id=1, source_target_pairs={{0,1},{1,2},{2,3},{3,0},{4,5},{5,6},{6,7},{7,4},{8,9},{9,10},{10,1... | collective-permute-start | bytes 786440 | tf_op jit(solution)/shard_map/ppermute | solution.py:501
  147.1 3.9 %collective-permute-start.9 = (bf16[64,64,128]{2,1,0:T(8,128)(2,1)S(1)}, bf16[64,64,128]{2,1,0:T(8,128)(2,1)S(1)}, u32[]{:S(2)}, u32[]{:S(2)}) collective-permute-start(bf16[64,64,128]{2,1,0:T(8,128)(2,1)S(1)} %shard_map.151.own_ref), channel_id=1, source_target_pairs={{0,64},{64,0},{1,65},{65,1},{2,66},{66,2},{3,67},{67,3},{4,68},{68... | collective-permute-start | bytes 3145736 | tf_op jit(solution)/shard_map/ppermute | solution.py:571
  174.0 56.6 %all-to-all-start.2 = ((bf16[128,64,128]{2,1,0:T(8,128)(2,1)}), bf16[128,64,128]{2,1,0:T(8,128)(2,1)}, u32[]{:S(2)}, u32[]{:S(2)}) async-start(bf16[128,64,128]{2,1,0:T(8,128)(2,1)} %get-tuple-element.25), calls=%async_computation.2 | async-start | bytes 4194304 | tf_op jit(solution)/shard_map/all_to_all | solution.py:510
  209.5 32.6 %collective-permute-start.10 = (bf16[64,64,128]{2,1,0:T(8,128)(2,1)S(1)}, bf16[64,64,128]{2,1,0:T(8,128)(2,1)S(1)}, u32[]{:S(2)}, u32[]{:S(2)}) collective-permute-start(bf16[64,64,128]{2,1,0:T(8,128)(2,1)S(1)} %get-tuple-element.31), channel_id=1, source_target_pairs={{0,64},{64,0},{1,65},{65,1},{2,66},{66,2},{3,67},{67,3},{4,68},{68... | collective-permute-start | bytes 3145736 | tf_op jit(solution)/shard_map/ppermute | solution.py:588
  230.7 131.3 %all-to-all-start.3 = ((bf16[128,64,128]{2,1,0:T(8,128)(2,1)}), bf16[128,64,128]{2,1,0:T(8,128)(2,1)}, u32[]{:S(2)}, u32[]{:S(2)}) async-start(bf16[128,64,128]{2,1,0:T(8,128)(2,1)} %get-tuple-element.29), calls=%async_computation.3 | async-start | bytes 4194304 | tf_op jit(solution)/shard_map/all_to_all | solution.py:510
  249.0 48.4 %collective-permute-start.13 = (bf16[1,4,4,64,128]{4,3,2,1,0:T(8,128)(2,1)S(1)}, bf16[1,4,4,64,128]{4,3,2,1,0:T(8,128)(2,1)S(1)}, u32[]{:S(2)}, u32[]{:S(2)}) collective-permute-start(bf16[1,4,4,64,128]{4,3,2,1,0:T(8,128)(2,1)S(1)} %get-tuple-element.45), channel_id=1, source_target_pairs={{0,48},{16,0},{32,16},{48,32},{1,49},{17,1},{33,17},{49,33},{2,50}... | collective-permute-start | bytes 786440 | tf_op jit(solution)/shard_map/ppermute | solution.py:501
  251.8 61.2 %collective-permute-start.12 = (bf16[1,4,4,64,128]{4,3,2,1,0:T(8,128)(2,1)S(1)}, bf16[1,4,4,64,128]{4,3,2,1,0:T(8,128)(2,1)S(1)}, u32[]{:S(2)}, u32[]{:S(2)}) collective-permute-start(bf16[1,4,4,64,128]{4,3,2,1,0:T(8,128)(2,1)S(1)} %get-tuple-element.46), channel_id=1, source_target_pairs={{0,32},{16,48},{32,0},{48,16},{1,33},{17,49},{33,1},{49,17},{2,34}... | collective-permute-start | bytes 786440 | tf_op jit(solution)/shard_map/ppermute | solution.py:501
  254.6 58.4 %collective-permute-start.11 = (bf16[1,4,4,64,128]{4,3,2,1,0:T(8,128)(2,1)S(1)}, bf16[1,4,4,64,128]{4,3,2,1,0:T(8,128)(2,1)S(1)}, u32[]{:S(2)}, u32[]{:S(2)}) collective-permute-start(bf16[1,4,4,64,128]{4,3,2,1,0:T(8,128)(2,1)S(1)} %get-tuple-element.47), channel_id=1, source_target_pairs={{0,16},{16,32},{32,48},{48,0},{1,17},{17,33},{33,49},{49,1},{2,18}... | collective-permute-start | bytes 786440 | tf_op jit(solution)/shard_map/ppermute | solution.py:501
  313.3 6.5 %collective-permute-start.16 = (bf16[4,1,4,64,128]{4,3,2,1,0:T(8,128)(2,1)S(1)}, bf16[4,1,4,64,128]{4,3,2,1,0:T(8,128)(2,1)S(1)}, u32[]{:S(2)}, u32[]{:S(2)}) collective-permute-start(bf16[4,1,4,64,128]{4,3,2,1,0:T(8,128)(2,1)S(1)} %get-tuple-element.41), channel_id=1, source_target_pairs={{0,12},{4,0},{8,4},{12,8},{1,13},{5,1},{9,5},{13,9},{2,14},{6,2},{... | collective-permute-start | bytes 786440 | tf_op jit(solution)/shard_map/ppermute | solution.py:501
  315.4 7.6 %collective-permute-start.15 = (bf16[4,1,4,64,128]{4,3,2,1,0:T(8,128)(2,1)S(1)}, bf16[4,1,4,64,128]{4,3,2,1,0:T(8,128)(2,1)S(1)}, u32[]{:S(2)}, u32[]{:S(2)}) collective-permute-start(bf16[4,1,4,64,128]{4,3,2,1,0:T(8,128)(2,1)S(1)} %get-tuple-element.42), channel_id=1, source_target_pairs={{0,8},{4,12},{8,0},{12,4},{1,9},{5,13},{9,1},{13,5},{2,10},{6,14},... | collective-permute-start | bytes 786440 | tf_op jit(solution)/shard_map/ppermute | solution.py:501
  316.3 14.4 %collective-permute-start.14 = (bf16[4,1,4,64,128]{4,3,2,1,0:T(8,128)(2,1)S(1)}, bf16[4,1,4,64,128]{4,3,2,1,0:T(8,128)(2,1)S(1)}, u32[]{:S(2)}, u32[]{:S(2)}) collective-permute-start(bf16[4,1,4,64,128]{4,3,2,1,0:T(8,128)(2,1)S(1)} %get-tuple-element.43), channel_id=1, source_target_pairs={{0,4},{4,8},{8,12},{12,0},{1,5},{5,9},{9,13},{13,1},{2,6},{6,10},{... | collective-permute-start | bytes 786440 | tf_op jit(solution)/shard_map/ppermute | solution.py:501
  331.0 7.7 %collective-permute-start.19 = (bf16[4,4,1,64,128]{4,3,2,1,0:T(8,128)(2,1)S(1)}, bf16[4,4,1,64,128]{4,3,2,1,0:T(8,128)(2,1)S(1)}, u32[]{:S(2)}, u32[]{:S(2)}) collective-permute-start(bf16[4,4,1,64,128]{4,3,2,1,0:T(8,128)(2,1)S(1)} %get-tuple-element.37), channel_id=1, source_target_pairs={{0,3},{1,0},{2,1},{3,2},{4,7},{5,4},{6,5},{7,6},{8,11},{9,8},{10,9... | collective-permute-start | bytes 786440 | tf_op jit(solution)/shard_map/ppermute | solution.py:501
  331.5 13.5 %collective-permute-start.18 = (bf16[4,4,1,64,128]{4,3,2,1,0:T(8,128)(2,1)S(1)}, bf16[4,4,1,64,128]{4,3,2,1,0:T(8,128)(2,1)S(1)}, u32[]{:S(2)}, u32[]{:S(2)}) collective-permute-start(bf16[4,4,1,64,128]{4,3,2,1,0:T(8,128)(2,1)S(1)} %get-tuple-element.38), channel_id=1, source_target_pairs={{0,2},{1,3},{2,0},{3,1},{4,6},{5,7},{6,4},{7,5},{8,10},{9,11},{10,... | collective-permute-start | bytes 786440 | tf_op jit(solution)/shard_map/ppermute | solution.py:501
  333.5 12.4 %collective-permute-start.17 = (bf16[4,4,1,64,128]{4,3,2,1,0:T(8,128)(2,1)S(1)}, bf16[4,4,1,64,128]{4,3,2,1,0:T(8,128)(2,1)S(1)}, u32[]{:S(2)}, u32[]{:S(2)}) collective-permute-start(bf16[4,4,1,64,128]{4,3,2,1,0:T(8,128)(2,1)S(1)} %get-tuple-element.39), channel_id=1, source_target_pairs={{0,1},{1,2},{2,3},{3,0},{4,5},{5,6},{6,7},{7,4},{8,9},{9,10},{10,1... | collective-permute-start | bytes 786440 | tf_op jit(solution)/shard_map/ppermute | solution.py:501
  (16 other events, 99.2 us)
